TPU v7x, 32 devices: a whole 2x2x4 slice. The times are simulated.
32 devices in a mesh: fsdp: 4 (over x, core), context: 4 (over z), tensor: 2 (over y).
Axes of the slice: x: 2, y: 2, z: 4, core: 2. Of those that a mesh axis runs over, the one named last changes fastest.
Arguments:
- tokens: bfloat16 [4, 2048, 2048], P('fsdp', 'context'), may hold values from -6 to 6
- segments: int32 [4, 2048], P('fsdp'), may hold values from 0 to 7, never falling along the last dimension, each value on 1 to 1024 neighbouring positions
- query_weight: bfloat16 [2048, 2048], P(('fsdp', 'context'), 'tensor'), may hold values from -0.125 to 0.125
- key_weight: bfloat16 [2048, 2048], P(('fsdp', 'context'), 'tensor'), may hold values from -0.125 to 0.125
- value_weight: bfloat16 [2048, 2048], P(('fsdp', 'context'), 'tensor'), may hold values from -0.125 to 0.125
- out_weight: bfloat16 [2048, 2048], P(('fsdp', 'context'), 'tensor'), may hold values from -0.375 to 0.375
- up_weight: bfloat16 [2048, 8192], P(('fsdp', 'context'), 'tensor'), may hold values from -0.125 to 0.125
- down_weight: bfloat16 [2048, 8192], P(('fsdp', 'context'), 'tensor'), may hold values from -0.0625 to 0.0625
- attn_gain: bfloat16 [2048], P(('fsdp', 'context')), may hold values from 0.5 to 1.5
- attn_bias: bfloat16 [2048], P(('fsdp', 'context')), may hold values from -1 to 1
- mlp_gain: bfloat16 [2048], P(('fsdp', 'context')), may hold values from 0.5 to 1.5
- mlp_bias: bfloat16 [2048], P(('fsdp', 'context')), may hold values from -1 to 1
- cotangent: bfloat16 [4, 2048, 2048], P('fsdp', 'context'), may hold values from -6 to 6
Outputs:
- output: bfloat16 [4, 2048, 2048], P('fsdp', 'context')
- tokens_grad: bfloat16 [4, 2048, 2048], P('fsdp', 'context')
- query_grad: float32 [2048, 2048], P(('fsdp', 'context'), 'tensor')
- key_grad: float32 [2048, 2048], P(('fsdp', 'context'), 'tensor')
- value_grad: float32 [2048, 2048], P(('fsdp', 'context'), 'tensor')
- out_grad: float32 [2048, 2048], P(('fsdp', 'context'), 'tensor')
- up_grad: float32 [2048, 8192], P(('fsdp', 'context'), 'tensor')
- down_grad: float32 [2048, 8192], P(('fsdp', 'context'), 'tensor')
- attn_gain_grad: float32 [2048], P(('fsdp', 'context'))
- attn_bias_grad: float32 [2048], P(('fsdp', 'context'))
- mlp_gain_grad: float32 [2048], P(('fsdp', 'context'))
- mlp_bias_grad: float32 [2048], P(('fsdp', 'context'))
Inputs may be any that keep to these rules, and one draw needn't show every extreme that they name: `segments`: in each sequence the document numbers run from 0 to 7 without falling; every document has 1 to 1024 tokens and one has exactly 1024.
All inputs are finite; a program needn't handle non-finite values.
Results may differ from a plain program's by a relative error of at most 0.017.
Values may be sent and summed in bfloat16 or wider, within the bound.
A program may use at most 320 MiB of HBM per device.

v0:
```python
import jax
import jax.numpy as jnp
from jax import lax
from jax.sharding import PartitionSpec as P

HEAD = 128


epsilon = 1e-05
big_negative = -1e30
density = 0.3989422804014327
half_root = 0.7071067811865476


def contract(left, right, left_dim, right_dim):
    return lax.dot_general(
        left, right, (((left_dim,), (right_dim,)), ((), ())), preferred_element_type=jnp.float32
    )


def norm_stats(row_vals):
    average = jnp.mean(row_vals, axis=-1, keepdims=True)
    centered = row_vals - average
    variance = jnp.mean(centered * centered, axis=-1, keepdims=True)
    inv_std = lax.rsqrt(variance + epsilon)
    return (centered * inv_std, inv_std)


def norm_back(grad_out, normed_hat, inv_std, gain_vals):
    scaled = grad_out * gain_vals
    first_mean = jnp.mean(scaled, axis=-1, keepdims=True)
    second_mean = jnp.mean(scaled * normed_hat, axis=-1, keepdims=True)
    return inv_std * (scaled - first_mean - normed_hat * second_mean)


def block_size():
    return 512


def per_device(
    tokens,
    segments,
    query_weight,
    key_weight,
    value_weight,
    out_weight,
    up_weight,
    down_weight,
    attn_gain,
    attn_bias,
    mlp_gain,
    mlp_bias,
    cotangent,
):
    seq_dev, group_len, model_width = tokens.shape
    token_count = seq_dev * group_len
    local_width = query_weight.shape[1]
    hidden_local = up_weight.shape[1]
    local_heads = local_width // HEAD
    seq_len = segments.shape[1]
    factor = HEAD ** (-0.5)
    offset = lax.axis_index("context") * group_len
    query_seg = lax.dynamic_slice_in_dim(segments, offset, group_len, 1)
    query_pos = offset + jnp.arange(group_len, dtype=jnp.int32)
    rows_in = tokens.reshape(token_count, model_width).astype(jnp.float32)
    full_query, full_key, full_value, full_out, gain_one, bias_one = (
        lax.all_gather(query_weight, ("fsdp", "context"), axis=0, tiled=True),
        lax.all_gather(key_weight, ("fsdp", "context"), axis=0, tiled=True),
        lax.all_gather(value_weight, ("fsdp", "context"), axis=0, tiled=True),
        lax.all_gather(out_weight, ("fsdp", "context"), axis=0, tiled=True),
        lax.all_gather(attn_gain, ("fsdp", "context"), axis=0, tiled=True),
        lax.all_gather(attn_bias, ("fsdp", "context"), axis=0, tiled=True),
    )
    hat_one, inv_one = norm_stats(rows_in)
    gain_one_f = gain_one.astype(jnp.float32)
    normed_one = (hat_one * gain_one_f + bias_one.astype(jnp.float32)).astype(jnp.bfloat16)
    shape_four = (seq_dev, group_len, local_heads, HEAD)
    query_four = (
        jnp.dot(normed_one, full_query, preferred_element_type=jnp.float32)
        .astype(jnp.bfloat16)
        .reshape(shape_four)
    )
    key_four = (
        jnp.dot(normed_one, full_key, preferred_element_type=jnp.float32)
        .astype(jnp.bfloat16)
        .reshape(shape_four)
    )
    value_four = (
        jnp.dot(normed_one, full_value, preferred_element_type=jnp.float32)
        .astype(jnp.bfloat16)
        .reshape(shape_four)
    )

    def mask_for(first_row, block_len):
        key_seg = lax.dynamic_slice_in_dim(segments, jnp.maximum(first_row, 0), block_len, 1)
        key_pos = first_row + jnp.arange(block_len, dtype=jnp.int32)
        same_doc = query_seg[:, None, :, None] == key_seg[:, None, None, :]
        causal = (query_pos[None, None, :, None] >= key_pos[None, None, None, :]) & (
            key_pos[None, None, None, :] >= 0
        )
        return same_doc & causal

    stat_shape = (seq_dev, local_heads, group_len)
    start_state = (
        jnp.full(stat_shape, big_negative, jnp.float32),
        jnp.zeros(stat_shape, jnp.float32),
        jnp.zeros(stat_shape + (HEAD,), jnp.float32),
    )
    key_piece = lax.all_gather(key_four, "context", axis=1, tiled=True)
    value_piece = lax.all_gather(value_four, "context", axis=1, tiled=True)
    block_len = block_size()

    def forward_step(block_index, carried):
        block_start = block_index * block_len
        allowed = mask_for(block_start, block_len)

        def forward_compute(state):
            run_max, run_sum, run_acc = state
            key_block = lax.dynamic_slice_in_dim(key_piece, block_start, block_len, 1)
            value_block = lax.dynamic_slice_in_dim(value_piece, block_start, block_len, 1)
            scores = (
                jnp.einsum(
                    "sqhd,skhd->shqk", query_four, key_block, preferred_element_type=jnp.float32
                )
                * factor
            )
            masked = jnp.where(allowed, scores, big_negative)
            new_max = jnp.maximum(run_max, jnp.max(masked, axis=-1))
            exp_terms = jnp.where(allowed, jnp.exp(masked - new_max[..., None]), 0.0)
            shrink = jnp.exp(run_max - new_max)
            new_sum = run_sum * shrink + jnp.sum(exp_terms, axis=-1)
            new_acc = run_acc * shrink[..., None] + jnp.einsum(
                "shqk,skhd->shqd",
                exp_terms.astype(jnp.bfloat16),
                value_block,
                preferred_element_type=jnp.float32,
            )
            return (new_max, new_sum, new_acc)

        return lax.cond(jnp.any(allowed), forward_compute, lambda state: state, carried)

    run_max, run_sum, run_acc = lax.fori_loop(
        0, key_piece.shape[1] // block_len, forward_step, start_state
    )
    attn_four = jnp.transpose(run_acc / run_sum[..., None], (0, 2, 1, 3))
    log_sum = run_max + jnp.log(run_sum)
    attn_bf = attn_four.reshape(token_count, local_width).astype(jnp.bfloat16)
    branch = lax.psum(contract(attn_bf, full_out, 1, 1).astype(jnp.bfloat16), "tensor").astype(
        jnp.float32
    )
    residual = rows_in + branch
    full_up, full_down, gain_two, bias_two = (
        lax.all_gather(up_weight, ("fsdp", "context"), axis=0, tiled=True),
        lax.all_gather(down_weight, ("fsdp", "context"), axis=0, tiled=True),
        lax.all_gather(mlp_gain, ("fsdp", "context"), axis=0, tiled=True),
        lax.all_gather(mlp_bias, ("fsdp", "context"), axis=0, tiled=True),
    )
    hat_two, inv_two = norm_stats(residual)
    gain_two_f = gain_two.astype(jnp.float32)
    normed_two = (hat_two * gain_two_f + bias_two.astype(jnp.float32)).astype(jnp.bfloat16)
    pre_act = jnp.dot(normed_two, full_up, preferred_element_type=jnp.float32)
    activated = jax.nn.gelu(pre_act, approximate=False).astype(jnp.bfloat16)
    mlp_out = lax.psum(contract(activated, full_down, 1, 1).astype(jnp.bfloat16), "tensor").astype(
        jnp.float32
    )
    output = (residual + mlp_out).astype(jnp.bfloat16).reshape(tokens.shape)
    grad_rows = cotangent.reshape(token_count, model_width)
    grad_act = jnp.dot(grad_rows, full_down, preferred_element_type=jnp.float32)
    normal_cdf = 0.5 * (1.0 + lax.erf(pre_act * half_root))
    slope = normal_cdf + pre_act * density * jnp.exp(-0.5 * pre_act * pre_act)
    grad_pre = (grad_act * slope).astype(jnp.bfloat16)
    grad_norm_two = lax.psum(
        contract(grad_pre, full_up, 1, 1).astype(jnp.bfloat16), "tensor"
    ).astype(jnp.float32)
    mlp_sums = lax.psum_scatter(
        jnp.concatenate(
            (contract(normed_two, grad_pre, 0, 0), contract(grad_rows, activated, 0, 0)), axis=1
        ),
        ("fsdp", "context"),
        scatter_dimension=0,
        tiled=True,
    )
    gain_two_term = jnp.sum(grad_norm_two * hat_two, axis=0)
    bias_two_term = jnp.sum(grad_norm_two, axis=0)
    grad_resid = grad_rows.astype(jnp.float32) + norm_back(
        grad_norm_two, hat_two, inv_two, gain_two_f
    )
    grad_branch = grad_resid.astype(jnp.bfloat16)
    out_term = contract(grad_branch, attn_bf, 0, 0)
    grad_attn_four = (
        jnp.dot(grad_branch, full_out, preferred_element_type=jnp.float32)
        .astype(jnp.bfloat16)
        .reshape(shape_four)
    )
    row_delta = jnp.einsum("sqhd,sqhd->shq", grad_attn_four.astype(jnp.float32), attn_four)
    full_shape = (seq_dev, seq_len, local_heads, HEAD)
    back_start = (
        jnp.zeros(shape_four, jnp.float32),
        jnp.zeros(full_shape, jnp.float32),
        jnp.zeros(full_shape, jnp.float32),
    )
    backward_key_piece = lax.all_gather(key_four, "context", axis=1, tiled=True)
    backward_value_piece = lax.all_gather(value_four, "context", axis=1, tiled=True)
    backward_block_len = block_size()

    def backward_step(block_index, carried):
        block_start = block_index * backward_block_len
        allowed = mask_for(block_start, backward_block_len)

        def backward_compute(state):
            grad_query, grad_key, grad_value = state
            key_block = lax.dynamic_slice_in_dim(
                backward_key_piece, block_start, backward_block_len, 1
            )
            value_block = lax.dynamic_slice_in_dim(
                backward_value_piece, block_start, backward_block_len, 1
            )
            scores = (
                jnp.einsum(
                    "sqhd,skhd->shqk", query_four, key_block, preferred_element_type=jnp.float32
                )
                * factor
            )
            masked = jnp.where(allowed, scores, big_negative)
            prob_rows = jnp.where(allowed, jnp.exp(masked - log_sum[..., None]), 0.0)
            grad_prob = jnp.einsum(
                "sqhd,skhd->shqk", grad_attn_four, value_block, preferred_element_type=jnp.float32
            )
            grad_score = (prob_rows * (grad_prob - row_delta[..., None])).astype(jnp.bfloat16)
            grad_query = (
                grad_query
                + jnp.einsum(
                    "shqk,skhd->sqhd", grad_score, key_block, preferred_element_type=jnp.float32
                )
                * factor
            )
            key_update = (
                jnp.einsum(
                    "shqk,sqhd->skhd", grad_score, query_four, preferred_element_type=jnp.float32
                )
                * factor
            )
            value_update = jnp.einsum(
                "shqk,sqhd->skhd",
                prob_rows.astype(jnp.bfloat16),
                grad_attn_four,
                preferred_element_type=jnp.float32,
            )
            grad_key = lax.dynamic_update_slice_in_dim(
                grad_key,
                lax.dynamic_slice_in_dim(grad_key, block_start, backward_block_len, 1) + key_update,
                block_start,
                1,
            )
            grad_value = lax.dynamic_update_slice_in_dim(
                grad_value,
                lax.dynamic_slice_in_dim(grad_value, block_start, backward_block_len, 1)
                + value_update,
                block_start,
                1,
            )
            return (grad_query, grad_key, grad_value)

        return lax.cond(jnp.any(allowed), backward_compute, lambda state: state, carried)

    grad_query, key_full, value_full = lax.fori_loop(
        0, backward_key_piece.shape[1] // backward_block_len, backward_step, back_start
    )
    key_local, value_local = (
        lax.psum_scatter(
            key_full.astype(jnp.bfloat16), "context", scatter_dimension=1, tiled=True
        ).astype(jnp.float32),
        lax.psum_scatter(
            value_full.astype(jnp.bfloat16), "context", scatter_dimension=1, tiled=True
        ).astype(jnp.float32),
    )
    query_bf = grad_query.reshape(token_count, local_width).astype(jnp.bfloat16)
    key_bf = key_local.reshape(token_count, local_width).astype(jnp.bfloat16)
    value_bf = value_local.reshape(token_count, local_width).astype(jnp.bfloat16)
    input_part = (
        contract(query_bf, full_query, 1, 1)
        + contract(key_bf, full_key, 1, 1)
        + contract(value_bf, full_value, 1, 1)
    )
    grad_norm_one = lax.psum(input_part.astype(jnp.bfloat16), "tensor").astype(jnp.float32)
    query_term = contract(normed_one, query_bf, 0, 0)
    key_term = contract(normed_one, key_bf, 0, 0)
    value_term = contract(normed_one, value_bf, 0, 0)
    gain_one_term = jnp.sum(grad_norm_one * hat_one, axis=0)
    bias_one_term = jnp.sum(grad_norm_one, axis=0)
    tokens_grad = (
        (grad_resid + norm_back(grad_norm_one, hat_one, inv_one, gain_one_f))
        .astype(jnp.bfloat16)
        .reshape(tokens.shape)
    )
    (
        query_grad,
        key_grad,
        value_grad,
        out_grad,
        attn_gain_grad,
        attn_bias_grad,
        mlp_gain_grad,
        mlp_bias_grad,
    ) = (
        lax.psum_scatter(query_term, ("fsdp", "context"), scatter_dimension=0, tiled=True),
        lax.psum_scatter(key_term, ("fsdp", "context"), scatter_dimension=0, tiled=True),
        lax.psum_scatter(value_term, ("fsdp", "context"), scatter_dimension=0, tiled=True),
        lax.psum_scatter(out_term, ("fsdp", "context"), scatter_dimension=0, tiled=True),
        lax.psum_scatter(gain_one_term, ("fsdp", "context"), scatter_dimension=0, tiled=True),
        lax.psum_scatter(bias_one_term, ("fsdp", "context"), scatter_dimension=0, tiled=True),
        lax.psum_scatter(gain_two_term, ("fsdp", "context"), scatter_dimension=0, tiled=True),
        lax.psum_scatter(bias_two_term, ("fsdp", "context"), scatter_dimension=0, tiled=True),
    )
    up_grad = mlp_sums[:, :hidden_local]
    down_grad = mlp_sums[:, hidden_local:]
    return (
        output,
        tokens_grad,
        query_grad,
        key_grad,
        value_grad,
        out_grad,
        up_grad,
        down_grad,
        attn_gain_grad,
        attn_bias_grad,
        mlp_gain_grad,
        mlp_bias_grad,
    )


def solution(mesh):
    placed = (
        P("fsdp", "context", None),
        P("fsdp", None),
        P(("fsdp", "context"), "tensor"),
        P(("fsdp", "context"), "tensor"),
        P(("fsdp", "context"), "tensor"),
        P(("fsdp", "context"), "tensor"),
        P(("fsdp", "context"), "tensor"),
        P(("fsdp", "context"), "tensor"),
        P(("fsdp", "context")),
        P(("fsdp", "context")),
        P(("fsdp", "context")),
        P(("fsdp", "context")),
        P("fsdp", "context", None),
    )
    return jax.shard_map(
        per_device,
        mesh=mesh,
        in_specs=placed,
        out_specs=(
            P("fsdp", "context", None),
            P("fsdp", "context", None),
            P(("fsdp", "context"), "tensor"),
            P(("fsdp", "context"), "tensor"),
            P(("fsdp", "context"), "tensor"),
            P(("fsdp", "context"), "tensor"),
            P(("fsdp", "context"), "tensor"),
            P(("fsdp", "context"), "tensor"),
            P(("fsdp", "context")),
            P(("fsdp", "context")),
            P(("fsdp", "context")),
            P(("fsdp", "context")),
        ),
        check_vma=False,
    )
```

profile of v0, /device:TPU:0, one launch (start us, length us, event | category | flops | bytes accessed | tf_op | source)
XLA Modules:
  0.0 2239.6 jit_solution(8759078227505884808)
XLA Ops:
  9.5 34.3 %all-gather = bf16[16,1,128]{2,1,0:T(2,128)(2,1)S(1)} all-gather(bf16[1,1,128]{2,1,0:T(2,128)(2,1)} %bitcast.307), channel_id=1, replica_groups=mesh['fsdp'=4,'context'=4,'tensor'=2] {'fsdp','context'}, dimensions={0}, use_global_device_ids=true | all-gather | bytes 4352 | tf_op jit(solution)/shard_map/all_gather | solution.py:71
  43.7 29.0 %all-gather.1 = bf16[16,1,128]{2,1,0:T(2,128)(2,1)S(1)} all-gather(bf16[1,1,128]{2,1,0:T(2,128)(2,1)} %bitcast.308), channel_id=1, replica_groups=mesh['fsdp'=4,'context'=4,'tensor'=2] {'fsdp','context'}, dimensions={0}, use_global_device_ids=true | all-gather | bytes 4352 | tf_op jit(solution)/shard_map/all_gather | solution.py:72
  81.5 33.2 %all-gather.13.cloned.1.call-done = bf16[2048,1024]{1,0:T(8,128)(2,1)} async-done(((bf16[128,1024]{1,0:T(8,128)(2,1)}), bf16[2048,1024]{1,0:T(8,128)(2,1)}) %all-gather.13.cloned.1.call-update) | async-done | bytes 4194320 | tf_op jit(solution)/shard_map/all_gather | solution.py:68
  121.6 44.3 %all-gather.17.cloned.1.call-done = bf16[2048,1024]{1,0:T(8,128)(2,1)} async-done(((bf16[128,1024]{1,0:T(8,128)(2,1)}), bf16[2048,1024]{1,0:T(8,128)(2,1)}) %all-gather.17.cloned.1.call-update) | async-done | bytes 4194320 | tf_op jit(solution)/shard_map/all_gather | solution.py:67
  170.9 76.3 %all-gather.21.cloned.1.call-done = bf16[1,2048,8,128]{3,1,2,0:T(8,128)(2,1)} async-done(((bf16[1,512,8,128]{3,1,2,0:T(8,128)(2,1)}), bf16[1,2048,8,128]{3,1,2,0:T(8,128)(2,1)}) %all-gather.21.cloned.1.call-update) | async-done | bytes 4194320 | tf_op jit(solution)/shard_map/all_gather | solution.py:110
  247.2 81.2 %all-gather.15.cloned.1.call-done = bf16[1,2048,8,128]{3,1,2,0:T(8,128)(2,1)} async-done(((bf16[1,512,8,128]{3,1,2,0:T(8,128)(2,1)}), bf16[1,2048,8,128]{3,1,2,0:T(8,128)(2,1)}) %all-gather.15.cloned.1.call-update) | async-done | bytes 4194320 | tf_op jit(solution)/shard_map/all_gather | solution.py:109
  352.5 26.9 %all-gather.23.cloned.1.call-done = bf16[2048,1024]{1,0:T(8,128)(2,1)} async-done(((bf16[128,1024]{1,0:T(8,128)(2,1)}), bf16[2048,1024]{1,0:T(8,128)(2,1)}) %all-gather.23.cloned.1.call-update) | async-done | bytes 4194320 | tf_op jit(solution)/shard_map/all_gather | solution.py:70
  387.2 30.1 %all-gather.2 = bf16[16,1,128]{2,1,0:T(2,128)(2,1)S(1)} all-gather(bf16[1,1,128]{2,1,0:T(2,128)(2,1)S(1)} %bitcast.309), channel_id=1, replica_groups=mesh['fsdp'=4,'context'=4,'tensor'=2] {'fsdp','context'}, dimensions={0}, use_global_device_ids=true | all-gather | bytes 4352 | tf_op jit(solution)/shard_map/all_gather | solution.py:155
  417.4 29.0 %all-gather.3 = bf16[16,1,128]{2,1,0:T(2,128)(2,1)S(1)} all-gather(bf16[1,1,128]{2,1,0:T(2,128)(2,1)S(1)} %bitcast.310), channel_id=1, replica_groups=mesh['fsdp'=4,'context'=4,'tensor'=2] {'fsdp','context'}, dimensions={0}, use_global_device_ids=true | all-gather | bytes 4352 | tf_op jit(solution)/shard_map/all_gather | solution.py:156
  450.7 125.3 %all-gather.25.cloned.1.call-done = bf16[2048,4096]{1,0:T(8,128)(2,1)} async-done(((bf16[128,4096]{1,0:T(8,128)(2,1)}), bf16[2048,4096]{1,0:T(8,128)(2,1)}) %all-gather.25.cloned.1.call-update) | async-done | bytes 16777232 | tf_op jit(solution)/shard_map/all_gather | solution.py:153
  576.0 33.4 %fusion.55 = (bf16[512,4096]{1,0:T(8,128)(2,1)}, f32[512,4096]{1,0:T(8,128)}) fusion(bf16[2048,4096]{1,0:T(8,128)(2,1)} %all-gather.25.cloned.1.call-done, f32[2048]{0:T(1024)S(1)} %bitcast.305, f32[2048]{0:T(1024)S(1)} %bitcast.291, f32[512]{0:T(512)S(1)} %add_rsqrt_fusion, f32[512]{0:T(512)S(1)} %broadcast_multiply_fusion.4, ...), kind=kOutput, calls=%fused_computation.72 | convolution fusion | flops 8734638080 | bytes 33574912 | tf_op jit(solution)/shard_map/dot_general | solution.py:161
  609.4 93.5 %all-gather.27.cloned.1.call-done = bf16[2048,4096]{1,0:T(8,128)(2,1)} async-done(((bf16[128,4096]{1,0:T(8,128)(2,1)}), bf16[2048,4096]{1,0:T(8,128)(2,1)}) %all-gather.27.cloned.1.call-update) | async-done | bytes 16777232 | tf_op jit(solution)/shard_map/all_gather | solution.py:154
  734.5 61.2 %all-reduce.12.cloned.1.call-done = bf16[512,2048]{1,0:T(8,128)(2,1)} async-done(((bf16[512,2048]{1,0:T(8,128)(2,1)}), bf16[512,2048]{1,0:T(8,128)(2,1)}) %all-reduce.12.cloned.1.call-update) | async-done | bytes 2097168 | tf_op jit(solution)/shard_map/psum | solution.py:172
  821.7 26.1 %while.37 = (s32[]{:T(128)}, f32[1,512,8,128]{1,3,2,0:T(8,128)S(1)}, f32[1,2048,8,128]{3,1,2,0:T(8,128)}, f32[1,2048,8,128]{3,1,2,0:T(8,128)}, s32[1,512]{1,0:T(...) while((s32[]{:T(128)}, ...), condition=%wide.region_20.0_spmd.clone, body=%wide.region_16.20_spmd.clone.sunk | while | flops 2713454592 | bytes 62719392 | solution.py:266
  823.7 18.7 conditional.7
  900.5 68.2 %reduce-scatter.8.cloned.1.call-done = bf16[1,512,8,128]{1,3,2,0:T(8,128)(2,1)} async-done(((bf16[1,2048,8,128]{1,3,2,0:T(8,128)(2,1)}), bf16[1,512,8,128]{1,3,2,0:T(8,128)(2,1)}) %reduce-scatter.8.cloned.1.call-update) | async-done | bytes 1048592 | tf_op jit(solution)/shard_map/reduce_scatter | solution.py:270
  975.7 72.6 %reduce-scatter.10.cloned.1.call-done = bf16[1,512,8,128]{1,3,2,0:T(8,128)(2,1)} async-done(((bf16[1,2048,8,128]{1,3,2,0:T(8,128)(2,1)}), bf16[1,512,8,128]{1,3,2,0:T(8,128)(2,1)}) %reduce-scatter.10.cloned.1.call-update) | async-done | bytes 1048592 | tf_op jit(solution)/shard_map/reduce_scatter | solution.py:273
  1077.0 44.7 %pad_maximum_fusion = f32[2048,8192]{1,0:T(8,128)} fusion(f32[2048,4096]{1,0:T(8,128)} %convolution_bitcast_fusion, f32[2048,4096]{1,0:T(8,128)} %fusion.112), kind=kLoop, calls=%fused_computation.66 | loop fusion | flops 16777216 | bytes 134217728 | tf_op jit(solution)/shard_map/concatenate | solution.py:176
  1169.1 61.3 %all-reduce.4 = (f32[2048]{0:T(1024)S(1)}, f32[2048]{0:T(1024)S(1)}, f32[2048]{0:T(1024)S(1)}, f32[2048]{0:T(1024)S(1)}) all-reduce(f32[2048]{0:T(1024)S(1)} %get-tuple-element.621, f32[2048]{0:T(1024)S(1)} %get-tuple-element.626, f32[2048]{0:T(1024)S(1)} %copy-done.21, ...), channel_id=9, replica_groups=mesh['fsdp'=4,'context'=4,'tensor'=2] {'fsdp','context'}, use_global_device_ids=true, to_apply=%region_32.33.clone | all-reduce | flops 8192 | bytes 65536
  1241.6 561.0 %reduce-scatter.20.cloned.1.call-done = f32[128,8192]{1,0:T(8,128)} async-done(((f32[2048,8192]{1,0:T(8,128)}), f32[128,8192]{1,0:T(8,128)}) %reduce-scatter.20.cloned.1.call-update) | async-done | bytes 4194320 | tf_op jit(solution)/shard_map/reduce_scatter | solution.py:175
  1807.3 102.4 %reduce-scatter.18.cloned.1.call-done = f32[128,1024]{1,0:T(8,128)} async-done(((f32[2048,1024]{1,0:T(8,128)}), f32[128,1024]{1,0:T(8,128)}) %reduce-scatter.18.cloned.1.call-update) | async-done | bytes 524304 | tf_op jit(solution)/shard_map/reduce_scatter | solution.py:309
  1909.7 107.6 %reduce-scatter.12.cloned.1.call-done = f32[128,1024]{1,0:T(8,128)} async-done(((f32[2048,1024]{1,0:T(8,128)}), f32[128,1024]{1,0:T(8,128)}) %reduce-scatter.12.cloned.1.call-update) | async-done | bytes 524304 | tf_op jit(solution)/shard_map/reduce_scatter | solution.py:306
  2017.3 107.6 %reduce-scatter.16.cloned.1.call-done = f32[128,1024]{1,0:T(8,128)} async-done(((f32[2048,1024]{1,0:T(8,128)}), f32[128,1024]{1,0:T(8,128)}) %reduce-scatter.16.cloned.1.call-update) | async-done | bytes 524304 | tf_op jit(solution)/shard_map/reduce_scatter | solution.py:308
  2124.9 107.6 %reduce-scatter.14.cloned.1.call-done = f32[128,1024]{1,0:T(8,128)} async-done(((f32[2048,1024]{1,0:T(8,128)}), f32[128,1024]{1,0:T(8,128)}) %reduce-scatter.14.cloned.1.call-update) | async-done | bytes 524304 | tf_op jit(solution)/shard_map/reduce_scatter | solution.py:307
  (240 shorter events, 313.9 us)
Async XLA Ops:
  7.2 68.3 %all-gather.19.cloned.1.call-start = ((), (), s32[]{:S(2)}) async-start(), calls=%async_computation.10 | async-start | bytes 4456448 | tf_op jit(solution)/shard_map/all_gather | solution.py:69
  7.9 106.8 %all-gather.13.cloned.1.call-start = ((), (), s32[]{:S(2)}) async-start(), calls=%async_computation.7 | async-start | bytes 4456448 | tf_op jit(solution)/shard_map/all_gather | solution.py:68
  8.7 157.2 %all-gather.17.cloned.1.call-start = ((), (), s32[]{:S(2)}) async-start(), calls=%async_computation.9 | async-start | bytes 4456448 | tf_op jit(solution)/shard_map/all_gather | solution.py:67
  9.4 237.8 %all-gather.21.cloned.1.call-start = ((), (), s32[]{:S(2)}) async-start(), calls=%async_computation.11 | async-start | bytes 5242880 | tf_op jit(solution)/shard_map/all_gather | solution.py:110
  43.7 122.2 %copy-start.14 = (f32[16,1,128]{2,1,0:T(1,128)}, f32[16,1,128]{2,1,0:T(1,128)S(1)}, u32[]{:S(2)}) copy-start(f32[16,1,128]{2,1,0:T(1,128)S(1)} %convert_element_type.182) | copy-start | bytes 24580
  72.7 93.2 %copy-start.29 = (f32[16,1,128]{2,1,0:T(1,128)}, f32[16,1,128]{2,1,0:T(1,128)S(1)}, u32[]{:S(2)}) copy-start(f32[16,1,128]{2,1,0:T(1,128)S(1)} %convert_element_type.183) | copy-start | bytes 24580
  81.5 246.9 %all-gather.15.cloned.1.call-start = ((), (), s32[]{:S(2)}) async-start(), calls=%async_computation.8 | async-start | bytes 5242880 | tf_op jit(solution)/shard_map/all_gather | solution.py:109
  120.8 258.7 %all-gather.23.cloned.1.call-start = ((), (), s32[]{:S(2)}) async-start(), calls=%async_computation.12 | async-start | bytes 4456448 | tf_op jit(solution)/shard_map/all_gather | solution.py:70
  121.3 326.0 %all-reduce.10.cloned.1.call-start = ((), (), s32[]{:S(2)}) async-start(), calls=%async_computation.13 | async-start | bytes 4194304 | tf_op jit(solution)/shard_map/psum | solution.py:148
  385.7 190.3 %all-gather.25.cloned.1.call-start = ((), (), s32[]{:S(2)}) async-start(), calls=%async_computation.14 | async-start | bytes 17825792 | tf_op jit(solution)/shard_map/all_gather | solution.py:153
  386.4 316.4 %all-gather.27.cloned.1.call-start = ((), (), s32[]{:S(2)}) async-start(), calls=%async_computation.15 | async-start | bytes 17825792 | tf_op jit(solution)/shard_map/all_gather | solution.py:154
  387.2 408.5 %all-reduce.12.cloned.1.call-start = ((), (), s32[]{:S(2)}) async-start(), calls=%async_computation.16 | async-start | bytes 4194304 | tf_op jit(solution)/shard_map/psum | solution.py:172
  417.4 383.5 %copy-start.16 = (f32[16,1,128]{2,1,0:T(1,128)}, f32[16,1,128]{2,1,0:T(1,128)S(1)}, u32[]{:S(2)}) copy-start(f32[16,1,128]{2,1,0:T(1,128)S(1)} %convert_element_type.184) | copy-start | bytes 24580
  446.4 129.6 %copy-start.31 = (f32[16,1,128]{2,1,0:T(1,128)}, f32[16,1,128]{2,1,0:T(1,128)S(1)}, u32[]{:S(2)}) copy-start(f32[16,1,128]{2,1,0:T(1,128)S(1)} %convert_element_type.185) | copy-start | bytes 24580
  449.7 351.1 %copy-start.19 = (f32[512]{0:T(512)}, f32[512]{0:T(512)S(1)}, u32[]{:S(2)}) copy-start(f32[512]{0:T(512)S(1)} %broadcast_multiply_fusion.4) | copy-start | bytes 6148
  450.7 350.2 %copy-start.27 = (f32[512]{0:T(512)}, f32[512]{0:T(512)S(1)}, u32[]{:S(2)}) copy-start(f32[512]{0:T(512)S(1)} %add_rsqrt_fusion) | copy-start | bytes 6148
  734.4 234.4 %reduce-scatter.8.cloned.1.call-start = ((), (), s32[]{:S(2)}) async-start(), calls=%async_computation.17 | async-start | bytes 5242880 | tf_op jit(solution)/shard_map/reduce_scatter | solution.py:270
  855.2 193.0 %reduce-scatter.10.cloned.1.call-start = ((), (), s32[]{:S(2)}) async-start(), calls=%async_computation.18 | async-start | bytes 5242880 | tf_op jit(solution)/shard_map/reduce_scatter | solution.py:273
  862.6 303.0 %all-reduce.14.cloned.1.call-start = ((), (), s32[]{:S(2)}) async-start(), calls=%async_computation.24 | async-start | bytes 8388608 | tf_op jit(solution)/shard_map/psum | solution.py:163
  1057.0 745.6 %reduce-scatter.20.cloned.1.call-start = ((), (), s32[]{:S(2)}) async-start(), calls=%async_computation.23 | async-start | bytes 71303168 | tf_op jit(solution)/shard_map/reduce_scatter | solution.py:175
  1121.7 788.0 %reduce-scatter.18.cloned.1.call-start = ((), (), s32[]{:S(2)}) async-start(), calls=%async_computation.22 | async-start | bytes 8912896 | tf_op jit(solution)/shard_map/reduce_scatter | solution.py:309
  1130.8 886.5 %reduce-scatter.12.cloned.1.call-start = ((), (), s32[]{:S(2)}) async-start(), calls=%async_computation.19 | async-start | bytes 8912896 | tf_op jit(solution)/shard_map/reduce_scatter | solution.py:306
  1138.0 986.9 %reduce-scatter.16.cloned.1.call-start = ((), (), s32[]{:S(2)}) async-start(), calls=%async_computation.21 | async-start | bytes 8912896 | tf_op jit(solution)/shard_map/reduce_scatter | solution.py:308
  1145.2 1087.3 %reduce-scatter.14.cloned.1.call-start = ((), (), s32[]{:S(2)}) async-start(), calls=%async_computation.20 | async-start | bytes 8912896 | tf_op jit(solution)/shard_map/reduce_scatter | solution.py:307
  (36 other events, 409.0 us)
Sparse Core Ops, SparseCore 0:
  10.2 53.3 all-gather.18
  65.8 48.8 all-gather.12
  117.0 48.8 all-gather.16
  167.9 79.2 all-gather.20
  249.2 79.2 all-gather.14
  330.5 48.8 all-gather.22
  385.8 61.5 all-reduce.9
  449.6 126.4 all-gather.24
  578.2 124.5 all-gather.26
  734.5 61.1 all-reduce.11
  855.3 113.3 reduce-scatter.7
  970.9 77.2 reduce-scatter.9
  1057.1 108.4 all-reduce.13
  1169.7 632.8 reduce-scatter.19
  1807.1 102.5 reduce-scatter.17
  1914.2 103.0 reduce-scatter.11
  2021.8 103.0 reduce-scatter.15
  2129.4 103.0 reduce-scatter.13
where the time goes:
time: 2250 us; the launch traced here: 2240 us
  waiting for transfers between devices  1690 us (75%)
  matrix products  208 us (9%)
  blocking collectives  184 us (8%)
  other arithmetic  87.4 us (4%)
  local copies, waits for them, and re-layouts  52.7 us (2%)
    reduce_scatter x1, waiting for transfers between devices, per_device(): lax.psum_scatter(jnp.concatenate((contract(normed_two, grad_pre, 0, 0), c...  561 us
    all_gather x1, waiting for transfers between devices, per_device(): lax.all_gather(up_weight, ('fsdp', 'context'), axis=0, tiled=True)  125 us
    dot_general x12, matrix products, contract(): lax.dot_general(left, right, (((left_dim,), (right_dim,)), ((), ())), pre...  116 us
    reduce_scatter x1, waiting for transfers between devices, per_device(): lax.psum_scatter(query_term, ('fsdp', 'context'), scatter_dimension=0, ti...  108 us
    reduce_scatter x1, waiting for transfers between devices, per_device(): lax.psum_scatter(key_term, ('fsdp', 'context'), scatter_dimension=0, tile...  108 us
    reduce_scatter x1, waiting for transfers between devices, per_device(): lax.psum_scatter(value_term, ('fsdp', 'context'), scatter_dimension=0, ti...  108 us
    reduce_scatter x1, waiting for transfers between devices, per_device(): lax.psum_scatter(out_term, ('fsdp', 'context'), scatter_dimension=0, tile...  102 us
    all_gather x1, waiting for transfers between devices, per_device(): lax.all_gather(down_weight, ('fsdp', 'context'), axis=0, tiled=True)  93.5 us
  transfers between devices with their start and end apart: 18, of which 17 were waited for; matrix products, arithmetic and copies ran while one was open for 11% of the time, Pallas kernels for 0%

commit v1 on v0

v1 whole, which is shorter than its diff:
```python
import functools

import jax
import jax.numpy as jnp
from jax import lax
from jax.experimental import pallas as pl
from jax.experimental.pallas import tpu as pltpu
from jax.sharding import PartitionSpec as P

HEAD = 128

epsilon = 1e-05
big_negative = -1e30
density = 0.3989422804014327
half_root = 0.7071067811865476
bf16 = jnp.bfloat16
f32 = jnp.float32


def contract(left, right, left_dim, right_dim):
    return lax.dot_general(
        left, right, (((left_dim,), (right_dim,)), ((), ())), preferred_element_type=f32
    )


def norm_stats(row_vals):
    average = jnp.mean(row_vals, axis=-1, keepdims=True)
    centered = row_vals - average
    variance = jnp.mean(centered * centered, axis=-1, keepdims=True)
    inv_std = lax.rsqrt(variance + epsilon)
    return (centered * inv_std, inv_std)


def norm_back(grad_out, normed_hat, inv_std, gain_vals):
    scaled = grad_out * gain_vals
    first_mean = jnp.mean(scaled, axis=-1, keepdims=True)
    second_mean = jnp.mean(scaled * normed_hat, axis=-1, keepdims=True)
    return inv_std * (scaled - first_mean - normed_hat * second_mean)


def attn_forward_kernel(reach, factor, flags, *refs):
    seg_row, seg_cols, query, own_key, own_value = refs[:5]
    far = refs[5 : 5 + 2 * reach]
    out, log_sum, run_max, run_sum, run_acc = refs[5 + 2 * reach :]
    rows = query.shape[0]

    def block(key_ref, value_ref, index, first):
        scores = contract(key_ref[...], query[...], 1, 1) * factor
        allowed = seg_cols[index] == seg_row[...]
        if first:
            key_pos = lax.broadcasted_iota(jnp.int32, (rows, rows), 0)
            query_pos = lax.broadcasted_iota(jnp.int32, (rows, rows), 1)
            allowed = allowed & (key_pos <= query_pos)
        scores = jnp.where(allowed, scores, big_negative)
        peak = jnp.max(scores, axis=0, keepdims=True)
        if not first:
            peak = jnp.maximum(peak, run_max[...])
        terms = jnp.where(allowed, jnp.exp(scores - peak), 0.0)
        total = jnp.sum(terms, axis=0, keepdims=True)
        value_sum = contract(value_ref[...], terms.astype(bf16), 0, 0)
        if first:
            run_sum[...] = total
            run_acc[...] = value_sum
        else:
            shrink = jnp.exp(run_max[...] - peak)
            run_sum[...] = run_sum[...] * shrink + total
            run_acc[...] = run_acc[...] * shrink + value_sum
        run_max[...] = peak

    block(own_key, own_value, 0, True)
    for step in range(reach):

        @pl.when(flags[step] > 0)
        def _(step=step):
            block(far[2 * step], far[2 * step + 1], step + 1, False)

    out[...] = (run_acc[...] / run_sum[...]).T.astype(bf16)
    log_sum[0] = run_max[...] + jnp.log(run_sum[...])


def attn_backward_kernel(reach, factor, flags, *refs):
    seg_row, seg_cols, query, own_key, own_value, grad_out, attn_out, log_sum = refs[:8]
    far = refs[8 : 8 + 2 * reach]
    outs = refs[8 + 2 * reach :]
    grad_query, own_key_grad, own_value_grad = outs[:3]
    far_grads = outs[3 : 3 + 2 * reach]
    acc = outs[3 + 2 * reach]
    rows = query.shape[0]
    delta = jnp.sum(
        (grad_out[...].astype(f32) * attn_out[...].astype(f32)).T, axis=0, keepdims=True
    )

    def block(key_ref, value_ref, key_grad, value_grad, index, first):
        scores = contract(key_ref[...], query[...], 1, 1) * factor
        allowed = seg_cols[index] == seg_row[...]
        if first:
            key_pos = lax.broadcasted_iota(jnp.int32, (rows, rows), 0)
            query_pos = lax.broadcasted_iota(jnp.int32, (rows, rows), 1)
            allowed = allowed & (key_pos <= query_pos)
        probs = jnp.where(
            allowed, jnp.exp(jnp.where(allowed, scores, big_negative) - log_sum[0]), 0.0
        )
        grad_probs = contract(value_ref[...], grad_out[...], 1, 1)
        grad_scores = (probs * (grad_probs - delta)).astype(bf16)
        key_grad[...] = (
            jnp.dot(grad_scores, query[...], preferred_element_type=f32) * factor
        ).astype(bf16)
        value_grad[...] = jnp.dot(
            probs.astype(bf16), grad_out[...], preferred_element_type=f32
        ).astype(bf16)
        update = contract(key_ref[...], grad_scores, 0, 0)
        if first:
            acc[...] = update
        else:
            acc[...] += update

    block(own_key, own_value, own_key_grad, own_value_grad, 0, True)
    for step in range(reach):

        @pl.when(flags[step] > 0)
        def _(step=step):
            block(
                far[2 * step],
                far[2 * step + 1],
                far_grads[2 * step],
                far_grads[2 * step + 1],
                step + 1,
                False,
            )

        @pl.when(flags[step] == 0)
        def _(step=step):
            far_grads[2 * step][...] = jnp.zeros_like(far_grads[2 * step])
            far_grads[2 * step + 1][...] = jnp.zeros_like(far_grads[2 * step + 1])

    grad_query[...] = (acc[...] * factor).T.astype(bf16)


def head_spec(rows, first):
    return pl.BlockSpec((rows, HEAD), lambda h, flags, first=first: (0, first + h))


def attention_forward(flags, seg_row, seg_cols, qkv, far, heads):
    rows = qkv.shape[0]
    reach = len(far)
    in_specs = [
        pl.BlockSpec((1, rows), lambda h, flags: (0, 0)),
        pl.BlockSpec(seg_cols.shape, lambda h, flags: (0, 0, 0)),
        head_spec(rows, 0),
        head_spec(rows, heads),
        head_spec(rows, 2 * heads),
    ]
    operands = [seg_row, seg_cols, qkv, qkv, qkv]
    for piece in far:
        in_specs += [head_spec(rows, 0), head_spec(rows, heads)]
        operands += [piece, piece]
    pairs = heads * rows * rows * (reach + 1)
    return pl.pallas_call(
        functools.partial(attn_forward_kernel, reach, HEAD ** (-0.5)),
        out_shape=(
            jax.ShapeDtypeStruct((rows, heads * HEAD), bf16),
            jax.ShapeDtypeStruct((heads, 1, rows), f32),
        ),
        grid_spec=pltpu.PrefetchScalarGridSpec(
            num_scalar_prefetch=1,
            grid=(heads,),
            in_specs=in_specs,
            out_specs=(
                head_spec(rows, 0),
                pl.BlockSpec((1, 1, rows), lambda h, flags: (h, 0, 0)),
            ),
            scratch_shapes=[
                pltpu.VMEM((1, rows), f32),
                pltpu.VMEM((1, rows), f32),
                pltpu.VMEM((HEAD, rows), f32),
            ],
        ),
        cost_estimate=pl.CostEstimate(
            flops=4 * HEAD * pairs, transcendentals=pairs, bytes_accessed=16 * rows * heads * HEAD
        ),
        name="attention_forward",
    )(flags, *operands)


def attention_backward(flags, seg_row, seg_cols, qkv, far, grad_out, attn_out, log_sum, heads):
    rows = qkv.shape[0]
    reach = len(far)
    in_specs = [
        pl.BlockSpec((1, rows), lambda h, flags: (0, 0)),
        pl.BlockSpec(seg_cols.shape, lambda h, flags: (0, 0, 0)),
        head_spec(rows, 0),
        head_spec(rows, heads),
        head_spec(rows, 2 * heads),
        head_spec(rows, 0),
        head_spec(rows, 0),
        pl.BlockSpec((1, 1, rows), lambda h, flags: (h, 0, 0)),
    ]
    operands = [seg_row, seg_cols, qkv, qkv, qkv, grad_out, attn_out, log_sum]
    for piece in far:
        in_specs += [head_spec(rows, 0), head_spec(rows, heads)]
        operands += [piece, piece]
    pairs = heads * rows * rows * (reach + 1)
    out = jax.ShapeDtypeStruct((rows, heads * HEAD), bf16)
    return pl.pallas_call(
        functools.partial(attn_backward_kernel, reach, HEAD ** (-0.5)),
        out_shape=(out,) * (3 + 2 * reach),
        grid_spec=pltpu.PrefetchScalarGridSpec(
            num_scalar_prefetch=1,
            grid=(heads,),
            in_specs=in_specs,
            out_specs=(head_spec(rows, 0),) * (3 + 2 * reach),
            scratch_shapes=[pltpu.VMEM((HEAD, rows), f32)],
        ),
        cost_estimate=pl.CostEstimate(
            flops=10 * HEAD * pairs, transcendentals=pairs, bytes_accessed=32 * rows * heads * HEAD
        ),
        name="attention_backward",
    )(flags, *operands)


def swap(array, axis, size):
    return lax.ppermute(array, axis, [(i, i ^ 1) for i in range(size)])


def line_move(array, axis, size, step):
    moves = [(i, i + step) for i in range(size) if 0 <= i + step < size]
    return lax.ppermute(array, axis, moves)


def direct_sum(own, axis, size, me):
    total = own(me)
    for step in range(1, size):
        target = lax.rem(me + step, size)
        moves = [(i, (i + step) % size) for i in range(size)]
        total = total + lax.ppermute(own(target).astype(bf16), axis, moves).astype(f32)
    return total


def tensor_sum(part, size):
    part = part.astype(bf16)
    if size == 2:
        return part.astype(f32) + swap(part, "tensor", 2).astype(f32)
    return lax.psum(part, "tensor").astype(f32)


def grad_scatter(part, sizes):
    fsdp, context = sizes["fsdp"], sizes["context"]
    chips = fsdp // 2
    mine = lax.axis_index("fsdp")
    core, chip = lax.rem(mine, 2), lax.div(mine, 2)
    place = lax.axis_index("context")

    def both_cores(target):
        sent = part(2 * target + 1 - core).astype(bf16)
        return part(2 * target + core) + swap(sent, "fsdp", fsdp).astype(f32)

    rows = both_cores(chip)
    for step in range(1, chips):
        sent = both_cores(lax.rem(chip + step, chips)).astype(bf16)
        moves = [(i, (i + 2 * step) % fsdp) for i in range(fsdp)]
        rows = rows + lax.ppermute(sent, "fsdp", moves).astype(f32)
    rows = rows.astype(bf16)
    count = rows.shape[0] // context
    return direct_sum(
        lambda t: lax.dynamic_slice_in_dim(rows, t * count, count, 0).astype(f32),
        "context",
        context,
        place,
    )


def product_scatter(left, right, sizes):
    block = left.shape[1] // sizes["fsdp"]

    def part(index):
        return contract(lax.dynamic_slice_in_dim(left, index * block, block, 1), right, 0, 0)

    return grad_scatter(part, sizes)


def vector_scatter(rows, sizes):
    fsdp, context = sizes["fsdp"], sizes["context"]
    if sizes["tensor"] == 2:
        rows = rows + swap(rows, "tensor", 2)
    else:
        rows = lax.psum(rows, "tensor")
    count = rows.shape[1] // (fsdp * context)
    mine, place = lax.axis_index("fsdp"), lax.axis_index("context")
    width = context * count

    def shift_sum(total, axis, size, me, width):
        own = lambda t: lax.dynamic_slice_in_dim(total, t * width, width, 1)
        result = own(me)
        for step in range(1, size):
            moves = [(i, (i + step) % size) for i in range(size)]
            result = result + lax.ppermute(own(lax.rem(me + step, size)), axis, moves)
        return result

    rows = shift_sum(rows, "fsdp", fsdp, mine, width)
    return shift_sum(rows, "context", context, place, count)


def per_device(
    sizes,
    tokens,
    segments,
    query_weight,
    key_weight,
    value_weight,
    out_weight,
    up_weight,
    down_weight,
    attn_gain,
    attn_bias,
    mlp_gain,
    mlp_bias,
    cotangent,
):
    seq_dev, group_len, model_width = tokens.shape
    assert seq_dev == 1
    shard_rows, local_width = query_weight.shape
    hidden_local = up_weight.shape[1]
    heads = local_width // HEAD
    seq_len = segments.shape[1]
    context, tensor = sizes["context"], sizes["tensor"]
    place = lax.axis_index("context")
    weight_axes = ("fsdp", "context")

    vectors = jnp.stack([attn_gain, attn_bias, mlp_gain, mlp_bias], axis=1)
    vectors = jnp.pad(vectors, ((0, 0), (0, HEAD - 4)))
    attn_full = lax.all_gather(
        jnp.concatenate([query_weight, key_weight, value_weight, out_weight, vectors], axis=1),
        weight_axes,
        axis=0,
        tiled=True,
    )
    mlp_full = lax.all_gather(
        jnp.concatenate([up_weight, down_weight], axis=1), weight_axes, axis=0, tiled=True
    )
    full_qkv = attn_full[:, : 3 * local_width]
    full_out = attn_full[:, 3 * local_width : 4 * local_width]
    vecs = attn_full[:, 4 * local_width : 4 * local_width + 4].T.astype(f32)
    gain_one, bias_one, gain_two, bias_two = vecs[0], vecs[1], vecs[2], vecs[3]
    full_up = mlp_full[:, :hidden_local]
    full_down = mlp_full[:, hidden_local:]

    rows_in = tokens.reshape(group_len, model_width).astype(f32)
    hat_one, inv_one = norm_stats(rows_in)
    normed_one = (hat_one * gain_one + bias_one).astype(bf16)
    qkv = jnp.dot(normed_one, full_qkv, preferred_element_type=f32).astype(bf16)

    reach = min(context - 1, -(-(seq_len // 2 - 1) // group_len))
    far = []
    piece = qkv[:, local_width:]
    for _ in range(reach):
        piece = line_move(piece, "context", context, 1)
        far.append(piece)
    first = place * group_len
    seg_row = lax.dynamic_slice_in_dim(segments, first, group_len, 1)
    seg_cols = [seg_row]
    for back in range(1, reach + 1):
        start = jnp.maximum(first - back * group_len, 0)
        block = lax.dynamic_slice_in_dim(segments, start, group_len, 1)
        seg_cols.append(jnp.where(place >= back, block, -1))
    flags = jnp.stack([(cols[0, -1] == seg_row[0, 0]).astype(jnp.int32) for cols in seg_cols[1:]])
    seg_cols = jnp.concatenate(seg_cols, axis=0)[:, :, None]

    attn, log_sum = attention_forward(flags, seg_row, seg_cols, qkv, far, heads)
    residual = rows_in + tensor_sum(contract(attn, full_out, 1, 1), tensor)

    hat_two, inv_two = norm_stats(residual)
    normed_two = (hat_two * gain_two + bias_two).astype(bf16)
    pre_act = jnp.dot(normed_two, full_up, preferred_element_type=f32)
    normal_cdf = 0.5 * (1.0 + lax.erf(pre_act * half_root))
    activated = (pre_act * normal_cdf).astype(bf16)
    slope = normal_cdf + pre_act * density * jnp.exp(-0.5 * pre_act * pre_act)
    grad_rows = cotangent.reshape(group_len, model_width)
    grad_act = jnp.dot(grad_rows, full_down, preferred_element_type=f32)
    grad_pre = (grad_act * slope).astype(bf16)
    norm_two_part = contract(grad_pre, full_up, 1, 1).astype(bf16)
    grad_norm_two = tensor_sum(norm_two_part, tensor)

    down_grad = product_scatter(grad_rows, activated, sizes)
    up_grad = product_scatter(normed_two, grad_pre, sizes)
    mlp_out = tensor_sum(contract(activated, full_down, 1, 1), tensor)
    output = (residual + mlp_out).astype(bf16).reshape(tokens.shape)

    grad_resid = grad_rows.astype(f32) + norm_back(grad_norm_two, hat_two, inv_two, gain_two)
    grad_branch = grad_resid.astype(bf16)
    grad_attn = jnp.dot(grad_branch, full_out, preferred_element_type=f32).astype(bf16)
    out_grad = product_scatter(grad_branch, attn, sizes)

    results = attention_backward(
        flags, seg_row, seg_cols, qkv, far, grad_attn, attn, log_sum, heads
    )
    query_bf = results[0]
    query_grad = product_scatter(normed_one, query_bf, sizes)
    carry = None
    for back in range(reach, -1, -1):
        term = jnp.concatenate(results[1 + 2 * back : 3 + 2 * back], axis=1)
        if carry is not None:
            term = (term.astype(f32) + carry.astype(f32)).astype(bf16)
        if back > 0:
            carry = line_move(term, "context", context, -1)
    pair_bf = term
    pair_grad = product_scatter(normed_one, pair_bf, sizes)
    input_part = contract(query_bf, full_qkv[:, :local_width], 1, 1) + contract(
        pair_bf, full_qkv[:, local_width:], 1, 1
    )
    norm_one_part = input_part.astype(bf16)
    grad_norm_one = tensor_sum(norm_one_part, tensor)
    tokens_grad = (
        (grad_resid + norm_back(grad_norm_one, hat_one, inv_one, gain_one))
        .astype(bf16)
        .reshape(tokens.shape)
    )
    one_f, two_f = norm_one_part.astype(f32), norm_two_part.astype(f32)
    vector_sums = jnp.stack(
        [
            jnp.sum(one_f * hat_one, axis=0),
            jnp.sum(one_f, axis=0),
            jnp.sum(two_f * hat_two, axis=0),
            jnp.sum(two_f, axis=0),
        ],
        axis=0,
    )
    vector_grads = vector_scatter(vector_sums, sizes)
    return (
        output,
        tokens_grad,
        query_grad,
        pair_grad[:, :local_width],
        pair_grad[:, local_width:],
        out_grad,
        up_grad,
        down_grad,
        vector_grads[0],
        vector_grads[1],
        vector_grads[2],
        vector_grads[3],
    )


def solution(mesh):
    weight = P(("fsdp", "context"), "tensor")
    vector = P(("fsdp", "context"))
    rows = P("fsdp", "context", None)
    return jax.shard_map(
        functools.partial(per_device, dict(mesh.shape)),
        mesh=mesh,
        in_specs=(rows, P("fsdp", None)) + (weight,) * 6 + (vector,) * 4 + (rows,),
        out_specs=(rows, rows) + (weight,) * 6 + (vector,) * 4,
        check_vma=False,
    )
```

time: 2250 us -> 1070 us (0.48)
  waiting for transfers between devices: 1690 us -> 669 us
  blocking collectives: 184 us -> 0 us
  starting transfers between devices: 1.11 us -> 98.2 us
  matrix products: 208 us -> 167 us
  local copies, waits for them, and re-layouts: 52.7 us -> 19 us
  other arithmetic: 87.4 us -> 62 us
  Pallas kernels: 0 us -> 24.3 us
    reduce_scatter x7 -> x0, waiting for transfers between devices: 1130 us -> none  [the longest x1 561 us: per_device(): lax.psum_scatter(jnp.concatenate((contract(normed_two, grad_pre, 0, 0), c...]
    ppermute x0 -> x45, waiting for transfers between devices: none -> 536 us  [the longest x4 183 us: line_move(): return lax.ppermute(array, axis, moves)]
    all_gather x8 -> x2, waiting for transfers between devices: 481 us -> 132 us  [the longest x1 94.9 us: per_device(): lax.all_gather(jnp.concatenate([query_weight, key_weight, value_weight, o...]
    all_gather x4 -> x0, blocking collectives: 122 us -> none  [the longest x1 34.3 us: per_device(): lax.all_gather(attn_gain, ('fsdp', 'context'), axis=0, tiled=True)]
    ppermute x0 -> x45, starting transfers between devices: none -> 98.2 us  [the longest x15 63.7 us: direct_sum(): lax.ppermute(own(target).astype(bf16), axis, moves).astype(f32)]
    psum x3 -> x0, waiting for transfers between devices: 73.5 us -> none  [the longest x1 61.2 us: per_device(): lax.psum(contract(grad_pre, full_up, 1, 1).astype(jnp.bfloat16), 'tensor')]
    unnamed x1 -> x0, blocking collectives: 61.3 us -> none
    dot_general x13 -> x4, matrix products: 91.7 us -> 49.2 us  [the longest x1 17.1 us: per_device(): grad_act = jnp.dot(grad_rows, full_down, preferred_element_type=f32)]
  transfers between devices with their start and end apart: 18 -> 47, of which waited for: 17 -> 25; matrix products, arithmetic and copies ran while one was open for 11% -> 18% of each run, Pallas kernels for 0% -> 2%
where the time goes in v1:
time: 1070 us; the launch traced here: 1060 us
  waiting for transfers between devices  669 us (63%)
  matrix products  167 us (16%)
  starting transfers between devices  98.2 us (9%)
  other arithmetic  62 us (6%)
  Pallas kernels  24.3 us (2%)
  local copies, waits for them, and re-layouts  19 us (2%)
  between operations  16.4 us (2%)
    ppermute x4, waiting for transfers between devices, line_move(): return lax.ppermute(array, axis, moves)  183 us
    ppermute x15, waiting for transfers between devices, direct_sum(): lax.ppermute(own(target).astype(bf16), axis, moves).astype(f32)  132 us
    ppermute x5, waiting for transfers between devices, grad_scatter(): rows = rows + lax.ppermute(sent, 'fsdp', moves).astype(f32)  122 us
    dot_general x25, matrix products, contract(): lax.dot_general(left, right, (((left_dim,), (right_dim,)), ((), ())), pre...  118 us
    ppermute x15, waiting for transfers between devices, swap(): return lax.ppermute(array, axis, [(i, i ^ 1) for i in range(size)])  96.5 us
    all_gather x1, waiting for transfers between devices, per_device(): lax.all_gather(jnp.concatenate([query_weight, key_weight, value_weight, o...  94.9 us
    ppermute x15, starting transfers between devices, direct_sum(): lax.ppermute(own(target).astype(bf16), axis, moves).astype(f32)  63.7 us
    all_gather x1, waiting for transfers between devices, per_device(): lax.all_gather(jnp.concatenate([up_weight, down_weight], axis=1), weight_...  37.5 us
  transfers between devices with their start and end apart: 47, of which 25 were waited for; matrix products, arithmetic and copies ran while one was open for 18% of the time, Pallas kernels for 2%

profile of v1, /device:TPU:0, one launch (start us, length us, event | category | flops | bytes accessed | tf_op | source)
XLA Modules:
  0.0 1055.8 jit_solution(13063880821755951828)
XLA Ops:
  17.4 94.9 %all-gather.3.cloned.1.call-done = bf16[2048,4224]{1,0:T(8,128)(2,1)} async-done(((bf16[128,4224]{1,0:T(8,128)(2,1)}), bf16[2048,4224]{1,0:T(8,128)(2,1)}) %all-gather.3.cloned.1.call-update) | async-done | bytes 17301520 | tf_op jit(solution)/shard_map/all_gather | solution.py:331
  133.3 66.3 %collective-permute-done.refs_5_.refs_6_.refs_8_.refs_9_ = bf16[512,2048]{1,0:T(8,128)(2,1)} collective-permute-done((bf16[512,2048]{1,0:T(8,128)(2,1)S(1)}, bf16[512,2048]{1,0:T(8,128)(2,1)}, u32[]{:S(2)}, u32[]{:S(2)}) %collective-permute-start) | collective-permute-done | bytes 2097184 | tf_op jit(solution)/shard_map/ppermute | solution.py:227
  212.2 59.5 %collective-permute-done.1.refs_7_.refs_8_.refs_10_.refs_11_ = bf16[512,2048]{1,0:T(8,128)(2,1)} collective-permute-done((bf16[512,2048]{1,0:T(8,128)(2,1)}, bf16[512,2048]{1,0:T(8,128)(2,1)}, u32[]{:S(2)}, u32[]{:S(2)}) %collective-permute-start.1) | collective-permute-done | bytes 2097184 | tf_op jit(solution)/shard_map/ppermute | solution.py:227
  290.7 44.0 %collective-permute-done.2 = bf16[512,2048]{1,0:T(8,128)(2,1)} collective-permute-done((bf16[512,2048]{1,0:T(8,128)(2,1)}, bf16[512,2048]{1,0:T(8,128)(2,1)}, u32[]{:S(2)}, u32[]{:S(2)}) %collective-permute-start.2) | collective-permute-done | bytes 2097184 | tf_op jit(solution)/shard_map/ppermute | solution.py:222
  342.0 37.5 %all-gather.5.cloned.1.call-done = bf16[2048,8192]{1,0:T(8,128)(2,1)} async-done(((bf16[128,8192]{1,0:T(8,128)(2,1)}), bf16[2048,8192]{1,0:T(8,128)(2,1)}) %all-gather.5.cloned.1.call-update) | async-done | bytes 33554448 | tf_op jit(solution)/shard_map/all_gather | solution.py:337
  379.6 15.5 %multiply_convert_fusion = (bf16[512,4096]{1,0:T(8,128)(2,1)S(1)}, f32[512,4096]{1,0:T(8,128)}) fusion(bf16[512,2048]{1,0:T(8,128)(2,1)} %add_convert_fusion.10, bf16[2048,8192]{1,0:T(8,128)(2,1)} %all-gather.5.cloned.1.call-done), kind=kOutput, calls=%fused_computation.22 | convolution fusion | flops 8600420352 | bytes 31457280 | tf_op jit(solution)/shard_map/dot_general | solution.py:373
  395.1 17.1 %fusion.14 = bf16[512,4096]{1,0:T(8,128)(2,1)S(1)} fusion(f32[512,4096]{1,0:T(8,128)} %get-tuple-element.80, bf16[2048,8192]{1,0:T(8,128)(2,1)} %all-gather.5.cloned.1.call-done, bf16[1,512,2048]{2,1,0:T(8,128)(2,1)S(1)} %copy-done.12), kind=kOutput, calls=%fused_computation.15 | convolution fusion | flops 8610906112 | bytes 31457280 | tf_op jit(solution)/shard_map/dot_general | solution.py:378
  412.1 14.9 %fusion.51 = bf16[512,2048]{1,0:T(8,128)(2,1)} fusion(bf16[512,4096]{1,0:T(8,128)(2,1)S(1)} %fusion.14, bf16[2048,8192]{1,0:T(8,128)(2,1)} %all-gather.5.cloned.1.call-done), kind=kOutput, calls=%fused_computation.75 | convolution fusion | flops 8590983168 | bytes 23068672 | tf_op jit(solution)/shard_map/dot_general | solution.py:21
  428.9 13.8 %fusion.54 = bf16[512,2048]{1,0:T(8,128)(2,1)} fusion(bf16[512,4096]{1,0:T(8,128)(2,1)S(1)} %get-tuple-element.79, bf16[2048,8192]{1,0:T(8,128)(2,1)} %all-gather.5.cloned.1.call-done), kind=kOutput, calls=%fused_computation.76 | convolution fusion | flops 8590983168 | bytes 23068672 | tf_op jit(solution)/shard_map/dot_general | solution.py:21
  463.9 12.0 %collective-permute-done.4 = bf16[512,2048]{1,0:T(8,128)(2,1)} collective-permute-done((bf16[512,2048]{1,0:T(8,128)(2,1)}, bf16[512,2048]{1,0:T(8,128)(2,1)}, u32[]{:S(2)}, u32[]{:S(2)}) %collective-permute-start.4) | collective-permute-done | bytes 2097184 | tf_op jit(solution)/shard_map/ppermute | solution.py:222
  479.6 24.1 %collective-permute-done.3 = bf16[512,2048]{1,0:T(8,128)(2,1)S(1)} collective-permute-done((bf16[512,2048]{1,0:T(8,128)(2,1)}, bf16[512,2048]{1,0:T(8,128)(2,1)S(1)}, u32[]{:S(2)}, u32[]{:S(2)}) %collective-permute-start.3) | collective-permute-done | bytes 2097184 | tf_op jit(solution)/shard_map/ppermute | solution.py:222
  515.9 13.4 %attention_backward.1 = (bf16[512,1024]{1,0:T(8,128)(2,1)}, bf16[512,1024]{1,0:T(8,128)(2,1)}, bf16[512,1024]{1,0:T(8,128)(2,1)}, bf16[512,1024]{1,0:T(8,128)(2,...) custom-call(s32[2]{0:T(128)} %add_convert_fusion.15.flags, ...), custom_call_target="tpu_custom_call" | custom-call | flops 8053063680 | bytes 16777216 | tf_op jit(solution)/shard_map/attention_backward/pallas_call | solution.py:204
  546.9 57.0 %collective-permute-done.5 = bf16[512,2048]{1,0:T(8,128)(2,1)S(1)} collective-permute-done((bf16[512,2048]{1,0:T(8,128)(2,1)S(1)}, bf16[512,2048]{1,0:T(8,128)(2,1)S(1)}, u32[]{:S(2)}, u32[]{:S(2)}) %collective-permute-start.5) | collective-permute-done | bytes 2097184 | tf_op jit(solution)/shard_map/ppermute | solution.py:227
  608.7 19.8 %collective-permute-done.22 = bf16[512,1024]{1,0:T(8,128)(2,1)S(1)} collective-permute-done((bf16[512,1024]{1,0:T(8,128)(2,1)S(1)}, bf16[512,1024]{1,0:T(8,128)(2,1)S(1)}, u32[]{:S(2)}, u32[]{:S(2)}) %collective-permute-start.22) | collective-permute-done | bytes 1048608 | tf_op jit(solution)/shard_map/ppermute | solution.py:261
  638.7 16.1 %collective-permute-done.10 = bf16[512,1024]{1,0:T(8,128)(2,1)} collective-permute-done((bf16[512,1024]{1,0:T(8,128)(2,1)}, bf16[512,1024]{1,0:T(8,128)(2,1)}, u32[]{:S(2)}, u32[]{:S(2)}) %collective-permute-start.10) | collective-permute-done | bytes 1048608 | tf_op jit(solution)/shard_map/ppermute | solution.py:261
  712.1 16.3 %collective-permute-done.7 = bf16[512,2048]{1,0:T(8,128)(2,1)S(1)} collective-permute-done((bf16[512,2048]{1,0:T(8,128)(2,1)S(1)}, bf16[512,2048]{1,0:T(8,128)(2,1)S(1)}, u32[]{:S(2)}, u32[]{:S(2)}) %collective-permute-start.7) | collective-permute-done | bytes 2097184 | tf_op jit(solution)/shard_map/ppermute | solution.py:222
  731.6 13.1 %collective-permute-done.34 = bf16[512,4096]{1,0:T(8,128)(2,1)S(1)} collective-permute-done((bf16[512,4096]{1,0:T(8,128)(2,1)}, bf16[512,4096]{1,0:T(8,128)(2,1)S(1)}, u32[]{:S(2)}, u32[]{:S(2)}) %collective-permute-start.34) | collective-permute-done | bytes 4194336 | tf_op jit(solution)/shard_map/ppermute | solution.py:261
  759.6 72.7 %collective-permute-done.28 = bf16[512,4096]{1,0:T(8,128)(2,1)} collective-permute-done((bf16[512,4096]{1,0:T(8,128)(2,1)}, bf16[512,4096]{1,0:T(8,128)(2,1)}, u32[]{:S(2)}, u32[]{:S(2)}) %collective-permute-start.28) | collective-permute-done | bytes 4194336 | tf_op jit(solution)/shard_map/ppermute | solution.py:261
  862.6 39.5 %collective-permute-done.36 = bf16[128,4096]{1,0:T(8,128)(2,1)S(1)} collective-permute-done((bf16[128,4096]{1,0:T(8,128)(2,1)}, bf16[128,4096]{1,0:T(8,128)(2,1)S(1)}, u32[]{:S(2)}, u32[]{:S(2)}) %collective-permute-start.36) | collective-permute-done | bytes 1048608 | tf_op jit(solution)/shard_map/ppermute | solution.py:235
  902.2 21.7 %collective-permute-done.37 = bf16[128,4096]{1,0:T(8,128)(2,1)S(1)} collective-permute-done((bf16[128,4096]{1,0:T(8,128)(2,1)S(1)}, bf16[128,4096]{1,0:T(8,128)(2,1)S(1)}, u32[]{:S(2)}, u32[]{:S(2)}) %collective-permute-start.37) | collective-permute-done | bytes 1048608 | tf_op jit(solution)/shard_map/ppermute | solution.py:235
  932.5 43.2 %collective-permute-start.17 = (bf16[128,2048]{1,0:T(8,128)(2,1)S(1)}, bf16[128,2048]{1,0:T(8,128)(2,1)S(1)}, u32[]{:S(2)}, u32[]{:S(2)}) collective-permute-start(bf16[128,2048]{1,0:T(8,128)(2,1)S(1)} %get-tuple-element.53), channel_id=1, source_target_pairs={{0,2},{2,4},{4,6},{6,0},{1,3},{3,5},{5,7},{7,1},{8,10},{10,12},{12... | collective-permute-start | bytes 1572872 | tf_op jit(solution)/shard_map/ppermute | solution.py:235
  980.1 11.1 %collective-permute-done.30 = bf16[128,4096]{1,0:T(8,128)(2,1)S(1)} collective-permute-done((bf16[128,4096]{1,0:T(8,128)(2,1)S(1)}, bf16[128,4096]{1,0:T(8,128)(2,1)S(1)}, u32[]{:S(2)}, u32[]{:S(2)}) %collective-permute-start.30) | collective-permute-done | bytes 1048608 | tf_op jit(solution)/shard_map/ppermute | solution.py:235
  991.2 33.7 %collective-permute-done.31 = bf16[128,4096]{1,0:T(8,128)(2,1)S(1)} collective-permute-done((bf16[128,4096]{1,0:T(8,128)(2,1)S(1)}, bf16[128,4096]{1,0:T(8,128)(2,1)S(1)}, u32[]{:S(2)}, u32[]{:S(2)}) %collective-permute-start.31) | collective-permute-done | bytes 1048608 | tf_op jit(solution)/shard_map/ppermute | solution.py:235
  1026.9 20.5 %collective-permute-done.18 = bf16[128,2048]{1,0:T(8,128)(2,1)S(1)} collective-permute-done((bf16[128,2048]{1,0:T(8,128)(2,1)S(1)}, bf16[128,2048]{1,0:T(8,128)(2,1)S(1)}, u32[]{:S(2)}, u32[]{:S(2)}) %collective-permute-start.18) | collective-permute-done | bytes 524320 | tf_op jit(solution)/shard_map/ppermute | solution.py:235
  (254 shorter events, 261.6 us)
Async XLA Ops:
  7.2 105.1 %all-gather.3.cloned.1.call-start = ((), (), s32[]{:S(2)}) async-start(), calls=%async_computation | async-start | bytes 18382848 | tf_op jit(solution)/shard_map/all_gather | solution.py:331
  13.2 366.4 %all-gather.5.cloned.1.call-start = ((), (), s32[]{:S(2)}) async-start(), calls=%async_computation.1 | async-start | bytes 35651584 | tf_op jit(solution)/shard_map/all_gather | solution.py:337
  128.6 71.0 %collective-permute-start = (bf16[512,2048]{1,0:T(8,128)(2,1)S(1)}, bf16[512,2048]{1,0:T(8,128)(2,1)}, u32[]{:S(2)}, u32[]{:S(2)}) collective-permute-start(bf16[512,2048]{1,0:T(8,128)(2,1)S(1)} %slice.93), channel_id=1, source_target_pairs={{0,2},{2,4},{4,6},{1,3},{3,5},{5,7},{8,10},{10,12},{12,14},{9,11},... | collective-permute-start | bytes 6291464 | tf_op jit(solution)/shard_map/ppermute | solution.py:227
  199.6 72.0 %collective-permute-start.1 = (bf16[512,2048]{1,0:T(8,128)(2,1)}, bf16[512,2048]{1,0:T(8,128)(2,1)}, u32[]{:S(2)}, u32[]{:S(2)}) collective-permute-start(bf16[512,2048]{1,0:T(8,128)(2,1)} %collective-permute-done.refs_5_.refs_6_.refs_8_.refs_9_), channel_id=1, source_target_pairs={{0,2},{2,4},{4,6},{1,3},{3,5},{5,7},{8,10},{10,12},{12,14},{9,11},... | collective-permute-start | bytes 6291464 | tf_op jit(solution)/shard_map/ppermute | solution.py:227
  451.8 177.9 %collective-permute-start.33 = (bf16[512,4096]{1,0:T(8,128)(2,1)}, bf16[512,4096]{1,0:T(8,128)(2,1)}, u32[]{:S(2)}, u32[]{:S(2)}) collective-permute-start(bf16[512,4096]{1,0:T(8,128)(2,1)} %convolution_convert_fusion), channel_id=1, source_target_pairs={{0,8},{8,0},{16,24},{24,16},{1,9},{9,1},{17,25},{25,17},{2,10},{10... | collective-permute-start | bytes 12582920 | tf_op jit(solution)/shard_map/ppermute | solution.py:222
  451.8 218.3 %collective-permute-start.27 = (bf16[512,4096]{1,0:T(8,128)(2,1)}, bf16[512,4096]{1,0:T(8,128)(2,1)}, u32[]{:S(2)}, u32[]{:S(2)}) collective-permute-start(bf16[512,4096]{1,0:T(8,128)(2,1)} %convolution_convert_fusion.2), channel_id=1, source_target_pairs={{0,8},{8,0},{16,24},{24,16},{1,9},{9,1},{17,25},{25,17},{2,10},{10... | collective-permute-start | bytes 12582920 | tf_op jit(solution)/shard_map/ppermute | solution.py:222
  531.3 72.6 %collective-permute-start.5 = (bf16[512,2048]{1,0:T(8,128)(2,1)S(1)}, bf16[512,2048]{1,0:T(8,128)(2,1)S(1)}, u32[]{:S(2)}, u32[]{:S(2)}) collective-permute-start(bf16[512,2048]{1,0:T(8,128)(2,1)S(1)} %pad_maximum_fusion.1), channel_id=1, source_target_pairs={{2,0},{4,2},{6,4},{3,1},{5,3},{7,5},{10,8},{12,10},{14,12},{11,9},... | collective-permute-start | bytes 6291464 | tf_op jit(solution)/shard_map/ppermute | solution.py:227
  546.0 62.7 %collective-permute-start.20 = (bf16[512,1024]{1,0:T(8,128)(2,1)S(1)}, bf16[512,1024]{1,0:T(8,128)(2,1)S(1)}, u32[]{:S(2)}, u32[]{:S(2)}) collective-permute-start(bf16[512,1024]{1,0:T(8,128)(2,1)S(1)} %convolution_convert_fusion.7), channel_id=1, source_target_pairs={{0,8},{8,0},{16,24},{24,16},{1,9},{9,1},{17,25},{25,17},{2,10},{10... | collective-permute-start | bytes 3145736 | tf_op jit(solution)/shard_map/ppermute | solution.py:222
  629.8 101.2 %collective-permute-start.32 = (bf16[512,4096]{1,0:T(8,128)(2,1)}, bf16[512,4096]{1,0:T(8,128)(2,1)S(1)}, u32[]{:S(2)}, u32[]{:S(2)}) collective-permute-start(bf16[512,4096]{1,0:T(8,128)(2,1)} %convolution_convert_fusion.1), channel_id=1, source_target_pairs={{0,8},{8,0},{16,24},{24,16},{1,9},{9,1},{17,25},{25,17},{2,10},{10... | collective-permute-start | bytes 12582920 | tf_op jit(solution)/shard_map/ppermute | solution.py:222
  636.9 107.7 %collective-permute-start.34 = (bf16[512,4096]{1,0:T(8,128)(2,1)}, bf16[512,4096]{1,0:T(8,128)(2,1)S(1)}, u32[]{:S(2)}, u32[]{:S(2)}) collective-permute-start(bf16[512,4096]{1,0:T(8,128)(2,1)} %add_convert_fusion.1), channel_id=1, source_target_pairs={{0,16},{8,24},{16,0},{24,8},{1,17},{9,25},{17,1},{25,9},{2,18},{10... | collective-permute-start | bytes 12582920 | tf_op jit(solution)/shard_map/ppermute | solution.py:261
  695.6 62.3 %collective-permute-start.26 = (bf16[512,4096]{1,0:T(8,128)(2,1)}, bf16[512,4096]{1,0:T(8,128)(2,1)}, u32[]{:S(2)}, u32[]{:S(2)}) collective-permute-start(bf16[512,4096]{1,0:T(8,128)(2,1)} %convolution_convert_fusion.3), channel_id=1, source_target_pairs={{0,8},{8,0},{16,24},{24,16},{1,9},{9,1},{17,25},{25,17},{2,10},{10... | collective-permute-start | bytes 12582920 | tf_op jit(solution)/shard_map/ppermute | solution.py:222
  697.0 135.3 %collective-permute-start.28 = (bf16[512,4096]{1,0:T(8,128)(2,1)}, bf16[512,4096]{1,0:T(8,128)(2,1)}, u32[]{:S(2)}, u32[]{:S(2)}) collective-permute-start(bf16[512,4096]{1,0:T(8,128)(2,1)} %add_convert_fusion.3), channel_id=1, source_target_pairs={{0,16},{8,24},{16,0},{24,8},{1,17},{9,25},{17,1},{25,9},{2,18},{10... | collective-permute-start | bytes 12582920 | tf_op jit(solution)/shard_map/ppermute | solution.py:261
  728.4 111.7 %collective-permute-start.15 = (bf16[512,2048]{1,0:T(8,128)(2,1)}, bf16[512,2048]{1,0:T(8,128)(2,1)}, u32[]{:S(2)}, u32[]{:S(2)}) collective-permute-start(bf16[512,2048]{1,0:T(8,128)(2,1)} %convolution_convert_fusion.4), channel_id=1, source_target_pairs={{0,8},{8,0},{16,24},{24,16},{1,9},{9,1},{17,25},{25,17},{2,10},{10... | collective-permute-start | bytes 6291464 | tf_op jit(solution)/shard_map/ppermute | solution.py:222
  731.0 198.6 %collective-permute-start.14 = (bf16[512,2048]{1,0:T(8,128)(2,1)}, bf16[512,2048]{1,0:T(8,128)(2,1)}, u32[]{:S(2)}, u32[]{:S(2)}) collective-permute-start(bf16[512,2048]{1,0:T(8,128)(2,1)} %convolution_convert_fusion.5), channel_id=1, source_target_pairs={{0,8},{8,0},{16,24},{24,16},{1,9},{9,1},{17,25},{25,17},{2,10},{10... | collective-permute-start | bytes 6291464 | tf_op jit(solution)/shard_map/ppermute | solution.py:222
  746.6 97.4 %collective-permute-start.38 = (f32[4,2048]{1,0:T(4,128)S(1)}, f32[4,2048]{1,0:T(4,128)S(1)}, u32[]{:S(2)}, u32[]{:S(2)}) collective-permute-start(f32[4,2048]{1,0:T(4,128)S(1)} %pad_maximum_fusion.2), channel_id=1, source_target_pairs={{0,1},{1,0},{2,3},{3,2},{4,5},{5,4},{6,7},{7,6},{8,9},{9,8},{10,11... | collective-permute-start | bytes 98312 | tf_op jit(solution)/shard_map/ppermute | solution.py:222
  757.9 104.7 %collective-permute-start.35 = (bf16[128,4096]{1,0:T(8,128)(2,1)}, bf16[128,4096]{1,0:T(8,128)(2,1)}, u32[]{:S(2)}, u32[]{:S(2)}) collective-permute-start(bf16[128,4096]{1,0:T(8,128)(2,1)} %get-tuple-element.46), channel_id=1, source_target_pairs={{0,2},{2,4},{4,6},{6,0},{1,3},{3,5},{5,7},{7,1},{8,10},{10,12},{12... | collective-permute-start | bytes 3145736 | tf_op jit(solution)/shard_map/ppermute | solution.py:235
  853.9 70.0 %collective-permute-start.37 = (bf16[128,4096]{1,0:T(8,128)(2,1)S(1)}, bf16[128,4096]{1,0:T(8,128)(2,1)S(1)}, u32[]{:S(2)}, u32[]{:S(2)}) collective-permute-start(bf16[128,4096]{1,0:T(8,128)(2,1)S(1)} %copy-done.29), channel_id=1, source_target_pairs={{0,6},{2,0},{4,2},{6,4},{1,7},{3,1},{5,3},{7,5},{8,14},{10,8},{12,... | collective-permute-start | bytes 3145736 | tf_op jit(solution)/shard_map/ppermute | solution.py:235
  856.3 73.4 %collective-permute-start.16 = (bf16[512,2048]{1,0:T(8,128)(2,1)S(1)}, bf16[512,2048]{1,0:T(8,128)(2,1)S(1)}, u32[]{:S(2)}, u32[]{:S(2)}) collective-permute-start(bf16[512,2048]{1,0:T(8,128)(2,1)S(1)} %add_convert_fusion.5), channel_id=1, source_target_pairs={{0,16},{8,24},{16,0},{24,8},{1,17},{9,25},{17,1},{25,9},{2,18},{10... | collective-permute-start | bytes 6291464 | tf_op jit(solution)/shard_map/ppermute | solution.py:261
  862.6 114.6 %collective-permute-start.29 = (bf16[128,4096]{1,0:T(8,128)(2,1)S(1)}, bf16[128,4096]{1,0:T(8,128)(2,1)S(1)}, u32[]{:S(2)}, u32[]{:S(2)}) collective-permute-start(bf16[128,4096]{1,0:T(8,128)(2,1)S(1)} %get-tuple-element.49), channel_id=1, source_target_pairs={{0,2},{2,4},{4,6},{6,0},{1,3},{3,5},{5,7},{7,1},{8,10},{10,12},{12... | collective-permute-start | bytes 3145736 | tf_op jit(solution)/shard_map/ppermute | solution.py:235
  902.2 89.1 %collective-permute-start.30 = (bf16[128,4096]{1,0:T(8,128)(2,1)S(1)}, bf16[128,4096]{1,0:T(8,128)(2,1)S(1)}, u32[]{:S(2)}, u32[]{:S(2)}) collective-permute-start(bf16[128,4096]{1,0:T(8,128)(2,1)S(1)} %get-tuple-element.51), channel_id=1, source_target_pairs={{0,4},{2,6},{4,0},{6,2},{1,5},{3,7},{5,1},{7,3},{8,12},{10,14},{12... | collective-permute-start | bytes 3145736 | tf_op jit(solution)/shard_map/ppermute | solution.py:235
  923.9 101.0 %collective-permute-start.31 = (bf16[128,4096]{1,0:T(8,128)(2,1)S(1)}, bf16[128,4096]{1,0:T(8,128)(2,1)S(1)}, u32[]{:S(2)}, u32[]{:S(2)}) collective-permute-start(bf16[128,4096]{1,0:T(8,128)(2,1)S(1)} %get-tuple-element.50), channel_id=1, source_target_pairs={{0,6},{2,0},{4,2},{6,4},{1,7},{3,1},{5,3},{7,5},{8,14},{10,8},{12,... | collective-permute-start | bytes 3145736 | tf_op jit(solution)/shard_map/ppermute | solution.py:235
  932.5 94.3 %collective-permute-start.17 = (bf16[128,2048]{1,0:T(8,128)(2,1)S(1)}, bf16[128,2048]{1,0:T(8,128)(2,1)S(1)}, u32[]{:S(2)}, u32[]{:S(2)}) collective-permute-start(bf16[128,2048]{1,0:T(8,128)(2,1)S(1)} %get-tuple-element.53), channel_id=1, source_target_pairs={{0,2},{2,4},{4,6},{6,0},{1,3},{3,5},{5,7},{7,1},{8,10},{10,12},{12... | collective-permute-start | bytes 1572872 | tf_op jit(solution)/shard_map/ppermute | solution.py:235
  975.7 71.7 %collective-permute-start.18 = (bf16[128,2048]{1,0:T(8,128)(2,1)S(1)}, bf16[128,2048]{1,0:T(8,128)(2,1)S(1)}, u32[]{:S(2)}, u32[]{:S(2)}) collective-permute-start(bf16[128,2048]{1,0:T(8,128)(2,1)S(1)} %get-tuple-element.55), channel_id=1, source_target_pairs={{0,4},{2,6},{4,0},{6,2},{1,5},{3,7},{5,1},{7,3},{8,12},{10,14},{12... | collective-permute-start | bytes 1572872 | tf_op jit(solution)/shard_map/ppermute | solution.py:235
  977.2 70.2 %collective-permute-start.19 = (bf16[128,2048]{1,0:T(8,128)(2,1)S(1)}, bf16[128,2048]{1,0:T(8,128)(2,1)S(1)}, u32[]{:S(2)}, u32[]{:S(2)}) collective-permute-start(bf16[128,2048]{1,0:T(8,128)(2,1)S(1)} %get-tuple-element.54), channel_id=1, source_target_pairs={{0,6},{2,0},{4,2},{6,4},{1,7},{3,1},{5,3},{7,5},{8,14},{10,8},{12,... | collective-permute-start | bytes 1572872 | tf_op jit(solution)/shard_map/ppermute | solution.py:235
  (69 other events, 1768.1 us)
Sparse Core Ops, SparseCore 0:
  13.3 98.9 all-gather.2
  114.4 265.1 all-gather.4

commit v2 on v1

--- a/solution.py
+++ b/solution.py
@@ -15,6 +15,8 @@
 half_root = 0.7071067811865476
 bf16 = jnp.bfloat16
 f32 = jnp.float32
+MESH = pl.DeviceIdType.MESH
+WIDTH = 256
 
 
 def contract(left, right, left_dim, right_dim):
@@ -227,77 +229,254 @@
     return lax.ppermute(array, axis, moves)
 
 
-def direct_sum(own, axis, size, me):
-    total = own(me)
-    for step in range(1, size):
-        target = lax.rem(me + step, size)
-        moves = [(i, (i + step) % size) for i in range(size)]
-        total = total + lax.ppermute(own(target).astype(bf16), axis, moves).astype(f32)
-    return total
-
-
-def tensor_sum(part, size):
-    part = part.astype(bf16)
+def tensor_other(part, size):
     if size == 2:
-        return part.astype(f32) + swap(part, "tensor", 2).astype(f32)
-    return lax.psum(part, "tensor").astype(f32)
-
-
-def grad_scatter(part, sizes):
+        return swap(part, "tensor", 2)
+    return lax.psum(part, "tensor") - part
+
+
+def after(value, *others):
+    return lax.optimization_barrier((value,) + others)[0]
+
+
+def reduce_kernel(sizes, width, pairs, left_count, right_count, *refs):
+    lefts, refs = refs[:left_count], refs[left_count:]
+    rights, refs = refs[:right_count], refs[right_count:]
+    outs, refs = refs[: len(pairs)], refs[len(pairs) :]
+    (core_send, core_recv, chip_send, chip_recv, line_send, line_recv, own, keep) = refs[:8]
+    (core_sems, chip_sems, line_sems, core_free, chip_free, line_free) = refs[8:]
     fsdp, context = sizes["fsdp"], sizes["context"]
     chips = fsdp // 2
-    mine = lax.axis_index("fsdp")
+    mine, place = lax.axis_index("fsdp"), lax.axis_index("context")
     core, chip = lax.rem(mine, 2), lax.div(mine, 2)
-    place = lax.axis_index("context")
-
-    def both_cores(target):
-        sent = part(2 * target + 1 - core).astype(bf16)
-        return part(2 * target + core) + swap(sent, "fsdp", fsdp).astype(f32)
-
-    rows = both_cores(chip)
-    for step in range(1, chips):
-        sent = both_cores(lax.rem(chip + step, chips)).astype(bf16)
-        moves = [(i, (i + 2 * step) % fsdp) for i in range(fsdp)]
-        rows = rows + lax.ppermute(sent, "fsdp", moves).astype(f32)
-    rows = rows.astype(bf16)
-    count = rows.shape[0] // context
-    return direct_sum(
-        lambda t: lax.dynamic_slice_in_dim(rows, t * count, count, 0).astype(f32),
-        "context",
-        context,
-        place,
-    )
-
-
-def product_scatter(left, right, sizes):
-    block = left.shape[1] // sizes["fsdp"]
-
-    def part(index):
-        return contract(lax.dynamic_slice_in_dim(left, index * block, block, 1), right, 0, 0)
-
-    return grad_scatter(part, sizes)
-
-
-def vector_scatter(rows, sizes):
+    rows = lefts[0].shape[0] // fsdp
+    piece = rows // context
+    starts, total = [], 0
+    for pair in pairs:
+        starts.append(total)
+        total += pair[3]
+
+    sibling = {"fsdp": mine + 1 - 2 * core}
+    chip_to = [{"fsdp": lax.rem(mine + 2 * k, fsdp)} for k in range(chips)]
+    chip_from = [{"fsdp": lax.rem(mine + fsdp - 2 * k, fsdp)} for k in range(chips)]
+    line_to = [{"context": lax.rem(place + k, context)} for k in range(context)]
+    line_from = [{"context": lax.rem(place + context - k, context)} for k in range(context)]
+
+    barrier = pltpu.get_barrier_semaphore()
+    for peer in [sibling] + chip_to[1:] + line_to[1:]:
+        pl.semaphore_signal(barrier, inc=1, device_id=peer, device_id_type=MESH)
+    pl.semaphore_wait(barrier, 1 + (chips - 1) + (context - 1))
+
+    def remote(source, target, sems, peer):
+        return pltpu.make_async_remote_copy(
+            src_ref=source,
+            dst_ref=target,
+            send_sem=sems[0],
+            recv_sem=sems[1],
+            device_id=peer,
+            device_id_type=MESH,
+        )
+
+    def core_copy(t):
+        slot = lax.rem(t, 2)
+        sems = (core_sems.at[0, slot], core_sems.at[1, slot])
+        return remote(core_send.at[slot], core_recv.at[slot], sems, sibling)
+
+    def chip_copy(t, k):
+        slot = lax.rem(t, 2)
+        sems = (chip_sems.at[0, slot, k - 1], chip_sems.at[1, slot, k - 1])
+        return remote(
+            chip_send.at[slot, k - 1], chip_recv.at[slot, k - 1], sems, chip_to[k]
+        )
+
+    def line_copy(t, k):
+        slot = lax.rem(t, 3)
+        sems = (line_sems.at[0, slot, k - 1], line_sems.at[1, slot, k - 1])
+        target = lax.rem(place + k, context)
+        return remote(line_send.at[slot, target], line_recv.at[slot, k - 1], sems, line_to[k])
+
+    def give(sem, peer):
+        pl.semaphore_signal(sem, inc=1, device_id=peer, device_id_type=MESH)
+
+    def each_pair(t, body):
+        for index, (left, right, first, count) in enumerate(pairs):
+
+            @pl.when((t >= starts[index]) & (t < starts[index] + count))
+            def _(index=index, left=left, right=right, first=first):
+                column = pl.multiple_of((first + t - starts[index]) * width, width)
+
+                def part(block):
+                    start = pl.multiple_of(block * rows, rows)
+                    if left < 0:
+                        return rights[right][pl.ds(start, rows), pl.ds(column, width)]
+                    return jnp.dot(
+                        lefts[left][pl.ds(start, rows), :],
+                        rights[right][:, pl.ds(column, width)],
+                        preferred_element_type=f32,
+                    )
+
+                body(part)
+
+    def first_stage(t):
+        slot = lax.rem(t, 2)
+
+        @pl.when(t >= 2)
+        def _():
+            core_copy(t - 2).wait_send()
+
+        def body(part):
+            for j in range(chips):
+                core_send[slot, j] = part(2 * j + 1 - core).astype(bf16)
+
+        each_pair(t, body)
+
+        @pl.when(t >= 2)
+        def _():
+            pl.semaphore_wait(core_free, 1)
+
+        core_copy(t).start()
+
+    def second_stage(t):
+        slot = lax.rem(t, 2)
+        core_copy(t).wait_recv()
+
+        @pl.when(t >= 2)
+        def _():
+            for k in range(1, chips):
+                chip_copy(t - 2, k).wait_send()
+
+        def body(part):
+            for k in list(range(1, chips)) + [0]:
+                target = lax.rem(chip + k, chips)
+                both = part(2 * target + core) + core_recv[slot, target].astype(f32)
+                if k:
+                    chip_send[slot, k - 1] = both.astype(bf16)
+                else:
+                    own[slot] = both
+
+        each_pair(t, body)
+
+        @pl.when(t <= total - 3)
+        def _():
+            give(core_free, sibling)
+
+        for k in range(1, chips):
+
+            @pl.when(t >= 2)
+            def _(k=k):
+                pl.semaphore_wait(chip_free.at[k - 1], 1)
+
+            chip_copy(t, k).start()
+
+    def third_stage(t):
+        slot, place_slot = lax.rem(t, 2), lax.rem(t, 3)
+        value = own[slot]
+        for k in range(1, chips):
+            chip_copy(t, k).wait_recv()
+            value = value + chip_recv[slot, k - 1].astype(f32)
+
+        @pl.when(t >= 3)
+        def _():
+            for k in range(1, context):
+                line_copy(t - 3, k).wait_send()
+
+        for p in range(context):
+            line_send[place_slot, p] = value[p * piece : (p + 1) * piece].astype(bf16)
+
+            @pl.when(place == p)
+            def _(p=p):
+                keep[place_slot] = value[p * piece : (p + 1) * piece]
+
+        @pl.when(t <= total - 3)
+        def _():
+            for k in range(1, chips):
+                give(chip_free.at[k - 1], chip_from[k])
+
+        for k in range(1, context):
+
+            @pl.when(t >= 3)
+            def _(k=k):
+                pl.semaphore_wait(line_free.at[k - 1], 1)
+
+            line_copy(t, k).start()
+
+    def last_stage(t):
+        slot = lax.rem(t, 3)
+        value = keep[slot]
+        for k in range(1, context):
+            line_copy(t, k).wait_recv()
+            value = value + line_recv[slot, k - 1].astype(f32)
+
+        @pl.when(t <= total - 4)
+        def _():
+            for k in range(1, context):
+                give(line_free.at[k - 1], line_from[k])
+
+        for index, pair in enumerate(pairs):
+
+            @pl.when((t >= starts[index]) & (t < starts[index] + pair[3]))
+            def _(index=index):
+                column = pl.multiple_of((t - starts[index]) * width, width)
+                outs[index][:, pl.ds(column, width)] = value
+
+    def step(s, carry):
+        for lag, stage in ((0, first_stage), (1, second_stage), (2, third_stage), (4, last_stage)):
+
+            @pl.when((s >= lag) & (s < total + lag))
+            def _(lag=lag, stage=stage):
+                stage(s - lag)
+
+        return carry
+
+    lax.fori_loop(0, total + 4, step, 0)
+    for t in range(total - 2, total):
+        core_copy(t).wait_send()
+        for k in range(1, chips):
+            chip_copy(t, k).wait_send()
+    for t in range(total - 3, total):
+        for k in range(1, context):
+            line_copy(t, k).wait_send()
+
+
+def reduce_products(lefts, rights, pairs, sizes, width, number):
     fsdp, context = sizes["fsdp"], sizes["context"]
-    if sizes["tensor"] == 2:
-        rows = rows + swap(rows, "tensor", 2)
-    else:
-        rows = lax.psum(rows, "tensor")
-    count = rows.shape[1] // (fsdp * context)
-    mine, place = lax.axis_index("fsdp"), lax.axis_index("context")
-    width = context * count
-
-    def shift_sum(total, axis, size, me, width):
-        own = lambda t: lax.dynamic_slice_in_dim(total, t * width, width, 1)
-        result = own(me)
-        for step in range(1, size):
-            moves = [(i, (i + step) % size) for i in range(size)]
-            result = result + lax.ppermute(own(lax.rem(me + step, size)), axis, moves)
-        return result
-
-    rows = shift_sum(rows, "fsdp", fsdp, mine, width)
-    return shift_sum(rows, "context", context, place, count)
+    chips = fsdp // 2
+    depth, count = lefts[0].shape
+    rows = depth // fsdp
+    piece = rows // context
+    chunks = tuple((a, b, first // width, n // width) for a, b, first, n in pairs)
+    columns = sum(pair[3] for pair in pairs)
+    vmem = pl.BlockSpec(memory_space=pltpu.VMEM)
+    dma, regular = pltpu.SemaphoreType.DMA, pltpu.SemaphoreType.REGULAR
+    return pl.pallas_call(
+        functools.partial(reduce_kernel, sizes, width, chunks, len(lefts), len(rights)),
+        out_shape=tuple(jax.ShapeDtypeStruct((piece, pair[3]), f32) for pair in pairs),
+        in_specs=[vmem] * (len(lefts) + len(rights)),
+        out_specs=(vmem,) * len(pairs),
+        scratch_shapes=[
+            pltpu.VMEM((2, chips, rows, width), bf16),
+            pltpu.VMEM((2, chips, rows, width), bf16),
+            pltpu.VMEM((2, chips - 1, rows, width), bf16),
+            pltpu.VMEM((2, chips - 1, rows, width), bf16),
+            pltpu.VMEM((3, context, piece, width), bf16),
+            pltpu.VMEM((3, context - 1, piece, width), bf16),
+            pltpu.VMEM((2, rows, width), f32),
+            pltpu.VMEM((3, piece, width), f32),
+            dma((2, 2)),
+            dma((2, 2, chips - 1)),
+            dma((2, 3, context - 1)),
+            regular,
+            regular((chips - 1,)),
+            regular((context - 1,)),
+        ],
+        compiler_params=pltpu.CompilerParams(collective_id=number, has_side_effects=True),
+        cost_estimate=pl.CostEstimate(
+            flops=2 * depth * count * columns * 4,
+            transcendentals=0,
+            bytes_accessed=2 * (depth * len(lefts) + columns) * count + 4 * piece * columns,
+        ),
+        name=f"reduce_products_{number}",
+    )(*lefts, *rights)
 
 
 def per_device(
@@ -366,7 +545,8 @@
     seg_cols = jnp.concatenate(seg_cols, axis=0)[:, :, None]
 
     attn, log_sum = attention_forward(flags, seg_row, seg_cols, qkv, far, heads)
-    residual = rows_in + tensor_sum(contract(attn, full_out, 1, 1), tensor)
+    branch = contract(attn, full_out, 1, 1).astype(bf16)
+    residual = rows_in + (branch.astype(f32) + tensor_other(branch, tensor).astype(f32))
 
     hat_two, inv_two = norm_stats(residual)
     normed_two = (hat_two * gain_two + bias_two).astype(bf16)
@@ -378,23 +558,51 @@
     grad_act = jnp.dot(grad_rows, full_down, preferred_element_type=f32)
     grad_pre = (grad_act * slope).astype(bf16)
     norm_two_part = contract(grad_pre, full_up, 1, 1).astype(bf16)
-    grad_norm_two = tensor_sum(norm_two_part, tensor)
-
-    down_grad = product_scatter(grad_rows, activated, sizes)
-    up_grad = product_scatter(normed_two, grad_pre, sizes)
-    mlp_out = tensor_sum(contract(activated, full_down, 1, 1), tensor)
+    norm_two_other = tensor_other(norm_two_part, tensor)
+    mlp_part = contract(after(activated, norm_two_part), full_down, 1, 1).astype(bf16)
+    mlp_other = tensor_other(mlp_part, tensor)
+
+    (down_grad,) = reduce_products(
+        (grad_rows.T,),
+        (after(activated, mlp_part, norm_two_part),),
+        ((0, 0, 0, hidden_local),),
+        sizes,
+        WIDTH,
+        1,
+    )
+    norm_two_other = after(norm_two_other, down_grad)
+    mlp_other = after(mlp_other, down_grad)
+    mlp_out = mlp_part.astype(f32) + mlp_other.astype(f32)
     output = (residual + mlp_out).astype(bf16).reshape(tokens.shape)
 
+    grad_norm_two = norm_two_part.astype(f32) + norm_two_other.astype(f32)
     grad_resid = grad_rows.astype(f32) + norm_back(grad_norm_two, hat_two, inv_two, gain_two)
     grad_branch = grad_resid.astype(bf16)
     grad_attn = jnp.dot(grad_branch, full_out, preferred_element_type=f32).astype(bf16)
-    out_grad = product_scatter(grad_branch, attn, sizes)
-
     results = attention_backward(
         flags, seg_row, seg_cols, qkv, far, grad_attn, attn, log_sum, heads
     )
     query_bf = results[0]
-    query_grad = product_scatter(normed_one, query_bf, sizes)
+
+    half = hidden_local // 2
+    up_left, out_left = normed_two.T, grad_branch.T
+
+    def first_work(tied):
+        return reduce_products(
+            (up_left,), (after(grad_pre, tied),), ((0, 0, 0, half),), sizes, WIDTH, 2
+        )
+
+    def second_work(tied):
+        return reduce_products(
+            (up_left, out_left),
+            (after(grad_pre, tied), attn),
+            ((0, 0, half, half), (1, 1, 0, local_width)),
+            sizes,
+            WIDTH,
+            3,
+        )
+
+    works, done = [first_work, second_work], []
     carry = None
     for back in range(reach, -1, -1):
         term = jnp.concatenate(results[1 + 2 * back : 3 + 2 * back], axis=1)
@@ -402,18 +610,20 @@
             term = (term.astype(f32) + carry.astype(f32)).astype(bf16)
         if back > 0:
             carry = line_move(term, "context", context, -1)
+            if works:
+                done.append(works.pop(0)(term))
+                carry = after(carry, done[-1][0])
     pair_bf = term
-    pair_grad = product_scatter(normed_one, pair_bf, sizes)
+    for work in works:
+        done.append(work(pair_bf))
+    up_grad = jnp.concatenate([done[0][0], done[1][0]], axis=1)
+    out_grad = done[1][1]
+
     input_part = contract(query_bf, full_qkv[:, :local_width], 1, 1) + contract(
         pair_bf, full_qkv[:, local_width:], 1, 1
     )
     norm_one_part = input_part.astype(bf16)
-    grad_norm_one = tensor_sum(norm_one_part, tensor)
-    tokens_grad = (
-        (grad_resid + norm_back(grad_norm_one, hat_one, inv_one, gain_one))
-        .astype(bf16)
-        .reshape(tokens.shape)
-    )
+    norm_one_other = tensor_other(norm_one_part, tensor)
     one_f, two_f = norm_one_part.astype(f32), norm_two_part.astype(f32)
     vector_sums = jnp.stack(
         [
@@ -424,13 +634,35 @@
         ],
         axis=0,
     )
-    vector_grads = vector_scatter(vector_sums, sizes)
+    vector_sums = jnp.pad(vector_sums, ((0, WIDTH - 4), (0, 0))).T
+    query_grad, key_grad, value_grad, vector_part = reduce_products(
+        (normed_one.T,),
+        (query_bf, pair_bf, vector_sums),
+        (
+            (0, 0, 0, local_width),
+            (0, 1, 0, local_width),
+            (0, 1, local_width, local_width),
+            (-1, 2, 0, WIDTH),
+        ),
+        sizes,
+        WIDTH,
+        4,
+    )
+    norm_one_other = after(norm_one_other, query_grad)
+    grad_norm_one = norm_one_part.astype(f32) + norm_one_other.astype(f32)
+    tokens_grad = (
+        (grad_resid + norm_back(grad_norm_one, hat_one, inv_one, gain_one))
+        .astype(bf16)
+        .reshape(tokens.shape)
+    )
+    vector_part = vector_part[:, :8]
+    vector_grads = (vector_part + tensor_other(vector_part, tensor)).T
     return (
         output,
         tokens_grad,
         query_grad,
-        pair_grad[:, :local_width],
-        pair_grad[:, local_width:],
+        key_grad,
+        value_grad,
         out_grad,
         up_grad,
         down_grad,

time: 1070 us -> 969 us (0.906)
  Pallas kernels: 24.3 us -> 439 us
  waiting for transfers between devices: 669 us -> 299 us
  starting transfers between devices: 98.2 us -> 19.8 us
  matrix products: 167 us -> 101 us
  local copies, waits for them, and re-layouts: 19 us -> 41.2 us
  other arithmetic: 62 us -> 43 us
    pallas_call x0 -> x4, Pallas kernels: none -> 414 us  [reduce_products(): pl.pallas_call(functools.partial(reduce_kernel, sizes, width, chunks, len...]
    ppermute x26 -> x0, waiting for transfers between devices: 257 us -> none  [the longest x15 132 us: direct_sum(): lax.ppermute(own(target).astype(bf16), axis, moves).astype(f32)]
    ppermute x26 -> x0, starting transfers between devices: 75.3 us -> none  [the longest x15 63.7 us: direct_sum(): lax.ppermute(own(target).astype(bf16), axis, moves).astype(f32)]
    dot_general x25 -> x5, matrix products: 118 us -> 48.3 us  [contract(): lax.dot_general(left, right, (((left_dim,), (right_dim,)), ((), ())), pre...]
    ppermute x4, waiting for transfers between devices: 183 us -> 126 us  [line_move(): return lax.ppermute(array, axis, moves)]
    ppermute x15 -> x5, waiting for transfers between devices: 96.5 us -> 40.8 us  [swap(): return lax.ppermute(array, axis, [(i, i ^ 1) for i in range(size)])]
    convert_element_type x6 -> x0, other arithmetic: 27 us -> none  [the longest x3 18.2 us: grad_scatter(): rows = rows.astype(bf16)]
    unnamed x97 -> x77, local copies, waits for them, and re-layouts: 10.4 us -> 30.9 us
  transfers between devices with their start and end apart: 47 -> 11, of which waited for: 25 -> 6; matrix products, arithmetic and copies ran while one was open for 18% -> 5% of each run, Pallas kernels for 2% -> 44%
where the time goes in v2:
time: 969 us; the launch traced here: 959 us
  Pallas kernels  439 us (45%)
  waiting for transfers between devices  299 us (31%)
  matrix products  101 us (10%)
  other arithmetic  43 us (4%)
  local copies, waits for them, and re-layouts  41.2 us (4%)
  starting transfers between devices  19.8 us (2%)
  between operations  16.1 us (2%)
    pallas_call x4, Pallas kernels, reduce_products(): pl.pallas_call(functools.partial(reduce_kernel, sizes, width, chunks, len...  414 us
    ppermute x4, waiting for transfers between devices, line_move(): return lax.ppermute(array, axis, moves)  126 us
    all_gather x1, waiting for transfers between devices, per_device(): lax.all_gather(jnp.concatenate([query_weight, key_weight, value_weight, o...  92.1 us
    dot_general x5, matrix products, contract(): lax.dot_general(left, right, (((left_dim,), (right_dim,)), ((), ())), pre...  48.3 us
    ppermute x5, waiting for transfers between devices, swap(): return lax.ppermute(array, axis, [(i, i ^ 1) for i in range(size)])  40.8 us
    all_gather x1, waiting for transfers between devices, per_device(): lax.all_gather(jnp.concatenate([up_weight, down_weight], axis=1), weight_...  40.4 us
    unnamed x77, local copies, waits for them, and re-layouts  30.9 us
  transfers between devices with their start and end apart: 11, of which 6 were waited for; matrix products, arithmetic and copies ran while one was open for 5% of the time, Pallas kernels for 44%

profile of v2, /device:TPU:0, one launch (start us, length us, event | category | flops | bytes accessed | tf_op | source)
XLA Modules:
  0.0 958.9 jit_solution(13460009138564893560)
XLA Ops:
  20.0 92.1 %all-gather.3.cloned.1.call-done = bf16[2048,4224]{1,0:T(8,128)(2,1)} async-done(((bf16[128,4224]{1,0:T(8,128)(2,1)}), bf16[2048,4224]{1,0:T(8,128)(2,1)}) %all-gather.3.cloned.1.call-update) | async-done | bytes 17301520 | tf_op jit(solution)/shard_map/all_gather | solution.py:510
  115.2 10.2 %fusion.26.refs_2_.refs_3_.refs_4_ = bf16[512,3072]{1,0:T(8,128)(2,1)S(1)} fusion(bf16[2048,4224]{1,0:T(8,128)(2,1)} %all-gather.3.cloned.1.call-done, bf16[1,512,2048]{1,2,0:T(8,128)(2,1)S(1)} %copy.53, f32[2048]{0:T(1024)S(1)} %get-tuple-element.106, f32[2048]{0:T(1024)S(1)} %get-tuple-element.107, f32[512]{0:T(512)S(1)} %add_rsqrt_fusion.1, ...), kind=kOutput, calls=%fused_computation.35 | convolution fusion | flops 6450315264 | bytes 17846272 | tf_op jit(solution)/shard_map/dot_general | solution.py:529
  127.2 4.7 collective-permute-start
  131.9 66.3 %collective-permute-done.refs_5_.refs_6_.refs_8_.refs_9_ = bf16[512,2048]{1,0:T(8,128)(2,1)} collective-permute-done((bf16[512,2048]{1,0:T(8,128)(2,1)S(1)}, bf16[512,2048]{1,0:T(8,128)(2,1)}, u32[]{:S(2)}, u32[]{:S(2)}) %collective-permute-start) | collective-permute-done | bytes 2097184 | tf_op jit(solution)/shard_map/ppermute | solution.py:229
  198.2 6.4 collective-permute-start.1
  210.9 59.4 %collective-permute-done.1.refs_7_.refs_8_.refs_10_.refs_11_ = bf16[512,2048]{1,0:T(8,128)(2,1)} collective-permute-done((bf16[512,2048]{1,0:T(8,128)(2,1)}, bf16[512,2048]{1,0:T(8,128)(2,1)}, u32[]{:S(2)}, u32[]{:S(2)}) %collective-permute-start.1) | collective-permute-done | bytes 2097184 | tf_op jit(solution)/shard_map/ppermute | solution.py:229
  270.2 10.9 %attention_forward.1 = (bf16[512,1024]{1,0:T(8,128)(2,1)}, f32[8,1,512]{2,1,0:T(1,128)}) custom-call(s32[2]{0:T(128)} %add_convert_fusion.5.flags, s32[1,512]{1,0:T(1,128)} %copy-done.27, s32[3,512,1]{2,1,0:T(8,128)} %copy.55.refs_1_, bf16[512,3072]{1,0:T(8,128)(2,1)} %copy-done.4, bf16[512,3072]{1,0:T(8,128)(2,1)} %copy-done.4, ...), custom_call_target="tpu_custom_call" | custom-call | flops 3221225472 | bytes 8388608 | tf_op jit(solution)/shard_map/attention_forward/pallas_call | solution.py:160
  281.1 6.4 fusion.57
  293.3 40.0 %collective-permute-done.2 = bf16[512,2048]{0,1:T(8,128)(2,1)} collective-permute-done((bf16[512,2048]{0,1:T(8,128)(2,1)}, bf16[512,2048]{0,1:T(8,128)(2,1)}, u32[]{:S(2)}, u32[]{:S(2)}) %collective-permute-start.2) | collective-permute-done | bytes 2097184 | tf_op jit(solution)/shard_map/ppermute | solution.py:224
  339.0 40.4 %all-gather.5.cloned.1.call-done = bf16[2048,8192]{1,0:T(8,128)(2,1)} async-done(((bf16[128,8192]{1,0:T(8,128)(2,1)}), bf16[2048,8192]{1,0:T(8,128)(2,1)}) %all-gather.5.cloned.1.call-update) | async-done | bytes 33554448 | tf_op jit(solution)/shard_map/all_gather | solution.py:516
  379.4 17.2 %multiply_convert_fusion = (bf16[512,4096]{1,0:T(8,128)(2,1)S(1)}, f32[512,4096]{1,0:T(8,128)}) fusion(bf16[2048,8192]{1,0:T(8,128)(2,1)} %all-gather.5.cloned.1.call-done, f32[512,2048]{0,1:T(8,128)} %copy-done.2, f32[2048]{0:T(1024)S(1)} %get-tuple-element.105, f32[2048]{0:T(1024)S(1)} %get-tuple-element.104, f32[512]{0:T(512)S(1)} %add_rsqrt_fusion, ...), kind=kOutput, calls=%fused_computation.18 | convolution fusion | flops 8605663232 | bytes 33574912 | tf_op jit(solution)/shard_map/dot_general | solution.py:553
  396.7 18.4 %fusion.14.refs_1_.refs_2_ = bf16[512,4096]{1,0:T(8,128)(2,1)} fusion(f32[512,4096]{1,0:T(8,128)} %get-tuple-element.125, bf16[2048,8192]{1,0:T(8,128)(2,1)} %all-gather.5.cloned.1.call-done, bf16[1,512,2048]{2,1,0:T(8,128)(2,1)S(1)} %copy-done.10), kind=kOutput, calls=%fused_computation.15 | convolution fusion | flops 8610906112 | bytes 31457280 | tf_op jit(solution)/shard_map/dot_general | solution.py:558
  415.0 13.6 %fusion.51 = bf16[512,2048]{0,1:T(8,128)(2,1)S(1)} fusion(bf16[512,4096]{1,0:T(8,128)(2,1)} %fusion.14.refs_1_.refs_2_, bf16[2048,8192]{1,0:T(8,128)(2,1)} %all-gather.5.cloned.1.call-done), kind=kOutput, calls=%fused_computation.65 | convolution fusion | flops 8590983168 | bytes 23068672 | tf_op jit(solution)/shard_map/dot_general | solution.py:23
  428.7 14.3 %fusion.54 = bf16[512,2048]{0,1:T(8,128)(2,1)} fusion(bf16[512,4096]{1,0:T(8,128)(2,1)S(1)} %get-tuple-element.38.refs_1_, bf16[2048,8192]{1,0:T(8,128)(2,1)} %all-gather.5.cloned.1.call-done), kind=kOutput, calls=%fused_computation.66 | convolution fusion | flops 8590983168 | bytes 23068672 | tf_op jit(solution)/shard_map/dot_general | solution.py:23
  445.0 109.4 %reduce_products_1.1 = f32[128,4096]{1,0:T(8,128)} custom-call(bf16[2048,512]{1,0:T(8,128)(2,1)} %bitcast.85, bf16[512,4096]{1,0:T(8,128)(2,1)} %copy-done.30), custom_call_target="tpu_custom_call" | custom-call | flops 34359738368 | bytes 8388608 | tf_op jit(solution)/shard_map/reduce_products_1/pallas_call | solution.py:451
  554.4 5.7 fusion.38
  560.1 5.6 convert_bitcast_fusion.2
  565.7 7.1 fusion.63.refs_5_
  572.8 13.4 %attention_backward.1 = (bf16[512,1024]{1,0:T(8,128)(2,1)}, bf16[512,1024]{1,0:T(8,128)(2,1)}, bf16[512,1024]{1,0:T(8,128)(2,1)}, bf16[512,1024]{1,0:T(8,128)(2,...) custom-call(s32[2]{0:T(128)} %add_convert_fusion.5.flags, ...), custom_call_target="tpu_custom_call" | custom-call | flops 8053063680 | bytes 16777216 | tf_op jit(solution)/shard_map/attention_backward/pallas_call | solution.py:206
  594.4 98.0 %reduce_products_2.1 = f32[128,2048]{1,0:T(8,128)} custom-call(bf16[2048,512]{1,0:T(8,128)(2,1)} %get-tuple-element.116.refs_0_, bf16[512,4096]{1,0:T(8,128)(2,1)} %fusion.14.refs_1_.refs_2_), custom_call_target="tpu_custom_call" | custom-call | flops 17179869184 | bytes 5242880 | tf_op jit(solution)/shard_map/reduce_products_2/pallas_call | solution.py:451
  696.4 118.0 %reduce_products_3.1 = (f32[128,2048]{1,0:T(8,128)}, f32[128,1024]{1,0:T(8,128)}) custom-call(bf16[2048,512]{1,0:T(8,128)(2,1)} %get-tuple-element.116.refs_0_, bf16[2048,512]{1,0:T(8,128)(2,1)} %get-tuple-element.112.refs_1_, bf16[512,4096]{1,0:T(8,128)(2,1)} %fusion.14.refs_1_.refs_2_, bf16[512,1024]{1,0:T(8,128)(2,1)} %get-tuple-element.36.refs_6_.refs_3_), custom_call_target="tpu_custom_call" | custom-call | flops 25769803776 | bytes 8912896 | tf_op jit(solution)/shard_map/reduce_products_3/pallas_call | solution.py:451
  817.2 7.8 fusion.15
  825.0 6.2 add_convert_fusion
  838.8 89.0 %reduce_products_4.1 = (f32[128,1024]{1,0:T(8,128)}, f32[128,1024]{1,0:T(8,128)}, f32[128,1024]{1,0:T(8,128)}, f32[128,256]{1,0:T(8,128)}) custom-call(bf16[2048,512]{1,0:T(8,128)(2,1)} %get-tuple-element.118.refs_0_, bf16[512,1024]{1,0:T(8,128)(2,1)} %get-tuple-element.42.refs_1_, bf16[512,2048]{1,0:T(8,128)(2,1)} %copy-done.9, ...), custom_call_target="tpu_custom_call" | custom-call | flops 27917287424 | bytes 7208960 | tf_op jit(solution)/shard_map/reduce_products_4/pallas_call | solution.py:451
  (131 shorter events, 82.4 us)
Async XLA Ops:
  7.2 104.9 %all-gather.3.cloned.1.call-start = ((), (), s32[]{:S(2)}) async-start(), calls=%async_computation | async-start | bytes 18382848 | tf_op jit(solution)/shard_map/all_gather | solution.py:510
  13.0 366.4 %all-gather.5.cloned.1.call-start = ((), (), s32[]{:S(2)}) async-start(), calls=%async_computation.1 | async-start | bytes 35651584 | tf_op jit(solution)/shard_map/all_gather | solution.py:516
  19.0 314.3 %copy-start = (bf16[1,512,2048]{1,2,0:T(8,128)(2,1)}, bf16[1,512,2048]{1,2,0:T(8,128)(2,1)S(1)}, u32[]{:S(2)}) copy-start(bf16[1,512,2048]{1,2,0:T(8,128)(2,1)S(1)} %copy.53) | copy-start | bytes 6291460
  19.4 106.0 %copy-start.21 = (f32[512]{0:T(512)}, f32[512]{0:T(512)S(1)}, u32[]{:S(2)}) copy-start(f32[512]{0:T(512)S(1)} %broadcast_multiply_fusion.5) | copy-start | bytes 6148
  20.0 105.4 %copy-start.25 = (f32[512]{0:T(512)}, f32[512]{0:T(512)S(1)}, u32[]{:S(2)}) copy-start(f32[512]{0:T(512)S(1)} %add_rsqrt_fusion.1) | copy-start | bytes 6148
  115.2 10.2 %copy-start.18 = (f32[2048]{0:T(1024)}, f32[2048]{0:T(1024)S(1)}, u32[]{:S(2)}) copy-start(f32[2048]{0:T(1024)S(1)} %get-tuple-element.107) | copy-start | bytes 24580
  115.2 10.2 %copy-start.23 = (f32[2048]{0:T(1024)}, f32[2048]{0:T(1024)S(1)}, u32[]{:S(2)}) copy-start(f32[2048]{0:T(1024)S(1)} %get-tuple-element.106) | copy-start | bytes 24580
  127.1 77.6 %copy-start.28 = (s32[1,2048]{1,0:T(1,128)S(1)}, s32[1,2048]{1,0:T(1,128)}, u32[]{:S(2)}) copy-start(s32[1,2048]{1,0:T(1,128)} %param.14) | copy-start | bytes 24580
  127.2 71.0 %collective-permute-start = (bf16[512,2048]{1,0:T(8,128)(2,1)S(1)}, bf16[512,2048]{1,0:T(8,128)(2,1)}, u32[]{:S(2)}, u32[]{:S(2)}) collective-permute-start(bf16[512,2048]{1,0:T(8,128)(2,1)S(1)} %slice.89), channel_id=1, source_target_pairs={{0,2},{2,4},{4,6},{1,3},{3,5},{5,7},{8,10},{10,12},{12,14},{9,11},... | collective-permute-start | bytes 6291464 | tf_op jit(solution)/shard_map/ppermute | solution.py:229
  198.2 72.0 %collective-permute-start.1 = (bf16[512,2048]{1,0:T(8,128)(2,1)}, bf16[512,2048]{1,0:T(8,128)(2,1)}, u32[]{:S(2)}, u32[]{:S(2)}) collective-permute-start(bf16[512,2048]{1,0:T(8,128)(2,1)} %collective-permute-done.refs_5_.refs_6_.refs_8_.refs_9_), channel_id=1, source_target_pairs={{0,2},{2,4},{4,6},{1,3},{3,5},{5,7},{8,10},{10,12},{12,14},{9,11},... | collective-permute-start | bytes 6291464 | tf_op jit(solution)/shard_map/ppermute | solution.py:229
  204.7 65.5 %copy-start.27 = (s32[1,512]{1,0:T(1,128)}, s32[1,512]{1,0:T(1,128)S(1)}, u32[]{:S(2)}) copy-start(s32[1,512]{1,0:T(1,128)S(1)} %get-tuple-element.119.refs_0_) | copy-start | bytes 6148
  287.5 45.8 %collective-permute-start.2 = (bf16[512,2048]{0,1:T(8,128)(2,1)}, bf16[512,2048]{0,1:T(8,128)(2,1)}, u32[]{:S(2)}, u32[]{:S(2)}) collective-permute-start(bf16[512,2048]{0,1:T(8,128)(2,1)} %fusion.57), channel_id=1, source_target_pairs={{0,1},{1,0},{2,3},{3,2},{4,5},{5,4},{6,7},{7,6},{8,9},{9,8},{10,11... | collective-permute-start | bytes 6291464 | tf_op jit(solution)/shard_map/ppermute | solution.py:224
  379.4 17.3 %copy-start.10 = (bf16[1,512,2048]{2,1,0:T(8,128)(2,1)S(1)}, bf16[1,512,2048]{2,1,0:T(8,128)(2,1)}, u32[]{:S(2)}) copy-start(bf16[1,512,2048]{2,1,0:T(8,128)(2,1)} %param.25) | copy-start | bytes 6291460
  396.7 32.0 %copy-start.30 = (bf16[512,4096]{1,0:T(8,128)(2,1)}, bf16[512,4096]{1,0:T(8,128)(2,1)S(1)}, u32[]{:S(2)}) copy-start(bf16[512,4096]{1,0:T(8,128)(2,1)S(1)} %get-tuple-element.38.refs_1_) | copy-start | bytes 12582916
  428.7 125.7 %copy-start.8 = (bf16[512,2048]{0,1:T(8,128)(2,1)}, bf16[512,2048]{0,1:T(8,128)(2,1)S(1)}, u32[]{:S(2)}) copy-start(bf16[512,2048]{0,1:T(8,128)(2,1)S(1)} %fusion.51) | copy-start | bytes 6291460
  443.0 111.4 %collective-permute-start.3 = (bf16[512,2048]{0,1:T(8,128)(2,1)}, bf16[512,2048]{0,1:T(8,128)(2,1)}, u32[]{:S(2)}, u32[]{:S(2)}) collective-permute-start(bf16[512,2048]{0,1:T(8,128)(2,1)} %fusion.54), channel_id=1, source_target_pairs={{0,1},{1,0},{2,3},{3,2},{4,5},{5,4},{6,7},{7,6},{8,9},{9,8},{10,11... | collective-permute-start | bytes 6291464 | tf_op jit(solution)/shard_map/ppermute | solution.py:224
  444.8 109.6 %collective-permute-start.4 = (bf16[512,2048]{0,1:T(8,128)(2,1)S(1)}, bf16[512,2048]{0,1:T(8,128)(2,1)}, u32[]{:S(2)}, u32[]{:S(2)}) collective-permute-start(bf16[512,2048]{0,1:T(8,128)(2,1)S(1)} %fusion.51), channel_id=1, source_target_pairs={{0,1},{1,0},{2,3},{3,2},{4,5},{5,4},{6,7},{7,6},{8,9},{9,8},{10,11... | collective-permute-start | bytes 6291464 | tf_op jit(solution)/shard_map/ppermute | solution.py:224
  590.7 101.7 %collective-permute-start.5 = (bf16[512,2048]{1,0:T(8,128)(2,1)}, bf16[512,2048]{1,0:T(8,128)(2,1)}, u32[]{:S(2)}, u32[]{:S(2)}) collective-permute-start(bf16[512,2048]{1,0:T(8,128)(2,1)} %constant_dynamic-update-slice_fusion.4), channel_id=1, source_target_pairs={{2,0},{4,2},{6,4},{3,1},{5,3},{7,5},{10,8},{12,10},{14,12},{11,9},... | collective-permute-start | bytes 6291464 | tf_op jit(solution)/shard_map/ppermute | solution.py:229
  594.4 98.1 %copy-start.15 = (bf16[512,1024]{1,0:T(8,128)(2,1)S(1)}, bf16[512,1024]{1,0:T(8,128)(2,1)}, u32[]{:S(2)}) copy-start(bf16[512,1024]{1,0:T(8,128)(2,1)} %get-tuple-element.45) | copy-start | bytes 3145732
  695.1 119.4 %collective-permute-start.6 = (bf16[512,2048]{1,0:T(8,128)(2,1)S(1)}, bf16[512,2048]{1,0:T(8,128)(2,1)}, u32[]{:S(2)}, u32[]{:S(2)}) collective-permute-start(bf16[512,2048]{1,0:T(8,128)(2,1)S(1)} %add_convert_fusion.2), channel_id=1, source_target_pairs={{2,0},{4,2},{6,4},{3,1},{5,3},{7,5},{10,8},{12,10},{14,12},{11,9},... | collective-permute-start | bytes 6291464 | tf_op jit(solution)/shard_map/ppermute | solution.py:229
  696.4 118.1 %copy-start.14 = (bf16[512,1024]{1,0:T(8,128)(2,1)S(1)}, bf16[512,1024]{1,0:T(8,128)(2,1)}, u32[]{:S(2)}) copy-start(bf16[512,1024]{1,0:T(8,128)(2,1)} %get-tuple-element.43) | copy-start | bytes 3145732
  835.4 98.3 %collective-permute-start.7 = (bf16[512,2048]{0,1:T(8,128)(2,1)}, bf16[512,2048]{0,1:T(8,128)(2,1)}, u32[]{:S(2)}, u32[]{:S(2)}) collective-permute-start(bf16[512,2048]{0,1:T(8,128)(2,1)} %add_convert_fusion), channel_id=1, source_target_pairs={{0,1},{1,0},{2,3},{3,2},{4,5},{5,4},{6,7},{7,6},{8,9},{9,8},{10,11... | collective-permute-start | bytes 6291464 | tf_op jit(solution)/shard_map/ppermute | solution.py:224
  838.8 90.6 %copy-start.13 = (f32[128,2048]{1,0:T(8,128)S(1)}, f32[128,2048]{1,0:T(8,128)}, u32[]{:S(2)}) copy-start(f32[128,2048]{1,0:T(8,128)} %reduce_products_2.1) | copy-start | bytes 3145732
  928.7 4.3 collective-permute-start.8
  (18 other events, 105.9 us)
Sparse Core Ops, SparseCore 0:
  13.1 98.9 all-gather.2
  114.2 265.1 all-gather.4

commit v3 on v2

v3 whole, which is shorter than its diff:
```python
import functools

import jax
import jax.numpy as jnp
from jax import lax
from jax.experimental import pallas as pl
from jax.experimental.pallas import tpu as pltpu
from jax.sharding import PartitionSpec as P

HEAD = 128

epsilon = 1e-05
big_negative = -1e30
density = 0.3989422804014327
half_root = 0.7071067811865476
bf16 = jnp.bfloat16
f32 = jnp.float32
MESH = pl.DeviceIdType.MESH
WIDTH = 256


def contract(left, right, left_dim, right_dim):
    return lax.dot_general(
        left, right, (((left_dim,), (right_dim,)), ((), ())), preferred_element_type=f32
    )


def norm_stats(row_vals):
    average = jnp.mean(row_vals, axis=-1, keepdims=True)
    centered = row_vals - average
    variance = jnp.mean(centered * centered, axis=-1, keepdims=True)
    inv_std = lax.rsqrt(variance + epsilon)
    return (centered * inv_std, inv_std)


def norm_back(grad_out, normed_hat, inv_std, gain_vals):
    scaled = grad_out * gain_vals
    first_mean = jnp.mean(scaled, axis=-1, keepdims=True)
    second_mean = jnp.mean(scaled * normed_hat, axis=-1, keepdims=True)
    return inv_std * (scaled - first_mean - normed_hat * second_mean)


def attn_forward_kernel(reach, factor, flags, *refs):
    seg_row, seg_cols, query, own_key, own_value = refs[:5]
    far = refs[5 : 5 + 2 * reach]
    out, log_sum, run_max, run_sum, run_acc = refs[5 + 2 * reach :]
    rows = query.shape[0]

    def block(key_ref, value_ref, index, first):
        scores = contract(key_ref[...], query[...], 1, 1) * factor
        allowed = seg_cols[index] == seg_row[...]
        if first:
            key_pos = lax.broadcasted_iota(jnp.int32, (rows, rows), 0)
            query_pos = lax.broadcasted_iota(jnp.int32, (rows, rows), 1)
            allowed = allowed & (key_pos <= query_pos)
        scores = jnp.where(allowed, scores, big_negative)
        peak = jnp.max(scores, axis=0, keepdims=True)
        if not first:
            peak = jnp.maximum(peak, run_max[...])
        terms = jnp.where(allowed, jnp.exp(scores - peak), 0.0)
        total = jnp.sum(terms, axis=0, keepdims=True)
        value_sum = contract(value_ref[...], terms.astype(bf16), 0, 0)
        if first:
            run_sum[...] = total
            run_acc[...] = value_sum
        else:
            shrink = jnp.exp(run_max[...] - peak)
            run_sum[...] = run_sum[...] * shrink + total
            run_acc[...] = run_acc[...] * shrink + value_sum
        run_max[...] = peak

    block(own_key, own_value, 0, True)
    for step in range(reach):

        @pl.when(flags[step] > 0)
        def _(step=step):
            block(far[2 * step], far[2 * step + 1], step + 1, False)

    out[...] = (run_acc[...] / run_sum[...]).T.astype(bf16)
    log_sum[0] = run_max[...] + jnp.log(run_sum[...])


def attn_backward_kernel(reach, factor, flags, *refs):
    seg_row, seg_cols, query, own_key, own_value, grad_out, attn_out, log_sum = refs[:8]
    far = refs[8 : 8 + 2 * reach]
    outs = refs[8 + 2 * reach :]
    grad_query, own_pair_grad = outs[:2]
    far_grads = outs[2 : 2 + reach]
    acc = outs[2 + reach]
    rows = query.shape[0]
    delta = jnp.sum(
        (grad_out[...].astype(f32) * attn_out[...].astype(f32)).T, axis=0, keepdims=True
    )

    def block(key_ref, value_ref, pair_grad, index, first):
        scores = contract(key_ref[...], query[...], 1, 1) * factor
        allowed = seg_cols[index] == seg_row[...]
        if first:
            key_pos = lax.broadcasted_iota(jnp.int32, (rows, rows), 0)
            query_pos = lax.broadcasted_iota(jnp.int32, (rows, rows), 1)
            allowed = allowed & (key_pos <= query_pos)
        probs = jnp.where(
            allowed, jnp.exp(jnp.where(allowed, scores, big_negative) - log_sum[0]), 0.0
        )
        grad_probs = contract(value_ref[...], grad_out[...], 1, 1)
        grad_scores = (probs * (grad_probs - delta)).astype(bf16)
        pair_grad[:, :HEAD] = (
            jnp.dot(grad_scores, query[...], preferred_element_type=f32) * factor
        ).astype(bf16)
        pair_grad[:, HEAD:] = jnp.dot(
            probs.astype(bf16), grad_out[...], preferred_element_type=f32
        ).astype(bf16)
        update = contract(key_ref[...], grad_scores, 0, 0)
        if first:
            acc[...] = update
        else:
            acc[...] += update

    block(own_key, own_value, own_pair_grad, 0, True)
    for step in range(reach):

        @pl.when(flags[step] > 0)
        def _(step=step):
            block(far[2 * step], far[2 * step + 1], far_grads[step], step + 1, False)

        @pl.when(flags[step] == 0)
        def _(step=step):
            far_grads[step][...] = jnp.zeros_like(far_grads[step])

    grad_query[...] = (acc[...] * factor).T.astype(bf16)


def head_spec(rows, first, stride=1):
    return pl.BlockSpec((rows, HEAD), lambda h, flags: (0, first + stride * h))


def attention_forward(flags, seg_row, seg_cols, qkv, far, heads):
    rows = qkv.shape[0]
    reach = len(far)
    in_specs = [
        pl.BlockSpec((1, rows), lambda h, flags: (0, 0)),
        pl.BlockSpec(seg_cols.shape, lambda h, flags: (0, 0, 0)),
        head_spec(rows, 0),
        head_spec(rows, heads, 2),
        head_spec(rows, heads + 1, 2),
    ]
    operands = [seg_row, seg_cols, qkv, qkv, qkv]
    for piece in far:
        in_specs += [head_spec(rows, 0, 2), head_spec(rows, 1, 2)]
        operands += [piece, piece]
    pairs = heads * rows * rows * (reach + 1)
    return pl.pallas_call(
        functools.partial(attn_forward_kernel, reach, HEAD ** (-0.5)),
        out_shape=(
            jax.ShapeDtypeStruct((rows, heads * HEAD), bf16),
            jax.ShapeDtypeStruct((heads, 1, rows), f32),
        ),
        grid_spec=pltpu.PrefetchScalarGridSpec(
            num_scalar_prefetch=1,
            grid=(heads,),
            in_specs=in_specs,
            out_specs=(
                head_spec(rows, 0),
                pl.BlockSpec((1, 1, rows), lambda h, flags: (h, 0, 0)),
            ),
            scratch_shapes=[
                pltpu.VMEM((1, rows), f32),
                pltpu.VMEM((1, rows), f32),
                pltpu.VMEM((HEAD, rows), f32),
            ],
        ),
        cost_estimate=pl.CostEstimate(
            flops=4 * HEAD * pairs, transcendentals=pairs, bytes_accessed=16 * rows * heads * HEAD
        ),
        name="attention_forward",
    )(flags, *operands)


def attention_backward(flags, seg_row, seg_cols, qkv, far, grad_out, attn_out, log_sum, heads):
    rows = qkv.shape[0]
    reach = len(far)
    in_specs = [
        pl.BlockSpec((1, rows), lambda h, flags: (0, 0)),
        pl.BlockSpec(seg_cols.shape, lambda h, flags: (0, 0, 0)),
        head_spec(rows, 0),
        head_spec(rows, heads, 2),
        head_spec(rows, heads + 1, 2),
        head_spec(rows, 0),
        head_spec(rows, 0),
        pl.BlockSpec((1, 1, rows), lambda h, flags: (h, 0, 0)),
    ]
    operands = [seg_row, seg_cols, qkv, qkv, qkv, grad_out, attn_out, log_sum]
    for piece in far:
        in_specs += [head_spec(rows, 0, 2), head_spec(rows, 1, 2)]
        operands += [piece, piece]
    pairs = heads * rows * rows * (reach + 1)
    pair_spec = pl.BlockSpec((rows, 2 * HEAD), lambda h, flags: (0, h))
    pair_out = jax.ShapeDtypeStruct((rows, 2 * heads * HEAD), bf16)
    return pl.pallas_call(
        functools.partial(attn_backward_kernel, reach, HEAD ** (-0.5)),
        out_shape=(jax.ShapeDtypeStruct((rows, heads * HEAD), bf16),) + (pair_out,) * (1 + reach),
        grid_spec=pltpu.PrefetchScalarGridSpec(
            num_scalar_prefetch=1,
            grid=(heads,),
            in_specs=in_specs,
            out_specs=(head_spec(rows, 0),) + (pair_spec,) * (1 + reach),
            scratch_shapes=[pltpu.VMEM((HEAD, rows), f32)],
        ),
        cost_estimate=pl.CostEstimate(
            flops=10 * HEAD * pairs, transcendentals=pairs, bytes_accessed=32 * rows * heads * HEAD
        ),
        name="attention_backward",
    )(flags, *operands)


def swap(array, axis, size):
    return lax.ppermute(array, axis, [(i, i ^ 1) for i in range(size)])


def line_move(array, axis, size, step):
    moves = [(i, i + step) for i in range(size) if 0 <= i + step < size]
    return lax.ppermute(array, axis, moves)


def tensor_other(part, size):
    if size == 2:
        return swap(part, "tensor", 2)
    return lax.psum(part, "tensor") - part


def after(value, *others):
    return lax.optimization_barrier((value,) + others)[0]


def remote(source, target, sems, peer):
    return pltpu.make_async_remote_copy(
        src_ref=source,
        dst_ref=target,
        send_sem=sems[0],
        recv_sem=sems[1],
        device_id=peer,
        device_id_type=MESH,
    )


def give(sem, peer):
    pl.semaphore_signal(sem, inc=1, device_id=peer, device_id_type=MESH)


def reduce_loop(sizes, width, depth, pairs, outs, scratch, others=(), extra=None):
    fsdp, context = sizes["fsdp"], sizes["context"]
    levels = context.bit_length() - 1
    (core_send, core_recv, chip_send, chip_recv, own) = scratch[:5]
    (core_sems, chip_sems, line_sems, core_free, chip_free, line_free) = scratch[5:11]
    line_send = scratch[11 : 11 + levels]
    line_recv = scratch[11 + levels : 11 + 2 * levels]
    line_keep = scratch[11 + 2 * levels : 11 + 3 * levels]
    chips = fsdp // 2
    mine, place = lax.axis_index("fsdp"), lax.axis_index("context")
    core, chip = lax.rem(mine, 2), lax.div(mine, 2)
    rows = depth // fsdp
    piece = rows // context
    starts, total = [], 0
    for pair in pairs:
        starts.append(total)
        total += pair[1]

    sibling = {"fsdp": mine + 1 - 2 * core}
    chip_to = [{"fsdp": lax.rem(mine + 2 * k, fsdp)} for k in range(chips)]
    chip_from = [{"fsdp": lax.rem(mine + fsdp - 2 * k, fsdp)} for k in range(chips)]
    bits = [lax.rem(lax.div(place, 1 << level), 2) for level in range(levels)]
    partners = [
        {"context": place + (1 - 2 * bits[level]) * (1 << level)} for level in range(levels)
    ]

    barrier = pltpu.get_barrier_semaphore()
    peers = [sibling] + chip_to[1:] + partners + list(others)
    for peer in peers:
        pl.semaphore_signal(barrier, inc=1, device_id=peer, device_id_type=MESH)
    pl.semaphore_wait(barrier, len(peers))

    def core_copy(t):
        slot = lax.rem(t, 2)
        sems = (core_sems.at[0, slot], core_sems.at[1, slot])
        return remote(core_send.at[slot], core_recv.at[slot], sems, sibling)

    def chip_copy(t, k):
        slot = lax.rem(t, 2)
        sems = (chip_sems.at[0, slot, k - 1], chip_sems.at[1, slot, k - 1])
        return remote(chip_send.at[slot, k - 1], chip_recv.at[slot, k - 1], sems, chip_to[k])

    def line_copy(t, level):
        slot = lax.rem(t, 3)
        sems = (line_sems.at[0, slot, level], line_sems.at[1, slot, level])
        source = line_send[level].at[slot, 1 - bits[level]]
        return remote(source, line_recv[level].at[slot], sems, partners[level])

    def line_out(t, level, value):
        slot = lax.rem(t, 3)

        @pl.when(t >= 3)
        def _():
            line_copy(t - 3, level).wait_send()

        for i in range(context >> level):
            line_send[level][slot, i % 2, i // 2] = value(i).astype(bf16)

            @pl.when(bits[level] == i % 2)
            def _(i=i):
                line_keep[level][slot, i // 2] = value(i)

        @pl.when(t >= 3)
        def _():
            pl.semaphore_wait(line_free.at[level], 1)

        line_copy(t, level).start()

    def each_pair(t, body):
        for start, (part, count, _) in zip(starts, pairs):

            @pl.when((t >= start) & (t < start + count))
            def _(start=start, part=part):
                body(lambda block: part(t - start, pl.multiple_of(block * rows, rows), rows))

    def first_stage(t):
        slot = lax.rem(t, 2)

        @pl.when(t >= 2)
        def _():
            core_copy(t - 2).wait_send()

        def body(part):
            for j in range(chips):
                core_send[slot, j] = part(2 * j + 1 - core).astype(bf16)

        each_pair(t, body)

        @pl.when(t >= 2)
        def _():
            pl.semaphore_wait(core_free, 1)

        core_copy(t).start()

    def second_stage(t):
        slot = lax.rem(t, 2)
        core_copy(t).wait_recv()

        @pl.when(t >= 2)
        def _():
            for k in range(1, chips):
                chip_copy(t - 2, k).wait_send()

        def body(part):
            for k in list(range(1, chips)) + [0]:
                target = lax.rem(chip + k, chips)
                both = part(2 * target + core) + core_recv[slot, target].astype(f32)
                if k:
                    chip_send[slot, k - 1] = both.astype(bf16)
                else:
                    own[slot] = both

        each_pair(t, body)

        @pl.when(t <= total - 3)
        def _():
            give(core_free, sibling)

        for k in range(1, chips):

            @pl.when(t >= 2)
            def _(k=k):
                pl.semaphore_wait(chip_free.at[k - 1], 1)

            chip_copy(t, k).start()

    def third_stage(t):
        slot = lax.rem(t, 2)
        value = own[slot]
        for k in range(1, chips):
            chip_copy(t, k).wait_recv()
            value = value + chip_recv[slot, k - 1].astype(f32)
        line_out(t, 0, lambda i: value[i * piece : (i + 1) * piece])

        @pl.when(t <= total - 3)
        def _():
            for k in range(1, chips):
                give(chip_free.at[k - 1], chip_from[k])

    def line_stage(t, level):
        slot = lax.rem(t, 3)
        line_copy(t, level).wait_recv()

        def value(i):
            return line_keep[level][slot, i] + line_recv[level][slot, i].astype(f32)

        if level + 1 < levels:
            line_out(t, level + 1, value)
        else:
            result = value(0)
            for start, (_, count, numbers) in zip(starts, pairs):

                @pl.when((t >= start) & (t < start + count))
                def _(start=start, numbers=numbers):
                    span = width // len(numbers)
                    column = pl.multiple_of((t - start) * span, span)
                    for index, number in enumerate(numbers):
                        outs[number][:, pl.ds(column, span)] = result[
                            :, index * span : (index + 1) * span
                        ]

        @pl.when(t <= total - 4)
        def _():
            give(line_free.at[level], partners[level])

    stages = [(0, first_stage), (1, second_stage), (2, third_stage)] + [
        (4 + 2 * level, functools.partial(line_stage, level=level)) for level in range(levels)
    ]

    def step(s, carry):
        for lag, stage in stages:

            @pl.when((s >= lag) & (s < total + lag))
            def _(lag=lag, stage=stage):
                stage(s - lag)

        if extra is not None:
            extra(s)
        return carry

    lax.fori_loop(0, total + 2 + 2 * levels, step, 0)
    for t in range(total - 2, total):
        core_copy(t).wait_send()
        for k in range(1, chips):
            chip_copy(t, k).wait_send()
    for t in range(total - 3, total):
        for level in range(levels):
            line_copy(t, level).wait_send()


def reduce_scratch(sizes, width, depth):
    fsdp, context = sizes["fsdp"], sizes["context"]
    chips = fsdp // 2
    rows = depth // fsdp
    piece = rows // context
    levels = context.bit_length() - 1
    assert context == 1 << levels
    dma, regular = pltpu.SemaphoreType.DMA, pltpu.SemaphoreType.REGULAR
    halves = [context >> (level + 1) for level in range(levels)]
    return (
        [
            pltpu.VMEM((2, chips, rows, width), bf16),
            pltpu.VMEM((2, chips, rows, width), bf16),
            pltpu.VMEM((2, chips - 1, rows, width), bf16),
            pltpu.VMEM((2, chips - 1, rows, width), bf16),
            pltpu.VMEM((2, rows, width), f32),
            dma((2, 2)),
            dma((2, 2, chips - 1)),
            dma((2, 3, levels)),
            regular,
            regular((chips - 1,)),
            regular((levels,)),
        ]
        + [pltpu.VMEM((3, 2, n, piece, width), bf16) for n in halves]
        + [pltpu.VMEM((3, n, piece, width), bf16) for n in halves]
        + [pltpu.VMEM((3, n, piece, width), f32) for n in halves]
    )


def product_part(left, right, first, width):
    def part(chunk, row, rows):
        column = pl.multiple_of((first + chunk) * width, width)
        return jnp.dot(
            left[pl.ds(row, rows), :], right[:, pl.ds(column, width)], preferred_element_type=f32
        )

    return part


def column_sums(first, second, row, width):
    first = jnp.sum(first, axis=0, keepdims=True)
    second = jnp.sum(second, axis=0, keepdims=True)
    line = lax.broadcasted_iota(jnp.int32, (128, width), 0)
    return jnp.where(line == row, first, jnp.where(line == row + 1, second, 0.0)).T


def middle_kernel(sizes, width, *refs):
    row_left, act, grad_pre, resid, rows, average, inverse, gain, weights, attn_full = refs[:10]
    down_grad, output, grad_resid, out_left, vec_two, grad_attn = refs[10:16]
    held, held_out, part_send, part_recv, means, acc = refs[16:22]
    held_sems, out_sem, part_sems = refs[22:25]
    scratch = refs[25:]
    depth, count = row_left.shape
    hidden = act.shape[1]
    local_width = grad_attn.shape[1]
    blocks = depth // width
    other = {"tensor": 1 - lax.axis_index("tensor")}
    pairs = [(product_part(row_left, act, 0, width), hidden // width, (0,))]
    total = hidden // width

    def held_copy(b):
        row = pl.multiple_of(lax.rem(b, blocks) * width, width)
        column = pl.multiple_of(lax.div(b, blocks) * hidden, hidden)
        slot = lax.rem(b, 2)
        return pltpu.make_async_copy(
            weights.at[pl.ds(row, width), pl.ds(column, hidden)], held.at[slot], held_sems.at[slot]
        )

    def out_copy():
        source = attn_full.at[:, pl.ds(3 * local_width, local_width)]
        return pltpu.make_async_copy(source, held_out, out_sem)

    def part_copy(b):
        sems = (part_sems.at[0, b], part_sems.at[1, b])
        return remote(part_send.at[b], part_recv.at[b], sems, other)

    def at(b):
        return pl.ds(pl.multiple_of(b * width, width), width)

    def normed_hat(b):
        return (resid[:, at(b)] - average[...]) * inverse[...]

    def send_block(b, left):
        held_copy(b).wait()
        rounded = contract(left[...], held[lax.rem(b, 2)], 1, 1).astype(bf16)
        part_send[b] = rounded
        part_copy(b).start()

        @pl.when(b + 2 < 2 * blocks)
        def _():
            held_copy(b + 2).start()

        return rounded.astype(f32)

    def norm_block(b):
        rounded = send_block(b, grad_pre)
        vec_two[at(b), :] = column_sums(rounded * normed_hat(b), rounded, 2, width)

    def both(b):
        return part_send[b].astype(f32) + part_recv[b].astype(f32)

    def norm_means():
        def add(b, sums):
            part_copy(b).wait_recv()
            scaled = both(b) * gain[:, at(b)]
            first = jnp.sum(scaled, axis=1, keepdims=True)
            second = jnp.sum(scaled * normed_hat(b), axis=1, keepdims=True)
            return (sums[0] + first, sums[1] + second)

        zero = jnp.zeros((count, 1), f32)
        first, second = lax.fori_loop(0, blocks, add, (zero, zero))
        means[0] = first * (1.0 / depth)
        means[1] = second * (1.0 / depth)

    def norm_result(b):
        back = both(b) * gain[:, at(b)] - means[0] - normed_hat(b) * means[1]
        result = rows[:, at(b)].astype(f32) + inverse[...] * back
        grad_resid[:, at(b)] = result
        out_left[at(b), :] = result.T.astype(bf16)
        update = jnp.dot(result.astype(bf16), held_out[at(b), :], preferred_element_type=f32)

        @pl.when(b == 0)
        def _():
            acc[...] = update

        @pl.when(b > 0)
        def _():
            acc[...] += update

        @pl.when(b == blocks - 1)
        def _():
            grad_attn[...] = acc[...].astype(bf16)

    def output_block(b):
        part_copy(blocks + b).wait_recv()
        output[:, at(b)] = (resid[:, at(b)] + both(blocks + b)).astype(bf16)

    def during(s, first, body):
        @pl.when((s >= first) & (s < first + blocks))
        def _():
            body(s - first)

    def extra(s):
        @pl.when(s == 0)
        def _():
            held_copy(0).start()
            held_copy(1).start()
            out_copy().start()

        during(s, 1, norm_block)
        during(s, 1 + blocks, lambda b: send_block(blocks + b, act))

        @pl.when(s == blocks + 3)
        def _():
            norm_means()
            out_copy().wait()

        during(s, blocks + 4, norm_result)
        during(s, blocks + 5, output_block)

    assert 2 * blocks <= total
    reduce_loop(sizes, width, depth, pairs, [down_grad], scratch, (other,), extra)
    for b in range(2 * blocks):
        part_copy(b).wait_send()


def backward_middle(left, act, grad_pre, resid, rows, norm, weights, attn_full, sizes, width, number):
    depth, count = left.shape
    hidden = act.shape[1]
    local_width = attn_full.shape[1] // HEAD // 4 * HEAD
    piece = depth // (sizes["fsdp"] * sizes["context"])
    blocks = depth // width
    vmem = pl.BlockSpec(memory_space=pltpu.VMEM)
    far = pl.BlockSpec(memory_space=pl.ANY)
    dma = pltpu.SemaphoreType.DMA
    return pl.pallas_call(
        functools.partial(middle_kernel, sizes, width),
        out_shape=(
            jax.ShapeDtypeStruct((piece, hidden), f32),
            jax.ShapeDtypeStruct((count, depth), bf16),
            jax.ShapeDtypeStruct((count, depth), f32),
            jax.ShapeDtypeStruct((depth, count), bf16),
            jax.ShapeDtypeStruct((depth, 128), f32),
            jax.ShapeDtypeStruct((count, local_width), bf16),
        ),
        in_specs=[vmem] * 8 + [far] * 2,
        out_specs=(vmem,) * 6,
        scratch_shapes=[
            pltpu.VMEM((2, width, hidden), bf16),
            pltpu.VMEM((depth, local_width), bf16),
            pltpu.VMEM((2 * blocks, count, width), bf16),
            pltpu.VMEM((2 * blocks, count, width), bf16),
            pltpu.VMEM((2, count, 1), f32),
            pltpu.VMEM((count, local_width), f32),
            dma((2,)),
            dma,
            dma((2, 2 * blocks)),
        ]
        + reduce_scratch(sizes, width, depth),
        compiler_params=pltpu.CompilerParams(
            collective_id=number, has_side_effects=True, vmem_limit_bytes=62 * 1024 * 1024
        ),
        cost_estimate=pl.CostEstimate(
            flops=12 * depth * count * hidden,
            transcendentals=0,
            bytes_accessed=4 * depth * hidden,
        ),
        name="backward_middle",
    )(left, act, grad_pre, resid, rows, *norm, weights, attn_full)


def tail_kernel(sizes, width, reach, *refs):
    up_left, out_left, one_left, grad_pre, attn, query, weights = refs[:7]
    tokens, average, inverse, gain, grad_resid, vec_two = refs[7:13]
    terms = refs[13 : 14 + reach]
    refs = refs[14 + reach :]
    outs, tokens_grad = refs[:6], refs[6]
    pair, hop_recv, carry, held, part_send, part_recv, vec_one, means = refs[7:15]
    hop_sems, hop_free, held_sems, part_sems = refs[15:19]
    scratch = refs[19:]
    context = sizes["context"]
    place = lax.axis_index("context")
    depth, count = up_left.shape
    local_width = query.shape[1]
    blocks = depth // width
    lower = {"context": lax.rem(place + context - 1, context)}
    upper = {"context": lax.rem(place + 1, context)}
    other = {"tensor": 1 - lax.axis_index("tensor")}

    def vec_part(chunk, row, rows):
        both = vec_one[pl.ds(row, rows), :] + vec_two[pl.ds(row, rows), :]
        return jnp.concatenate([both] * (width // both.shape[1]), axis=1)

    pairs = [
        (product_part(up_left, grad_pre, 0, width), grad_pre.shape[1] // width, (0,)),
        (product_part(out_left, attn, 0, width), local_width // width, (1,)),
        (product_part(one_left, query, 0, width), local_width // width, (2,)),
        (product_part(one_left, pair, 0, width), 2 * local_width // width, (3, 4)),
        (vec_part, 1, (5,)),
    ]
    total = sum(p[1] for p in pairs)
    begin = sum(p[1] for p in pairs[:3])
    hop_steps = [h * (begin - 2) // max(reach, 1) for h in range(reach + 1)]

    def hop_copy(h):
        source = terms[reach] if h == 0 else carry.at[h % carry.shape[0]]
        sems = (hop_sems.at[0, h], hop_sems.at[1, h])
        return remote(source, hop_recv.at[h % 2], sems, lower)

    def hop(h):
        term = terms[reach - h]
        target = pair if h == reach else carry.at[h % carry.shape[0]]
        if h > carry.shape[0] and h < reach:

            @pl.when(place > 0)
            def _():
                hop_copy(h - carry.shape[0]).wait_send()

        if h > 0:

            @pl.when(place < context - 1)
            def _():
                hop_copy(h - 1).wait_recv()

                def add(i, c):
                    at = pl.ds(pl.multiple_of(i * 64, 64), 64)
                    got = hop_recv[(h - 1) % 2, at, :].astype(f32)
                    target[at, :] = (term[at, :].astype(f32) + got).astype(bf16)
                    return c

                lax.fori_loop(0, count // 64, add, 0)
                if h + 1 < reach:
                    give(hop_free, upper)

            @pl.when(place == context - 1)
            def _():
                target[...] = term[...]

        elif reach == 0:
            pair[...] = term[...]
        if h < reach:

            @pl.when(place > 0)
            def _():
                if h >= 2:
                    pl.semaphore_wait(hop_free, 1)
                hop_copy(h).start()

    def held_copy(b):
        slot = lax.rem(b, 2)
        row = pl.multiple_of(b * width, width)
        return pltpu.make_async_copy(
            weights.at[pl.ds(row, width), pl.ds(0, 3 * local_width)],
            held.at[slot],
            held_sems.at[slot],
        )

    def part_copy(b):
        sems = (part_sems.at[0, b], part_sems.at[1, b])
        return remote(part_send.at[b], part_recv.at[b], sems, other)

    def normed_hat(b):
        columns = pl.ds(pl.multiple_of(b * width, width), width)
        return (tokens[:, columns].astype(f32) - average[...]) * inverse[...]

    def input_block(b):
        slot = lax.rem(b, 2)
        held_copy(b).wait()
        value = contract(query[...], held[slot, :, :local_width], 1, 1)
        value = value + contract(pair[...], held[slot, :, local_width:], 1, 1)
        rounded = value.astype(bf16)
        part_send[b] = rounded
        part_copy(b).start()

        @pl.when(b + 2 < blocks)
        def _():
            held_copy(b + 2).start()

        rounded = rounded.astype(f32)
        vec_one[pl.ds(pl.multiple_of(b * width, width), width), :] = column_sums(
            rounded * normed_hat(b), rounded, 0, width
        )

    def scaled_block(b):
        columns = pl.ds(pl.multiple_of(b * width, width), width)
        value = part_send[b].astype(f32) + part_recv[b].astype(f32)
        return value * gain[:, columns]

    def norm_means():
        def add(b, sums):
            part_copy(b).wait_recv()
            scaled = scaled_block(b)
            first = jnp.sum(scaled, axis=1, keepdims=True)
            second = jnp.sum(scaled * normed_hat(b), axis=1, keepdims=True)
            return (sums[0] + first, sums[1] + second)

        zero = jnp.zeros((count, 1), f32)
        first, second = lax.fori_loop(0, blocks, add, (zero, zero))
        means[0] = first * (1.0 / depth)
        means[1] = second * (1.0 / depth)

    def norm_result():
        def write(b, c):
            columns = pl.ds(pl.multiple_of(b * width, width), width)
            back = scaled_block(b) - means[0] - normed_hat(b) * means[1]
            tokens_grad[:, columns] = (
                grad_resid[:, columns] + inverse[...] * back
            ).astype(bf16)
            return c

        lax.fori_loop(0, blocks, write, 0)

    def extra(s):
        for h in range(reach + 1):

            @pl.when(s == hop_steps[h])
            def _(h=h):
                hop(h)

        @pl.when(s == begin - 2)
        def _():
            held_copy(0).start()
            held_copy(1).start()

        @pl.when((s >= begin) & (s < begin + blocks))
        def _():
            input_block(s - begin)

        @pl.when(s == total + 1)
        def _():
            norm_means()

        @pl.when(s == total + 2)
        def _():
            norm_result()

    assert begin + blocks < total
    reduce_loop(sizes, width, depth, pairs, outs, scratch, (other, lower, upper), extra)

    @pl.when(place > 0)
    def _():
        for h in range(reach):
            if h == 0 or h >= reach - carry.shape[0]:
                hop_copy(h).wait_send()

    for b in range(blocks):
        part_copy(b).wait_send()


def backward_tail(
    lefts, grad_pre, attn, query, weights, norm, grad_resid, vec_two, terms, sizes, width, number
):
    depth, count = lefts[0].shape
    local_width = query.shape[1]
    hidden = grad_pre.shape[1]
    reach = len(terms) - 1
    piece = depth // (sizes["fsdp"] * sizes["context"])
    blocks = depth // width
    vmem = pl.BlockSpec(memory_space=pltpu.VMEM)
    dma = pltpu.SemaphoreType.DMA
    columns = (hidden, local_width, local_width, local_width, local_width, width)
    operands = [*lefts, grad_pre, attn, query, weights, *norm, grad_resid, vec_two, *terms]
    in_specs = [vmem] * len(operands)
    in_specs[6] = pl.BlockSpec(memory_space=pl.ANY)
    slots = max(1, min(2, reach - 1))
    hops = max(reach, 1)
    return pl.pallas_call(
        functools.partial(tail_kernel, sizes, width, reach),
        out_shape=tuple(jax.ShapeDtypeStruct((piece, n), f32) for n in columns)
        + (jax.ShapeDtypeStruct((count, depth), bf16),),
        in_specs=in_specs,
        out_specs=(vmem,) * 7,
        scratch_shapes=[
            pltpu.VMEM((count, 2 * local_width), bf16),
            pltpu.VMEM((min(2, hops), count, 2 * local_width), bf16),
            pltpu.VMEM((slots, count, 2 * local_width), bf16),
            pltpu.VMEM((2, width, 3 * local_width), bf16),
            pltpu.VMEM((blocks, count, width), bf16),
            pltpu.VMEM((blocks, count, width), bf16),
            pltpu.VMEM((depth, 128), f32),
            pltpu.VMEM((2, count, 1), f32),
            dma((2, hops)),
            pltpu.SemaphoreType.REGULAR,
            dma((2,)),
            dma((2, blocks)),
        ]
        + reduce_scratch(sizes, width, depth),
        compiler_params=pltpu.CompilerParams(
            collective_id=number, has_side_effects=True, vmem_limit_bytes=62 * 1024 * 1024
        ),
        cost_estimate=pl.CostEstimate(
            flops=8 * depth * count * (hidden + 4 * local_width),
            transcendentals=0,
            bytes_accessed=16 * depth * count,
        ),
        name="backward_tail",
    )(*operands)


def per_device(
    sizes,
    tokens,
    segments,
    query_weight,
    key_weight,
    value_weight,
    out_weight,
    up_weight,
    down_weight,
    attn_gain,
    attn_bias,
    mlp_gain,
    mlp_bias,
    cotangent,
):
    seq_dev, group_len, model_width = tokens.shape
    assert seq_dev == 1
    shard_rows, local_width = query_weight.shape
    hidden_local = up_weight.shape[1]
    heads = local_width // HEAD
    seq_len = segments.shape[1]
    context, tensor = sizes["context"], sizes["tensor"]
    place = lax.axis_index("context")
    weight_axes = ("fsdp", "context")

    vectors = jnp.stack([attn_gain, attn_bias, mlp_gain, mlp_bias], axis=1)
    vectors = jnp.pad(vectors, ((0, 0), (0, HEAD - 4)))
    pair_weight = jnp.stack(
        [w.reshape(shard_rows, heads, HEAD) for w in (key_weight, value_weight)], axis=2
    ).reshape(shard_rows, 2 * local_width)
    attn_full = lax.all_gather(
        jnp.concatenate([query_weight, pair_weight, out_weight, vectors], axis=1),
        weight_axes,
        axis=0,
        tiled=True,
    )
    mlp_full = lax.all_gather(
        jnp.concatenate([up_weight, down_weight], axis=1), weight_axes, axis=0, tiled=True
    )
    full_qkv = attn_full[:, : 3 * local_width]
    full_out = attn_full[:, 3 * local_width : 4 * local_width]
    vecs = attn_full[:, 4 * local_width : 4 * local_width + 4].T.astype(f32)
    gain_one, bias_one, gain_two, bias_two = vecs[0], vecs[1], vecs[2], vecs[3]
    full_up = mlp_full[:, :hidden_local]
    full_down = mlp_full[:, hidden_local:]

    rows_in = tokens.reshape(group_len, model_width).astype(f32)
    hat_one, inv_one = norm_stats(rows_in)
    mean_one = jnp.mean(rows_in, axis=-1, keepdims=True)
    normed_one = (hat_one * gain_one + bias_one).astype(bf16)
    qkv = jnp.dot(normed_one, full_qkv, preferred_element_type=f32).astype(bf16)

    reach = min(context - 1, -(-(seq_len // 2 - 1) // group_len))
    far = []
    piece = qkv[:, local_width:]
    for _ in range(reach):
        piece = line_move(piece, "context", context, 1)
        far.append(piece)
    first = place * group_len
    seg_row = lax.dynamic_slice_in_dim(segments, first, group_len, 1)
    seg_cols = [seg_row]
    for back in range(1, reach + 1):
        start = jnp.maximum(first - back * group_len, 0)
        block = lax.dynamic_slice_in_dim(segments, start, group_len, 1)
        seg_cols.append(jnp.where(place >= back, block, -1))
    flags = jnp.stack([(cols[0, -1] == seg_row[0, 0]).astype(jnp.int32) for cols in seg_cols[1:]])
    seg_cols = jnp.concatenate(seg_cols, axis=0)[:, :, None]

    attn, log_sum = attention_forward(flags, seg_row, seg_cols, qkv, far, heads)
    branch = contract(attn, full_out, 1, 1).astype(bf16)
    residual = rows_in + (branch.astype(f32) + tensor_other(branch, tensor).astype(f32))

    hat_two, inv_two = norm_stats(residual)
    normed_two = (hat_two * gain_two + bias_two).astype(bf16)
    row_left, up_left, one_left = lax.optimization_barrier(
        (cotangent.reshape(group_len, model_width).T, normed_two.T, normed_one.T)
    )
    pre_act = jnp.dot(
        after(normed_two, row_left, up_left, one_left), full_up, preferred_element_type=f32
    )
    normal_cdf = 0.5 * (1.0 + lax.erf(pre_act * half_root))
    activated = (pre_act * normal_cdf).astype(bf16)
    slope = normal_cdf + pre_act * density * jnp.exp(-0.5 * pre_act * pre_act)
    grad_rows = cotangent.reshape(group_len, model_width)
    grad_act = jnp.dot(grad_rows, full_down, preferred_element_type=f32)
    grad_pre = (grad_act * slope).astype(bf16)
    mean_two = jnp.mean(residual, axis=-1, keepdims=True)
    down_grad, output, grad_resid, out_left, vec_two, grad_attn = backward_middle(
        row_left,
        activated,
        grad_pre,
        residual,
        grad_rows,
        (mean_two, inv_two, gain_two[None]),
        mlp_full,
        attn_full,
        sizes,
        WIDTH,
        1,
    )
    output = output.reshape(tokens.shape)
    results = attention_backward(
        flags, seg_row, seg_cols, qkv, far, grad_attn, attn, log_sum, heads
    )
    up_grad, out_grad, query_grad, key_grad, value_grad, vector_part, tokens_grad = backward_tail(
        (up_left, out_left, one_left),
        grad_pre,
        attn,
        results[0],
        attn_full,
        (tokens.reshape(group_len, model_width), mean_one, inv_one, gain_one[None]),
        grad_resid,
        vec_two,
        results[1:],
        sizes,
        WIDTH,
        2,
    )
    tokens_grad = tokens_grad.reshape(tokens.shape)
    vector_part = vector_part[:, :8]
    vector_grads = (vector_part + tensor_other(vector_part, tensor)).T
    return (
        output,
        tokens_grad,
        query_grad,
        key_grad,
        value_grad,
        out_grad,
        up_grad,
        down_grad,
        vector_grads[0],
        vector_grads[1],
        vector_grads[2],
        vector_grads[3],
    )


def solution(mesh):
    weight = P(("fsdp", "context"), "tensor")
    vector = P(("fsdp", "context"))
    rows = P("fsdp", "context", None)
    return jax.shard_map(
        functools.partial(per_device, dict(mesh.shape)),
        mesh=mesh,
        in_specs=(rows, P("fsdp", None)) + (weight,) * 6 + (vector,) * 4 + (rows,),
        out_specs=(rows, rows) + (weight,) * 6 + (vector,) * 4,
        check_vma=False,
    )
```

time: 969 us -> 864 us (0.89)
  matrix products: 101 us -> 50 us
  waiting for transfers between devices: 299 us -> 269 us
  other arithmetic: 43 us -> 23.7 us
  local copies, waits for them, and re-layouts: 41.2 us -> 57.2 us
    dot_general x5 -> x1, matrix products: 48.3 us -> 6.22 us  [contract(): lax.dot_general(left, right, (((left_dim,), (right_dim,)), ((), ())), pre...]
    all_gather x0 -> x1, local copies, waits for them, and re-layouts: none -> 21.9 us  [per_device(): lax.all_gather(jnp.concatenate([query_weight, pair_weight, out_weight, ve...]
    all_gather x1, waiting for transfers between devices: 40.4 us -> 20.3 us  [per_device(): lax.all_gather(jnp.concatenate([up_weight, down_weight], axis=1), weight_...]
    unnamed x77 -> x46, local copies, waits for them, and re-layouts: 30.9 us -> 14.7 us
    ppermute x5 -> x2, waiting for transfers between devices: 40.8 us -> 25.1 us  [swap(): return lax.ppermute(array, axis, [(i, i ^ 1) for i in range(size)])]
    reduce_sum x3 -> x0, other arithmetic: 12.8 us -> none  [the longest x1 5.68 us: per_device(): jnp.sum(two_f * hat_two, axis=0)]
    optimization_barrier x0 -> x3, local copies, waits for them, and re-layouts: none -> 10.6 us  [per_device(): lax.optimization_barrier((cotangent.reshape(group_len, model_width).T, no...]
    dot_general x2 -> x1, matrix products: 24.3 us -> 16.3 us  [per_device(): jnp.dot(after(normed_two, row_left, up_left, one_left), full_up, preferre...]
  transfers between devices with their start and end apart: 11 -> 6, of which waited for: 6 -> 6; matrix products, arithmetic and copies ran while one was open for 5% -> 9% of each run, Pallas kernels for 44% -> 1%
where the time goes in v3:
time: 864 us; the launch traced here: 863 us
  Pallas kernels  434 us (50%)
  waiting for transfers between devices  269 us (31%)
  local copies, waits for them, and re-layouts  57.2 us (7%)
  matrix products  50 us (6%)
  other arithmetic  23.7 us (3%)
  between operations  15.5 us (2%)
  starting transfers between devices  13.5 us (2%)
    pallas_call x1, Pallas kernels, backward_tail(): pl.pallas_call(functools.partial(tail_kernel, sizes, width, reach), out_s...  287 us
    ppermute x2, waiting for transfers between devices, line_move(): return lax.ppermute(array, axis, moves)  128 us
    pallas_call x1, Pallas kernels, backward_middle(): pl.pallas_call(functools.partial(middle_kernel, sizes, width), out_shape=...  122 us
    all_gather x1, waiting for transfers between devices, per_device(): lax.all_gather(jnp.concatenate([query_weight, pair_weight, out_weight, ve...  95.7 us
    ppermute x2, waiting for transfers between devices, swap(): return lax.ppermute(array, axis, [(i, i ^ 1) for i in range(size)])  25.1 us
    all_gather x1, local copies, waits for them, and re-layouts, per_device(): lax.all_gather(jnp.concatenate([query_weight, pair_weight, out_weight, ve...  21.9 us
    all_gather x1, waiting for transfers between devices, per_device(): lax.all_gather(jnp.concatenate([up_weight, down_weight], axis=1), weight_...  20.3 us
  transfers between devices with their start and end apart: 6, of which 6 were waited for; matrix products, arithmetic and copies ran while one was open for 9% of the time, Pallas kernels for 1%

profile of v3, /device:TPU:0, one launch (start us, length us, event | category | flops | bytes accessed | tf_op | source)
XLA Modules:
  0.0 862.8 jit_solution(5118676897844040204)
XLA Ops:
  13.7 2.8 pad_maximum_fusion
  17.7 95.7 %all-gather.3.cloned.1.call-done = bf16[2048,4224]{0,1:T(8,128)(2,1)} async-done(((bf16[128,4224]{0,1:T(8,128)(2,1)}), bf16[2048,4224]{0,1:T(8,128)(2,1)}) %all-gather.3.cloned.1.call-update) | async-done | bytes 17301520 | tf_op jit(solution)/shard_map/all_gather | solution.py:910
  114.2 10.4 %fusion.15.refs_2_.refs_3_.refs_4_ = bf16[512,3072]{1,0:T(8,128)(2,1)S(1)} fusion(bf16[2048,4224]{0,1:T(8,128)(2,1)} %all-gather.3.cloned.1.call-done, f32[2048]{0:T(1024)S(1)} %bitcast.63, f32[2048]{0:T(1024)S(1)} %bitcast.61, f32[512]{0:T(512)S(1)} %add_rsqrt_fusion.1, f32[512]{0:T(512)S(1)} %broadcast_multiply_fusion.1, bf16[1,512,2048]{2,1,0:T(8,128)(2,1)} %param.13), kind=kOutput, calls=%fused_computation.19 | convolution fusion | flops 6450315264 | bytes 17846272 | tf_op jit(solution)/shard_map/dot_general | solution.py:930
  124.8 4.8 collective-permute-start
  129.6 67.1 %collective-permute-done.refs_5_.refs_6_.refs_8_.refs_9_ = bf16[512,2048]{1,0:T(8,128)(2,1)} collective-permute-done((bf16[512,2048]{1,0:T(8,128)(2,1)S(1)}, bf16[512,2048]{1,0:T(8,128)(2,1)}, u32[]{:S(2)}, u32[]{:S(2)}) %collective-permute-start) | collective-permute-done | bytes 2097184 | tf_op jit(solution)/shard_map/ppermute | solution.py:222
  196.7 5.8 collective-permute-start.1
  208.7 60.9 %collective-permute-done.1.refs_7_.refs_8_.refs_10_.refs_11_ = bf16[512,2048]{1,0:T(8,128)(2,1)} collective-permute-done((bf16[512,2048]{1,0:T(8,128)(2,1)}, bf16[512,2048]{1,0:T(8,128)(2,1)}, u32[]{:S(2)}, u32[]{:S(2)}) %collective-permute-start.1) | collective-permute-done | bytes 2097184 | tf_op jit(solution)/shard_map/ppermute | solution.py:222
  269.6 10.8 %attention_forward.1 = (bf16[512,1024]{1,0:T(8,128)(2,1)}, f32[8,1,512]{2,1,0:T(1,128)}) custom-call(s32[2]{0:T(128)} %add_convert_fusion.1.flags, s32[1,512]{1,0:T(1,128)} %copy-done.16, s32[3,512,1]{2,1,0:T(8,128)} %copy.39.refs_1_, bf16[512,3072]{1,0:T(8,128)(2,1)} %copy-done.1, bf16[512,3072]{1,0:T(8,128)(2,1)} %copy-done.1, ...), custom_call_target="tpu_custom_call" | custom-call | flops 3221225472 | bytes 8388608 | tf_op jit(solution)/shard_map/attention_forward/pallas_call | solution.py:152
  280.4 6.2 fusion.24
  290.0 21.9 %copy.44.refs_9_.refs_6_ = bf16[2048,4224]{1,0:T(8,128)(2,1)} copy(bf16[2048,4224]{0,1:T(8,128)(2,1)} %all-gather.3.cloned.1.call-done) | data formatting | bytes 34603008 | tf_op jit(solution)/shard_map/all_gather | solution.py:910
  311.9 22.0 %collective-permute-done.2 = bf16[512,2048]{1,0:T(8,128)(2,1)} collective-permute-done((bf16[512,2048]{1,0:T(8,128)(2,1)}, bf16[512,2048]{1,0:T(8,128)(2,1)}, u32[]{:S(2)}, u32[]{:S(2)}) %collective-permute-start.2) | collective-permute-done | bytes 2097184 | tf_op jit(solution)/shard_map/ppermute | solution.py:217
  333.9 4.6 fusion.37
  342.7 4.3 fusion.42
  347.0 4.1 copy.41.refs_0_
  351.2 4.0 copy.46.refs_0_
  357.6 4.4 add_convert_fusion
  362.0 20.3 %all-gather.5.cloned.1.call-done.refs_8_ = bf16[2048,8192]{1,0:T(8,128)(2,1)} async-done(((bf16[128,8192]{1,0:T(8,128)(2,1)}), bf16[2048,8192]{1,0:T(8,128)(2,1)}) %all-gather.5.cloned.1.call-update) | async-done | bytes 33554448 | tf_op jit(solution)/shard_map/all_gather | solution.py:916
  382.3 16.3 %multiply_convert_fusion = (bf16[512,4096]{1,0:T(8,128)(2,1)}, f32[512,4096]{1,0:T(8,128)}) fusion(bf16[512,2048]{1,0:T(8,128)(2,1)} %add_convert_fusion, bf16[2048,8192]{1,0:T(8,128)(2,1)} %all-gather.5.cloned.1.call-done.refs_8_), kind=kOutput, calls=%fused_computation.12 | convolution fusion | flops 8600420352 | bytes 31457280 | tf_op jit(solution)/shard_map/dot_general | solution.py:957
  398.7 17.1 %fusion.10.refs_2_.refs_3_ = bf16[512,4096]{1,0:T(8,128)(2,1)} fusion(f32[512,4096]{1,0:T(8,128)} %get-tuple-element.75, bf16[2048,8192]{1,0:T(8,128)(2,1)} %all-gather.5.cloned.1.call-done.refs_8_, bf16[1,512,2048]{2,1,0:T(8,128)(2,1)S(1)} %copy-done.5), kind=kOutput, calls=%fused_computation.11 | convolution fusion | flops 8610906112 | bytes 31457280 | tf_op jit(solution)/shard_map/dot_general | solution.py:964
  415.7 122.4 %backward_middle.1 = (f32[128,4096]{1,0:T(8,128)}, bf16[512,2048]{1,0:T(8,128)(2,1)}, f32[512,2048]{1,0:T(8,128)}, bf16[2048,512]{1,0:T(8,128)(2,1)}, f32[2048,128]{1,0:T(8,128)}, /*index=5*/bf16[512,1024]{1,0:T(8,128)(2,1)}) custom-call(bf16[2048,512]{1,0:T(8,128)(2,1)} %copy.41.refs_0_, bf16[512,4096]{1,0:T(8,128)(2,1)} %get-tuple-element.74.refs_1_, ...), custom_call_target="tpu_custom_call" | custom-call | flops 51539607552 | bytes 33554432 | tf_op jit(solution)/shard_map/backward_middle/pallas_call | solution.py:615
  538.2 13.2 %attention_backward.1 = (bf16[512,1024]{1,0:T(8,128)(2,1)}, bf16[512,2048]{1,0:T(8,128)(2,1)}, bf16[512,2048]{1,0:T(8,128)(2,1)}, bf16[512,2048]{1,0:T(8,128)(2,1)}) custom-call(s32[2]{0:T(128)} %add_convert_fusion.1.flags, s32[1,512]{1,0:T(1,128)} %copy-done.16, s32[3,512,1]{2,1,0:T(8,128)} %copy.39.refs_1_, bf16[512,3072]{1,0:T(8,128)(2,1)} %copy-done.1, ...), custom_call_target="tpu_custom_call" | custom-call | flops 8053063680 | bytes 16777216 | tf_op jit(solution)/shard_map/attention_backward/pallas_call | solution.py:199
  551.4 287.2 %backward_tail.1 = (f32[128,4096]{1,0:T(8,128)}, f32[128,1024]{1,0:T(8,128)}, f32[128,1024]{1,0:T(8,128)}, f32[128,1024]{1,0:T(8,128)}, f32[128,1024]{1,0:T(8,12...) custom-call(bf16[2048,512]{1,0:T(8,128)(2,1)} %copy.46.refs_0_, bf16[2048,512]{1,0:T(8,128)(2,1)} %get-tuple-element.41.refs_1_, ...), custom_call_target="tpu_custom_call" | custom-call | flops 68719476736 | bytes 16777216 | tf_op jit(solution)/shard_map/backward_tail/pallas_call | solution.py:846
  840.8 3.1 collective-permute-done.3
  845.5 3.2 copy.62
  (81 shorter events, 34.4 us)
Async XLA Ops:
  7.2 6.6 copy-start.9
  7.2 106.2 %all-gather.3.cloned.1.call-start = ((), (), s32[]{:S(2)}) async-start(), calls=%async_computation | async-start | bytes 18382848 | tf_op jit(solution)/shard_map/all_gather | solution.py:910
  13.7 3.0 copy-start.2
  13.7 368.7 %all-gather.5.cloned.1.call-start = ((), (), s32[]{:S(2)}) async-start(), calls=%async_computation.1 | async-start | bytes 35651584 | tf_op jit(solution)/shard_map/all_gather | solution.py:916
  114.2 219.7 %copy-start.15 = (f32[1,2048]{1,0:T(1,128)}, f32[1,2048]{1,0:T(1,128)S(1)}, u32[]{:S(2)}) copy-start(f32[1,2048]{1,0:T(1,128)S(1)} %get-tuple-element.68.refs_10_) | copy-start | bytes 24580
  114.2 243.4 %copy-start.14 = (f32[1,2048]{1,0:T(1,128)}, f32[1,2048]{1,0:T(1,128)S(1)}, u32[]{:S(2)}) copy-start(f32[1,2048]{1,0:T(1,128)S(1)} %get-tuple-element.65.refs_7_) | copy-start | bytes 24580
  124.6 145.0 %copy-start.1 = (bf16[512,3072]{1,0:T(8,128)(2,1)}, bf16[512,3072]{1,0:T(8,128)(2,1)S(1)}, u32[]{:S(2)}) copy-start(bf16[512,3072]{1,0:T(8,128)(2,1)S(1)} %fusion.15.refs_2_.refs_3_.refs_4_) | copy-start | bytes 9437188
  124.6 77.9 %copy-start.17 = (s32[1,2048]{1,0:T(1,128)S(1)}, s32[1,2048]{1,0:T(1,128)}, u32[]{:S(2)}) copy-start(s32[1,2048]{1,0:T(1,128)} %param.14) | copy-start | bytes 24580
  124.8 71.9 %collective-permute-start = (bf16[512,2048]{1,0:T(8,128)(2,1)S(1)}, bf16[512,2048]{1,0:T(8,128)(2,1)}, u32[]{:S(2)}, u32[]{:S(2)}) collective-permute-start(bf16[512,2048]{1,0:T(8,128)(2,1)S(1)} %slice.79), channel_id=1, source_target_pairs={{0,2},{2,4},{4,6},{1,3},{3,5},{5,7},{8,10},{10,12},{12,14},{9,11},... | collective-permute-start | bytes 6291464 | tf_op jit(solution)/shard_map/ppermute | solution.py:222
  196.7 72.9 %collective-permute-start.1 = (bf16[512,2048]{1,0:T(8,128)(2,1)}, bf16[512,2048]{1,0:T(8,128)(2,1)}, u32[]{:S(2)}, u32[]{:S(2)}) collective-permute-start(bf16[512,2048]{1,0:T(8,128)(2,1)} %collective-permute-done.refs_5_.refs_6_.refs_8_.refs_9_), channel_id=1, source_target_pairs={{0,2},{2,4},{4,6},{1,3},{3,5},{5,7},{8,10},{10,12},{12,14},{9,11},... | collective-permute-start | bytes 6291464 | tf_op jit(solution)/shard_map/ppermute | solution.py:222
  202.6 67.0 %copy-start.16 = (s32[1,512]{1,0:T(1,128)}, s32[1,512]{1,0:T(1,128)S(1)}, u32[]{:S(2)}) copy-start(s32[1,512]{1,0:T(1,128)S(1)} %get-tuple-element.69.refs_0_) | copy-start | bytes 6148
  286.7 47.2 %collective-permute-start.2 = (bf16[512,2048]{1,0:T(8,128)(2,1)}, bf16[512,2048]{1,0:T(8,128)(2,1)}, u32[]{:S(2)}, u32[]{:S(2)}) collective-permute-start(bf16[512,2048]{1,0:T(8,128)(2,1)} %fusion.24), channel_id=1, source_target_pairs={{0,1},{1,0},{2,3},{3,2},{4,5},{5,4},{6,7},{7,6},{8,9},{9,8},{10,11... | collective-permute-start | bytes 6291464 | tf_op jit(solution)/shard_map/ppermute | solution.py:217
  290.0 43.9 %copy-start.3 = (bf16[1,512,2048]{2,1,0:T(8,128)(2,1)S(1)}, bf16[1,512,2048]{2,1,0:T(8,128)(2,1)}, u32[]{:S(2)}) copy-start(bf16[1,512,2048]{2,1,0:T(8,128)(2,1)} %param.13) | copy-start | bytes 6291460
  338.4 2.0 copy-start
  347.0 8.1 copy-start.4
  362.0 36.6 %copy-start.5 = (bf16[1,512,2048]{2,1,0:T(8,128)(2,1)S(1)}, bf16[1,512,2048]{2,1,0:T(8,128)(2,1)}, u32[]{:S(2)}) copy-start(bf16[1,512,2048]{2,1,0:T(8,128)(2,1)} %param.25) | copy-start | bytes 6291460
  838.6 10.1 %copy-start.8 = (bf16[512,2048]{1,0:T(8,128)(2,1)S(1)}, bf16[512,2048]{1,0:T(8,128)(2,1)}, u32[]{:S(2)}) copy-start(bf16[512,2048]{1,0:T(8,128)(2,1)} %get-tuple-element.50) | copy-start | bytes 6291460
  839.6 4.3 collective-permute-start.3
  845.5 4.6 copy-start.13
  845.5 5.4 copy-start.12
  848.8 2.9 copy-start.11
  848.8 3.7 copy-start.10
  848.8 4.5 copy-start.7
  850.1 4.5 copy-start.6
Sparse Core Ops, SparseCore 0:
  13.8 99.5 all-gather.2
  115.5 266.7 all-gather.4

commit v4 on v3

--- a/solution.py
+++ b/solution.py
@@ -78,56 +78,6 @@
 
     out[...] = (run_acc[...] / run_sum[...]).T.astype(bf16)
     log_sum[0] = run_max[...] + jnp.log(run_sum[...])
-
-
-def attn_backward_kernel(reach, factor, flags, *refs):
-    seg_row, seg_cols, query, own_key, own_value, grad_out, attn_out, log_sum = refs[:8]
-    far = refs[8 : 8 + 2 * reach]
-    outs = refs[8 + 2 * reach :]
-    grad_query, own_pair_grad = outs[:2]
-    far_grads = outs[2 : 2 + reach]
-    acc = outs[2 + reach]
-    rows = query.shape[0]
-    delta = jnp.sum(
-        (grad_out[...].astype(f32) * attn_out[...].astype(f32)).T, axis=0, keepdims=True
-    )
-
-    def block(key_ref, value_ref, pair_grad, index, first):
-        scores = contract(key_ref[...], query[...], 1, 1) * factor
-        allowed = seg_cols[index] == seg_row[...]
-        if first:
-            key_pos = lax.broadcasted_iota(jnp.int32, (rows, rows), 0)
-            query_pos = lax.broadcasted_iota(jnp.int32, (rows, rows), 1)
-            allowed = allowed & (key_pos <= query_pos)
-        probs = jnp.where(
-            allowed, jnp.exp(jnp.where(allowed, scores, big_negative) - log_sum[0]), 0.0
-        )
-        grad_probs = contract(value_ref[...], grad_out[...], 1, 1)
-        grad_scores = (probs * (grad_probs - delta)).astype(bf16)
-        pair_grad[:, :HEAD] = (
-            jnp.dot(grad_scores, query[...], preferred_element_type=f32) * factor
-        ).astype(bf16)
-        pair_grad[:, HEAD:] = jnp.dot(
-            probs.astype(bf16), grad_out[...], preferred_element_type=f32
-        ).astype(bf16)
-        update = contract(key_ref[...], grad_scores, 0, 0)
-        if first:
-            acc[...] = update
-        else:
-            acc[...] += update
-
-    block(own_key, own_value, own_pair_grad, 0, True)
-    for step in range(reach):
-
-        @pl.when(flags[step] > 0)
-        def _(step=step):
-            block(far[2 * step], far[2 * step + 1], far_grads[step], step + 1, False)
-
-        @pl.when(flags[step] == 0)
-        def _(step=step):
-            far_grads[step][...] = jnp.zeros_like(far_grads[step])
-
-    grad_query[...] = (acc[...] * factor).T.astype(bf16)
 
 
 def head_spec(rows, first, stride=1):
@@ -173,43 +123,6 @@
             flops=4 * HEAD * pairs, transcendentals=pairs, bytes_accessed=16 * rows * heads * HEAD
         ),
         name="attention_forward",
-    )(flags, *operands)
-
-
-def attention_backward(flags, seg_row, seg_cols, qkv, far, grad_out, attn_out, log_sum, heads):
-    rows = qkv.shape[0]
-    reach = len(far)
-    in_specs = [
-        pl.BlockSpec((1, rows), lambda h, flags: (0, 0)),
-        pl.BlockSpec(seg_cols.shape, lambda h, flags: (0, 0, 0)),
-        head_spec(rows, 0),
-        head_spec(rows, heads, 2),
-        head_spec(rows, heads + 1, 2),
-        head_spec(rows, 0),
-        head_spec(rows, 0),
-        pl.BlockSpec((1, 1, rows), lambda h, flags: (h, 0, 0)),
-    ]
-    operands = [seg_row, seg_cols, qkv, qkv, qkv, grad_out, attn_out, log_sum]
-    for piece in far:
-        in_specs += [head_spec(rows, 0, 2), head_spec(rows, 1, 2)]
-        operands += [piece, piece]
-    pairs = heads * rows * rows * (reach + 1)
-    pair_spec = pl.BlockSpec((rows, 2 * HEAD), lambda h, flags: (0, h))
-    pair_out = jax.ShapeDtypeStruct((rows, 2 * heads * HEAD), bf16)
-    return pl.pallas_call(
-        functools.partial(attn_backward_kernel, reach, HEAD ** (-0.5)),
-        out_shape=(jax.ShapeDtypeStruct((rows, heads * HEAD), bf16),) + (pair_out,) * (1 + reach),
-        grid_spec=pltpu.PrefetchScalarGridSpec(
-            num_scalar_prefetch=1,
-            grid=(heads,),
-            in_specs=in_specs,
-            out_specs=(head_spec(rows, 0),) + (pair_spec,) * (1 + reach),
-            scratch_shapes=[pltpu.VMEM((HEAD, rows), f32)],
-        ),
-        cost_estimate=pl.CostEstimate(
-            flops=10 * HEAD * pairs, transcendentals=pairs, bytes_accessed=32 * rows * heads * HEAD
-        ),
-        name="attention_backward",
     )(flags, *operands)
 
 
@@ -649,18 +562,21 @@
 
 
 def tail_kernel(sizes, width, reach, *refs):
-    up_left, out_left, one_left, grad_pre, attn, query, weights = refs[:7]
-    tokens, average, inverse, gain, grad_resid, vec_two = refs[7:13]
-    terms = refs[13 : 14 + reach]
-    refs = refs[14 + reach :]
+    up_left, out_left, one_left, grad_pre, attn = refs[:5]
+    tokens, average, inverse, gain, grad_resid, vec_two = refs[5:11]
+    seg_row, seg_cols, log_sum, weights, grad_attn, qkv = refs[11:17]
+    far = refs[17 : 17 + reach]
+    refs = refs[17 + reach :]
     outs, tokens_grad = refs[:6], refs[6]
-    pair, hop_recv, carry, held, part_send, part_recv, vec_one, means = refs[7:15]
-    hop_sems, hop_free, held_sems, part_sems = refs[15:19]
-    scratch = refs[19:]
+    query, terms, hop_recv, queries, grads, kept, held, part_send, part_recv = refs[7:16]
+    vec_one, means, hop_sems, head_sems, held_sems, part_sems = refs[16:22]
+    scratch = refs[22:]
     context = sizes["context"]
     place = lax.axis_index("context")
     depth, count = up_left.shape
     local_width = query.shape[1]
+    heads = local_width // HEAD
+    factor = HEAD ** (-0.5)
     blocks = depth // width
     lower = {"context": lax.rem(place + context - 1, context)}
     upper = {"context": lax.rem(place + 1, context)}
@@ -670,60 +586,87 @@
         both = vec_one[pl.ds(row, rows), :] + vec_two[pl.ds(row, rows), :]
         return jnp.concatenate([both] * (width // both.shape[1]), axis=1)
 
+    def pair_part(chunk, row, rows):
+        return jnp.dot(one_left[pl.ds(row, rows), :], terms[0, chunk], preferred_element_type=f32)
+
     pairs = [
         (product_part(up_left, grad_pre, 0, width), grad_pre.shape[1] // width, (0,)),
         (product_part(out_left, attn, 0, width), local_width // width, (1,)),
         (product_part(one_left, query, 0, width), local_width // width, (2,)),
-        (product_part(one_left, pair, 0, width), 2 * local_width // width, (3, 4)),
+        (pair_part, heads, (3, 4)),
         (vec_part, 1, (5,)),
     ]
     total = sum(p[1] for p in pairs)
     begin = sum(p[1] for p in pairs[:3])
-    hop_steps = [h * (begin - 2) // max(reach, 1) for h in range(reach + 1)]
-
-    def hop_copy(h):
-        source = terms[reach] if h == 0 else carry.at[h % carry.shape[0]]
-        sems = (hop_sems.at[0, h], hop_sems.at[1, h])
-        return remote(source, hop_recv.at[h % 2], sems, lower)
-
-    def hop(h):
-        term = terms[reach - h]
-        target = pair if h == reach else carry.at[h % carry.shape[0]]
-        if h > carry.shape[0] and h < reach:
+    gap = (begin - 1 - heads) // reach
+
+    def head_copies(h):
+        slot = lax.rem(h, 2)
+        one = pl.ds(pl.multiple_of(h * HEAD, HEAD), HEAD)
+        near = pl.ds(pl.multiple_of(local_width + 2 * h * HEAD, HEAD), 2 * HEAD)
+        two = pl.ds(pl.multiple_of(2 * h * HEAD, HEAD), 2 * HEAD)
+        sources = [(qkv.at[:, one], queries.at[slot]), (grad_attn.at[:, one], grads.at[slot])]
+        sources.append((qkv.at[:, near], kept.at[slot, 0]))
+        sources += [(far[i].at[:, two], kept.at[slot, i + 1]) for i in range(reach)]
+        return [
+            pltpu.make_async_copy(source, target, head_sems.at[slot, i])
+            for i, (source, target) in enumerate(sources)
+        ]
+
+    def head_block(h):
+        slot = lax.rem(h, 2)
+        one = pl.ds(pl.multiple_of(h * HEAD, HEAD), HEAD)
+        for copy in head_copies(h):
+            copy.wait()
+        own_query, own_grad = queries[slot], grads[slot]
+        delta = own_grad.astype(f32) * attn[:, one].astype(f32)
+        delta = jnp.sum(delta.T, axis=0, keepdims=True)
+        update = None
+        for index in range(reach + 1):
+            key, value = kept[slot, index, :, :HEAD], kept[slot, index, :, HEAD:]
+            scores = contract(key, own_query, 1, 1) * factor
+            allowed = seg_cols[index] == seg_row[...]
+            if index == 0:
+                key_pos = lax.broadcasted_iota(jnp.int32, (count, count), 0)
+                query_pos = lax.broadcasted_iota(jnp.int32, (count, count), 1)
+                allowed = allowed & (key_pos <= query_pos)
+            scores = jnp.where(allowed, scores, big_negative)
+            probs = jnp.where(allowed, jnp.exp(scores - log_sum[h]), 0.0)
+            grad_probs = contract(value, own_grad, 1, 1)
+            grad_scores = (probs * (grad_probs - delta)).astype(bf16)
+            key_grad = jnp.dot(grad_scores, own_query, preferred_element_type=f32) * factor
+            value_grad = jnp.dot(probs.astype(bf16), own_grad, preferred_element_type=f32)
+            terms[index, h, :, :HEAD] = key_grad.astype(bf16)
+            terms[index, h, :, HEAD:] = value_grad.astype(bf16)
+            change = contract(key, grad_scores, 0, 0)
+            update = change if update is None else update + change
+        query[:, one] = (update * factor).T.astype(bf16)
+
+        @pl.when(h + 2 < heads)
+        def _():
+            for copy in head_copies(h + 2):
+                copy.start()
+
+    def hop_copy(j, h):
+        sems = (hop_sems.at[0, j, h], hop_sems.at[1, j, h])
+        return remote(terms.at[reach - j, h], hop_recv.at[j, h], sems, lower)
+
+    def hop(j, h):
+        if j == 0:
+            head_block(h)
+        else:
+
+            @pl.when(place < context - 1)
+            def _():
+                hop_copy(j - 1, h).wait_recv()
+                both = terms[reach - j, h].astype(f32) + hop_recv[j - 1, h].astype(f32)
+                terms[reach - j, h] = both.astype(bf16)
+
+        if j < reach:
 
             @pl.when(place > 0)
             def _():
-                hop_copy(h - carry.shape[0]).wait_send()
-
-        if h > 0:
-
-            @pl.when(place < context - 1)
-            def _():
-                hop_copy(h - 1).wait_recv()
-
-                def add(i, c):
-                    at = pl.ds(pl.multiple_of(i * 64, 64), 64)
-                    got = hop_recv[(h - 1) % 2, at, :].astype(f32)
-                    target[at, :] = (term[at, :].astype(f32) + got).astype(bf16)
-                    return c
-
-                lax.fori_loop(0, count // 64, add, 0)
-                if h + 1 < reach:
-                    give(hop_free, upper)
-
-            @pl.when(place == context - 1)
-            def _():
-                target[...] = term[...]
-
-        elif reach == 0:
-            pair[...] = term[...]
-        if h < reach:
-
-            @pl.when(place > 0)
-            def _():
-                if h >= 2:
-                    pl.semaphore_wait(hop_free, 1)
-                hop_copy(h).start()
+                hop_copy(j, h).start()
 
     def held_copy(b):
         slot = lax.rem(b, 2)
@@ -746,7 +689,9 @@
         slot = lax.rem(b, 2)
         held_copy(b).wait()
         value = contract(query[...], held[slot, :, :local_width], 1, 1)
-        value = value + contract(pair[...], held[slot, :, local_width:], 1, 1)
+        for h in range(heads):
+            first = local_width + 2 * h * HEAD
+            value = value + contract(terms[0, h], held[slot, :, first : first + 2 * HEAD], 1, 1)
         rounded = value.astype(bf16)
         part_send[b] = rounded
         part_copy(b).start()
@@ -790,11 +735,18 @@
         lax.fori_loop(0, blocks, write, 0)
 
     def extra(s):
-        for h in range(reach + 1):
-
-            @pl.when(s == hop_steps[h])
-            def _(h=h):
-                hop(h)
+        @pl.when(s == 0)
+        def _():
+            for h in range(min(2, heads)):
+                for copy in head_copies(h):
+                    copy.start()
+
+        for j in range(reach + 1):
+            first = 1 + j * gap
+
+            @pl.when((s >= first) & (s < first + heads))
+            def _(j=j, first=first):
+                hop(j, s - first)
 
         @pl.when(s == begin - 2)
         def _():
@@ -813,59 +765,60 @@
         def _():
             norm_result()
 
-    assert begin + blocks < total
+    assert begin + blocks < total and width == 2 * HEAD and gap > 0
     reduce_loop(sizes, width, depth, pairs, outs, scratch, (other, lower, upper), extra)
 
     @pl.when(place > 0)
     def _():
-        for h in range(reach):
-            if h == 0 or h >= reach - carry.shape[0]:
-                hop_copy(h).wait_send()
+        for j in range(reach):
+            for h in range(heads):
+                hop_copy(j, h).wait_send()
 
     for b in range(blocks):
         part_copy(b).wait_send()
 
 
 def backward_tail(
-    lefts, grad_pre, attn, query, weights, norm, grad_resid, vec_two, terms, sizes, width, number
+    lefts, grad_pre, attn, norm, grad_resid, vec_two, masks, weights, pieces, sizes, width, number
 ):
     depth, count = lefts[0].shape
-    local_width = query.shape[1]
+    local_width = attn.shape[1]
+    heads = local_width // HEAD
     hidden = grad_pre.shape[1]
-    reach = len(terms) - 1
+    reach = len(pieces) - 2
     piece = depth // (sizes["fsdp"] * sizes["context"])
     blocks = depth // width
     vmem = pl.BlockSpec(memory_space=pltpu.VMEM)
     dma = pltpu.SemaphoreType.DMA
     columns = (hidden, local_width, local_width, local_width, local_width, width)
-    operands = [*lefts, grad_pre, attn, query, weights, *norm, grad_resid, vec_two, *terms]
-    in_specs = [vmem] * len(operands)
-    in_specs[6] = pl.BlockSpec(memory_space=pl.ANY)
-    slots = max(1, min(2, reach - 1))
-    hops = max(reach, 1)
+    near = [*lefts, grad_pre, attn, *norm, grad_resid, vec_two, *masks]
+    far = [weights, *pieces]
     return pl.pallas_call(
         functools.partial(tail_kernel, sizes, width, reach),
         out_shape=tuple(jax.ShapeDtypeStruct((piece, n), f32) for n in columns)
         + (jax.ShapeDtypeStruct((count, depth), bf16),),
-        in_specs=in_specs,
+        in_specs=[vmem] * len(near) + [pl.BlockSpec(memory_space=pl.ANY)] * len(far),
         out_specs=(vmem,) * 7,
         scratch_shapes=[
-            pltpu.VMEM((count, 2 * local_width), bf16),
-            pltpu.VMEM((min(2, hops), count, 2 * local_width), bf16),
-            pltpu.VMEM((slots, count, 2 * local_width), bf16),
+            pltpu.VMEM((count, local_width), bf16),
+            pltpu.VMEM((reach + 1, heads, count, 2 * HEAD), bf16),
+            pltpu.VMEM((reach, heads, count, 2 * HEAD), bf16),
+            pltpu.VMEM((2, count, HEAD), bf16),
+            pltpu.VMEM((2, count, HEAD), bf16),
+            pltpu.VMEM((2, reach + 1, count, 2 * HEAD), bf16),
             pltpu.VMEM((2, width, 3 * local_width), bf16),
             pltpu.VMEM((blocks, count, width), bf16),
             pltpu.VMEM((blocks, count, width), bf16),
             pltpu.VMEM((depth, 128), f32),
             pltpu.VMEM((2, count, 1), f32),
-            dma((2, hops)),
-            pltpu.SemaphoreType.REGULAR,
+            dma((2, reach, heads)),
+            dma((2, reach + 3)),
             dma((2,)),
             dma((2, blocks)),
         ]
         + reduce_scratch(sizes, width, depth),
         compiler_params=pltpu.CompilerParams(
-            collective_id=number, has_side_effects=True, vmem_limit_bytes=62 * 1024 * 1024
+            collective_id=number, has_side_effects=True, vmem_limit_bytes=63 * 1024 * 1024
         ),
         cost_estimate=pl.CostEstimate(
             flops=8 * depth * count * (hidden + 4 * local_width),
@@ -873,7 +826,7 @@
             bytes_accessed=16 * depth * count,
         ),
         name="backward_tail",
-    )(*operands)
+    )(*near, *far)
 
 
 def per_device(
@@ -978,19 +931,16 @@
         1,
     )
     output = output.reshape(tokens.shape)
-    results = attention_backward(
-        flags, seg_row, seg_cols, qkv, far, grad_attn, attn, log_sum, heads
-    )
     up_grad, out_grad, query_grad, key_grad, value_grad, vector_part, tokens_grad = backward_tail(
         (up_left, out_left, one_left),
         grad_pre,
         attn,
-        results[0],
-        attn_full,
         (tokens.reshape(group_len, model_width), mean_one, inv_one, gain_one[None]),
         grad_resid,
         vec_two,
-        results[1:],
+        (seg_row, seg_cols, log_sum),
+        attn_full,
+        (grad_attn, qkv, *far),
         sizes,
         WIDTH,
         2,

time: 864 us -> 836 us (0.968)
  Pallas kernels: 434 us -> 402 us
  local copies, waits for them, and re-layouts: 57.2 us -> 39.1 us
  waiting for transfers between devices: 269 us -> 282 us
    all_gather x1 -> x0, local copies, waits for them, and re-layouts: 21.9 us -> none  [per_device(): lax.all_gather(jnp.concatenate([query_weight, pair_weight, out_weight, ve...]
    pallas_call x1, Pallas kernels: 287 us -> 269 us  [backward_tail(): pl.pallas_call(functools.partial(tail_kernel, sizes, width, reach), out_s...]
    ppermute x2, waiting for transfers between devices: 25.1 us -> 42 us  [swap(): return lax.ppermute(array, axis, [(i, i ^ 1) for i in range(size)])]
    pallas_call x1 -> x0, Pallas kernels: 13.2 us -> none  [attention_backward(): pl.pallas_call(functools.partial(attn_backward_kernel, reach, HEAD ** (-0...]
  transfers between devices with their start and end apart: 6 -> 6, of which waited for: 6 -> 6; matrix products, arithmetic and copies ran while one was open for 9% -> 7% of each run, Pallas kernels for 1% -> 1%
where the time goes in v4:
time: 836 us; the launch traced here: 829 us
  Pallas kernels  402 us (48%)
  waiting for transfers between devices  282 us (34%)
  matrix products  50.2 us (6%)
  local copies, waits for them, and re-layouts  39.1 us (5%)
  other arithmetic  25.3 us (3%)
  between operations  16 us (2%)
  starting transfers between devices  13.9 us (2%)
    pallas_call x1, Pallas kernels, backward_tail(): pl.pallas_call(functools.partial(tail_kernel, sizes, width, reach), out_s...  269 us
    ppermute x2, waiting for transfers between devices, line_move(): return lax.ppermute(array, axis, moves)  126 us
    pallas_call x1, Pallas kernels, backward_middle(): pl.pallas_call(functools.partial(middle_kernel, sizes, width), out_shape=...  122 us
    all_gather x1, waiting for transfers between devices, per_device(): lax.all_gather(jnp.concatenate([query_weight, pair_weight, out_weight, ve...  95.1 us
    ppermute x2, waiting for transfers between devices, swap(): return lax.ppermute(array, axis, [(i, i ^ 1) for i in range(size)])  42 us
    all_gather x1, waiting for transfers between devices, per_device(): lax.all_gather(jnp.concatenate([up_weight, down_weight], axis=1), weight_...  18.5 us
    dot_general x1, matrix products, per_device(): grad_act = jnp.dot(grad_rows, full_down, preferred_element_type=f32)  17.1 us
  transfers between devices with their start and end apart: 6, of which 6 were waited for; matrix products, arithmetic and copies ran while one was open for 7% of the time, Pallas kernels for 1%

profile of v4, /device:TPU:0, one launch (start us, length us, event | category | flops | bytes accessed | tf_op | source)
XLA Modules:
  0.0 829.0 jit_solution(753888012496855874)
XLA Ops:
  13.2 2.8 pad_maximum_fusion
  17.2 95.1 %all-gather.3.cloned.1.call-done.refs_9_.refs_14_ = bf16[2048,4224]{1,0:T(8,128)(2,1)} async-done(((bf16[128,4224]{1,0:T(8,128)(2,1)}), bf16[2048,4224]{1,0:T(8,128)(2,1)}) %all-gather.3.cloned.1.call-update) | async-done | bytes 17301520 | tf_op jit(solution)/shard_map/all_gather | solution.py:863
  113.4 2.5 fusion.33
  115.9 10.4 %fusion.15.refs_2_.refs_3_.refs_4_.refs_16_ = bf16[512,3072]{1,0:T(8,128)(2,1)S(1)} fusion(bf16[2048,4224]{1,0:T(8,128)(2,1)} %all-gather.3.cloned.1.call-done.refs_9_.refs_14_, f32[2048]{0:T(1024)S(1)} %get-tuple-element.63, f32[2048]{0:T(1024)S(1)} %get-tuple-element.65, f32[512]{0:T(512)S(1)} %add_rsqrt_fusion.1, f32[512]{0:T(512)S(1)} %broadcast_multiply_fusion.1, ...), kind=kOutput, calls=%fused_computation.19 | convolution fusion | flops 6450315264 | bytes 17846272 | tf_op jit(solution)/shard_map/dot_general | solution.py:883
  126.5 4.8 collective-permute-start
  131.3 66.2 %collective-permute-done.refs_5_.refs_6_.refs_17_ = bf16[512,2048]{1,0:T(8,128)(2,1)} collective-permute-done((bf16[512,2048]{1,0:T(8,128)(2,1)S(1)}, bf16[512,2048]{1,0:T(8,128)(2,1)}, u32[]{:S(2)}, u32[]{:S(2)}) %collective-permute-start) | collective-permute-done | bytes 2097184 | tf_op jit(solution)/shard_map/ppermute | solution.py:135
  197.6 5.8 collective-permute-start.1
  209.6 60.0 %collective-permute-done.1.refs_7_.refs_8_.refs_18_ = bf16[512,2048]{1,0:T(8,128)(2,1)} collective-permute-done((bf16[512,2048]{1,0:T(8,128)(2,1)}, bf16[512,2048]{1,0:T(8,128)(2,1)}, u32[]{:S(2)}, u32[]{:S(2)}) %collective-permute-start.1) | collective-permute-done | bytes 2097184 | tf_op jit(solution)/shard_map/ppermute | solution.py:135
  269.6 11.1 %attention_forward.1 = (bf16[512,1024]{1,0:T(8,128)(2,1)}, f32[8,1,512]{2,1,0:T(1,128)}) custom-call(s32[2]{0:T(128)} %add_convert_fusion.1.flags, s32[1,512]{1,0:T(1,128)} %copy-done.17, s32[3,512,1]{2,1,0:T(8,128)} %copy.58.refs_1_.refs_12_, bf16[512,3072]{1,0:T(8,128)(2,1)} %copy-done.1, bf16[512,3072]{1,0:T(8,128)(2,1)} %copy-done.1, ...), custom_call_target="tpu_custom_call" | custom-call | flops 3221225472 | bytes 8388608 | tf_op jit(solution)/shard_map/attention_forward/pallas_call | solution.py:102
  280.7 6.4 fusion.24
  293.8 39.2 %collective-permute-done.2 = bf16[512,2048]{1,0:T(8,128)(2,1)} collective-permute-done((bf16[512,2048]{1,0:T(8,128)(2,1)}, bf16[512,2048]{1,0:T(8,128)(2,1)}, u32[]{:S(2)}, u32[]{:S(2)}) %collective-permute-start.2) | collective-permute-done | bytes 2097184 | tf_op jit(solution)/shard_map/ppermute | solution.py:130
  333.0 4.7 fusion.32
  341.9 4.3 fusion.37
  346.2 4.1 copy.60.refs_0_
  350.3 4.0 copy.64.refs_0_
  354.3 2.5 copy.65.refs_2_
  356.7 4.3 add_convert_fusion
  361.1 18.5 %all-gather.5.cloned.1.call-done.refs_8_ = bf16[2048,8192]{1,0:T(8,128)(2,1)} async-done(((bf16[128,8192]{1,0:T(8,128)(2,1)}), bf16[2048,8192]{1,0:T(8,128)(2,1)}) %all-gather.5.cloned.1.call-update) | async-done | bytes 33554448 | tf_op jit(solution)/shard_map/all_gather | solution.py:869
  379.6 16.3 %multiply_convert_fusion = (bf16[512,4096]{1,0:T(8,128)(2,1)}, f32[512,4096]{1,0:T(8,128)}) fusion(bf16[512,2048]{1,0:T(8,128)(2,1)} %add_convert_fusion, bf16[2048,8192]{1,0:T(8,128)(2,1)} %all-gather.5.cloned.1.call-done.refs_8_), kind=kOutput, calls=%fused_computation.12 | convolution fusion | flops 8600420352 | bytes 31457280 | tf_op jit(solution)/shard_map/dot_general | solution.py:910
  395.9 17.1 %fusion.10.refs_2_.refs_3_ = bf16[512,4096]{1,0:T(8,128)(2,1)} fusion(f32[512,4096]{1,0:T(8,128)} %get-tuple-element.73, bf16[2048,8192]{1,0:T(8,128)(2,1)} %all-gather.5.cloned.1.call-done.refs_8_, bf16[1,512,2048]{2,1,0:T(8,128)(2,1)S(1)} %copy-done.6), kind=kOutput, calls=%fused_computation.11 | convolution fusion | flops 8610906112 | bytes 31457280 | tf_op jit(solution)/shard_map/dot_general | solution.py:917
  413.0 122.4 %backward_middle.1 = (f32[128,4096]{1,0:T(8,128)}, bf16[512,2048]{1,0:T(8,128)(2,1)}, f32[512,2048]{1,0:T(8,128)}, bf16[2048,512]{1,0:T(8,128)(2,1)}, f32[2048,128]{1,0:T(8,128)}, /*index=5*/bf16[512,1024]{1,0:T(8,128)(2,1)}) custom-call(bf16[2048,512]{1,0:T(8,128)(2,1)} %copy.60.refs_0_, bf16[512,4096]{1,0:T(8,128)(2,1)} %get-tuple-element.72.refs_1_, ...), custom_call_target="tpu_custom_call" | custom-call | flops 51539607552 | bytes 33554432 | tf_op jit(solution)/shard_map/backward_middle/pallas_call | solution.py:528
  535.4 269.0 %backward_tail.1 = (f32[128,4096]{1,0:T(8,128)}, f32[128,1024]{1,0:T(8,128)}, f32[128,1024]{1,0:T(8,128)}, f32[128,1024]{1,0:T(8,128)}, f32[128,1024]{1,0:T(8,12...) custom-call(bf16[2048,512]{1,0:T(8,128)(2,1)} %copy.64.refs_0_, bf16[2048,512]{1,0:T(8,128)(2,1)} %get-tuple-element.37.refs_1_, ...), custom_call_target="tpu_custom_call" | custom-call | flops 68719476736 | bytes 16777216 | tf_op jit(solution)/shard_map/backward_tail/pallas_call | solution.py:796
  806.8 2.8 collective-permute-done.3
  811.3 3.2 copy.79
  (83 shorter events, 35.3 us)
Async XLA Ops:
  7.2 4.9 copy-start.15
  7.2 4.9 copy-start.16
  7.2 6.0 copy-start.10
  7.2 105.1 %all-gather.3.cloned.1.call-start = ((), (), s32[]{:S(2)}) async-start(), calls=%async_computation | async-start | bytes 18382848 | tf_op jit(solution)/shard_map/all_gather | solution.py:863
  13.2 3.0 copy-start.2
  13.2 366.4 %all-gather.5.cloned.1.call-start = ((), (), s32[]{:S(2)}) async-start(), calls=%async_computation.1 | async-start | bytes 35651584 | tf_op jit(solution)/shard_map/all_gather | solution.py:869
  126.4 143.2 %copy-start.1 = (bf16[512,3072]{1,0:T(8,128)(2,1)}, bf16[512,3072]{1,0:T(8,128)(2,1)S(1)}, u32[]{:S(2)}) copy-start(bf16[512,3072]{1,0:T(8,128)(2,1)S(1)} %fusion.15.refs_2_.refs_3_.refs_4_.refs_16_) | copy-start | bytes 9437188
  126.4 77.0 %copy-start.18 = (s32[1,2048]{1,0:T(1,128)S(1)}, s32[1,2048]{1,0:T(1,128)}, u32[]{:S(2)}) copy-start(s32[1,2048]{1,0:T(1,128)} %param.14) | copy-start | bytes 24580
  126.5 71.0 %collective-permute-start = (bf16[512,2048]{1,0:T(8,128)(2,1)S(1)}, bf16[512,2048]{1,0:T(8,128)(2,1)}, u32[]{:S(2)}, u32[]{:S(2)}) collective-permute-start(bf16[512,2048]{1,0:T(8,128)(2,1)S(1)} %slice.79), channel_id=1, source_target_pairs={{0,2},{2,4},{4,6},{1,3},{3,5},{5,7},{8,10},{10,12},{12,14},{9,11},... | collective-permute-start | bytes 6291464 | tf_op jit(solution)/shard_map/ppermute | solution.py:135
  197.6 72.0 %collective-permute-start.1 = (bf16[512,2048]{1,0:T(8,128)(2,1)}, bf16[512,2048]{1,0:T(8,128)(2,1)}, u32[]{:S(2)}, u32[]{:S(2)}) collective-permute-start(bf16[512,2048]{1,0:T(8,128)(2,1)} %collective-permute-done.refs_5_.refs_6_.refs_17_), channel_id=1, source_target_pairs={{0,2},{2,4},{4,6},{1,3},{3,5},{5,7},{8,10},{10,12},{12,14},{9,11},... | collective-permute-start | bytes 6291464 | tf_op jit(solution)/shard_map/ppermute | solution.py:135
  203.4 66.1 %copy-start.17 = (s32[1,512]{1,0:T(1,128)}, s32[1,512]{1,0:T(1,128)S(1)}, u32[]{:S(2)}) copy-start(s32[1,512]{1,0:T(1,128)S(1)} %get-tuple-element.67.refs_0_.refs_11_) | copy-start | bytes 6148
  280.7 12.1 %copy-start.5 = (f32[1,2048]{0,1:T(8,128)S(1)}, f32[1,2048]{0,1:T(8,128)}, u32[]{:S(2)}) copy-start(f32[1,2048]{0,1:T(8,128)} %get-tuple-element.62) | copy-start | bytes 24580
  280.7 52.3 %copy-start.3 = (bf16[1,512,2048]{2,1,0:T(8,128)(2,1)S(1)}, bf16[1,512,2048]{2,1,0:T(8,128)(2,1)}, u32[]{:S(2)}) copy-start(bf16[1,512,2048]{2,1,0:T(8,128)(2,1)} %param.13) | copy-start | bytes 6291460
  287.1 45.8 %collective-permute-start.2 = (bf16[512,2048]{1,0:T(8,128)(2,1)}, bf16[512,2048]{1,0:T(8,128)(2,1)}, u32[]{:S(2)}, u32[]{:S(2)}) collective-permute-start(bf16[512,2048]{1,0:T(8,128)(2,1)} %fusion.24), channel_id=1, source_target_pairs={{0,1},{1,0},{2,3},{3,2},{4,5},{5,4},{6,7},{7,6},{8,9},{9,8},{10,11... | collective-permute-start | bytes 6291464 | tf_op jit(solution)/shard_map/ppermute | solution.py:130
  346.2 8.0 copy-start.4
  361.1 34.9 %copy-start.6 = (bf16[1,512,2048]{2,1,0:T(8,128)(2,1)S(1)}, bf16[1,512,2048]{2,1,0:T(8,128)(2,1)}, u32[]{:S(2)}) copy-start(bf16[1,512,2048]{2,1,0:T(8,128)(2,1)} %param.25) | copy-start | bytes 6291460
  804.4 10.1 %copy-start.9 = (bf16[512,2048]{1,0:T(8,128)(2,1)S(1)}, bf16[512,2048]{1,0:T(8,128)(2,1)}, u32[]{:S(2)}) copy-start(bf16[512,2048]{1,0:T(8,128)(2,1)} %get-tuple-element.42) | copy-start | bytes 6291460
  805.4 4.3 collective-permute-start.3
  811.3 4.6 copy-start.14
  811.3 5.4 copy-start.13
  814.5 2.9 copy-start.12
  814.5 3.7 copy-start.11
  814.5 4.5 copy-start.8
  815.8 4.5 copy-start.7
  (1 other events, 2.0 us)
Sparse Core Ops, SparseCore 0:
  13.3 98.9 all-gather.2
  114.4 265.1 all-gather.4

commit v5 on v4

--- a/solution.py
+++ b/solution.py
@@ -598,7 +598,8 @@
     ]
     total = sum(p[1] for p in pairs)
     begin = sum(p[1] for p in pairs[:3])
-    gap = (begin - 1 - heads) // reach
+    stride = 2
+    gap = (begin - 2 - stride * (heads - 1)) // reach
 
     def head_copies(h):
         slot = lax.rem(h, 2)
@@ -744,9 +745,13 @@
         for j in range(reach + 1):
             first = 1 + j * gap
 
-            @pl.when((s >= first) & (s < first + heads))
+            @pl.when(
+                (s >= first)
+                & (s < first + stride * heads)
+                & (lax.rem(s + stride - first % stride, stride) == 0)
+            )
             def _(j=j, first=first):
-                hop(j, s - first)
+                hop(j, lax.div(s - first, stride))
 
         @pl.when(s == begin - 2)
         def _():
@@ -855,6 +860,23 @@
     place = lax.axis_index("context")
     weight_axes = ("fsdp", "context")
 
+    assert tensor == 2
+    reach = min(context - 1, -(-(seq_len // 2 - 1) // group_len))
+    half_len = group_len // 2
+    side = lax.axis_index("tensor")
+    piece = lax.dynamic_slice_in_dim(
+        tokens.reshape(group_len, model_width), side * half_len, half_len, 0
+    )
+    far_tokens = []
+    for _ in range(reach):
+        piece = line_move(piece, "context", context, 1)
+        other = swap(piece, "tensor", tensor)
+        far_tokens.append(
+            jnp.where(side == 0, jnp.stack([piece, other]), jnp.stack([other, piece])).reshape(
+                group_len, model_width
+            )
+        )
+
     vectors = jnp.stack([attn_gain, attn_bias, mlp_gain, mlp_bias], axis=1)
     vectors = jnp.pad(vectors, ((0, 0), (0, HEAD - 4)))
     pair_weight = jnp.stack(
@@ -882,12 +904,15 @@
     normed_one = (hat_one * gain_one + bias_one).astype(bf16)
     qkv = jnp.dot(normed_one, full_qkv, preferred_element_type=f32).astype(bf16)
 
-    reach = min(context - 1, -(-(seq_len // 2 - 1) // group_len))
     far = []
-    piece = qkv[:, local_width:]
-    for _ in range(reach):
-        piece = line_move(piece, "context", context, 1)
-        far.append(piece)
+    for block in far_tokens:
+        far_hat, _ = norm_stats(block.astype(f32))
+        far_normed = (far_hat * gain_one + bias_one).astype(bf16)
+        far.append(
+            jnp.dot(
+                far_normed, full_qkv[:, local_width:], preferred_element_type=f32
+            ).astype(bf16)
+        )
     first = place * group_len
     seg_row = lax.dynamic_slice_in_dim(segments, first, group_len, 1)
     seg_cols = [seg_row]

time: 836 us -> 784 us (0.938)
  waiting for transfers between devices: 282 us -> 203 us
  other arithmetic: 25.3 us -> 46.2 us
  matrix products: 50.2 us -> 62.9 us
    ppermute x2, waiting for transfers between devices: 126 us -> 58.3 us  [line_move(): return lax.ppermute(array, axis, moves)]
    all_gather x1, waiting for transfers between devices: 95.1 us -> 28.2 us  [per_device(): lax.all_gather(jnp.concatenate([query_weight, pair_weight, out_weight, ve...]
    all_gather x1, waiting for transfers between devices: 18.5 us -> 63.5 us  [per_device(): lax.all_gather(jnp.concatenate([up_weight, down_weight], axis=1), weight_...]
    dot_general x0 -> x2, matrix products: none -> 14.9 us  [per_device(): jnp.dot(far_normed, full_qkv[:, local_width:], preferred_element_type=f32)]
    convert_element_type x0 -> x3, other arithmetic: none -> 11.2 us  [the longest x2 7.93 us: per_device(): far_hat, _ = norm_stats(block.astype(f32))]
    ppermute x2 -> x4, waiting for transfers between devices: 42 us -> 52.8 us  [swap(): return lax.ppermute(array, axis, [(i, i ^ 1) for i in range(size)])]
  transfers between devices with their start and end apart: 6 -> 8, of which waited for: 6 -> 7; matrix products, arithmetic and copies ran while one was open for 7% -> 12% of each run, Pallas kernels for 1% -> 1%
where the time goes in v5:
time: 784 us; the launch traced here: 780 us
  Pallas kernels  397 us (51%)
  waiting for transfers between devices  203 us (26%)
  matrix products  62.9 us (8%)
  other arithmetic  46.2 us (6%)
  local copies, waits for them, and re-layouts  39.9 us (5%)
  between operations  15.9 us (2%)
  starting transfers between devices  15.5 us (2%)
    pallas_call x1, Pallas kernels, backward_tail(): pl.pallas_call(functools.partial(tail_kernel, sizes, width, reach), out_s...  265 us
    pallas_call x1, Pallas kernels, backward_middle(): pl.pallas_call(functools.partial(middle_kernel, sizes, width), out_shape=...  121 us
    all_gather x1, waiting for transfers between devices, per_device(): lax.all_gather(jnp.concatenate([up_weight, down_weight], axis=1), weight_...  63.5 us
    ppermute x2, waiting for transfers between devices, line_move(): return lax.ppermute(array, axis, moves)  58.3 us
    ppermute x4, waiting for transfers between devices, swap(): return lax.ppermute(array, axis, [(i, i ^ 1) for i in range(size)])  52.8 us
    all_gather x1, waiting for transfers between devices, per_device(): lax.all_gather(jnp.concatenate([query_weight, pair_weight, out_weight, ve...  28.2 us
    dot_general x1, matrix products, per_device(): grad_act = jnp.dot(grad_rows, full_down, preferred_element_type=f32)  17.2 us
    dot_general x1, matrix products, per_device(): jnp.dot(after(normed_two, row_left, up_left, one_left), full_up, preferre...  16.1 us
  transfers between devices with their start and end apart: 8, of which 7 were waited for; matrix products, arithmetic and copies ran while one was open for 12% of the time, Pallas kernels for 1%

profile of v5, /device:TPU:0, one launch (start us, length us, event | category | flops | bytes accessed | tf_op | source)
XLA Modules:
  0.0 779.7 jit_solution(4797370970422826723)
XLA Ops:
  17.2 5.0 collective-permute-start
  22.3 34.1 %collective-permute-done = bf16[256,2048]{1,0:T(8,128)(2,1)S(1)} collective-permute-done((bf16[256,2048]{1,0:T(8,128)(2,1)}, bf16[256,2048]{1,0:T(8,128)(2,1)S(1)}, u32[]{:S(2)}, u32[]{:S(2)}) %collective-permute-start) | collective-permute-done | bytes 1048608 | tf_op jit(solution)/shard_map/ppermute | solution.py:135
  56.4 5.2 collective-permute-start.2
  70.2 24.2 %collective-permute-done.2 = bf16[256,2048]{1,0:T(8,128)(2,1)} collective-permute-done((bf16[256,2048]{1,0:T(8,128)(2,1)S(1)}, bf16[256,2048]{1,0:T(8,128)(2,1)}, u32[]{:S(2)}, u32[]{:S(2)}) %collective-permute-start.2) | collective-permute-done | bytes 1048608 | tf_op jit(solution)/shard_map/ppermute | solution.py:135
  100.3 4.0 fusion.46
  104.3 13.2 %collective-permute-done.3 = bf16[256,2048]{1,0:T(8,128)(2,1)S(1)} collective-permute-done((bf16[256,2048]{1,0:T(8,128)(2,1)}, bf16[256,2048]{1,0:T(8,128)(2,1)S(1)}, u32[]{:S(2)}, u32[]{:S(2)}) %collective-permute-start.3) | collective-permute-done | bytes 1048608 | tf_op jit(solution)/shard_map/ppermute | solution.py:130
  122.2 3.9 fusion.47
  126.1 28.2 %all-gather.3.cloned.1.call-done.refs_9_.refs_14_ = bf16[2048,4224]{1,0:T(8,128)(2,1)} async-done(((bf16[128,4224]{1,0:T(8,128)(2,1)}), bf16[2048,4224]{1,0:T(8,128)(2,1)}) %all-gather.3.cloned.1.call-update) | async-done | bytes 17301520 | tf_op jit(solution)/shard_map/all_gather | solution.py:885
  161.5 9.3 %fusion.42.refs_7_.refs_8_.refs_18_ = bf16[512,2048]{1,0:T(8,128)(2,1)} fusion(bf16[512,2048]{1,0:T(8,128)(2,1)S(1)} %get-tuple-element.67, bf16[2048,4224]{1,0:T(8,128)(2,1)} %all-gather.3.cloned.1.call-done.refs_9_.refs_14_), kind=kOutput, calls=%fused_computation.46 | convolution fusion | flops 4296015872 | bytes 12582912 | tf_op jit(solution)/shard_map/dot_general | solution.py:912
  170.7 5.7 fusion.39.refs_5_.refs_6_.refs_17_
  176.4 8.3 %fusion.19.refs_2_.refs_3_.refs_4_.refs_16_ = bf16[512,3072]{1,0:T(8,128)(2,1)} fusion(bf16[2048,4224]{1,0:T(8,128)(2,1)S(1)} %bitcast.96, f32[2048]{0:T(1024)S(1)} %get-tuple-element.63, f32[2048]{0:T(1024)S(1)} %get-tuple-element.65, f32[512]{0:T(512)S(1)} %add_rsqrt_fusion.1, f32[512]{0:T(512)S(1)} %broadcast_multiply_fusion.3, ...), kind=kOutput, calls=%fused_computation.23 | convolution fusion | flops 6450315264 | bytes 17846272 | tf_op jit(solution)/shard_map/dot_general | solution.py:905
  184.7 11.1 %attention_forward.1 = (bf16[512,1024]{1,0:T(8,128)(2,1)}, f32[8,1,512]{2,1,0:T(1,128)}) custom-call(s32[2]{0:T(128)} %add_convert_fusion.1.flags, s32[1,512]{1,0:T(1,128)} %copy-done.15, s32[3,512,1]{2,1,0:T(8,128)} %copy.58.refs_1_.refs_12_, bf16[512,3072]{1,0:T(8,128)(2,1)} %fusion.19.refs_2_.refs_3_.refs_4_.refs_16_, ...), custom_call_target="tpu_custom_call" | custom-call | flops 3221225472 | bytes 8388608 | tf_op jit(solution)/shard_map/attention_forward/pallas_call | solution.py:102
  195.8 6.3 fusion.36
  208.4 36.5 %collective-permute-done.4 = bf16[512,2048]{1,0:T(8,128)(2,1)} collective-permute-done((bf16[512,2048]{1,0:T(8,128)(2,1)}, bf16[512,2048]{1,0:T(8,128)(2,1)}, u32[]{:S(2)}, u32[]{:S(2)}) %collective-permute-start.4) | collective-permute-done | bytes 2097184 | tf_op jit(solution)/shard_map/ppermute | solution.py:130
  244.9 4.6 fusion.56
  253.8 4.4 fusion.63
  258.2 4.1 copy.60.refs_0_
  262.3 3.9 copy.64.refs_0_
  268.7 4.4 add_convert_fusion
  273.1 63.5 %all-gather.5.cloned.1.call-done.refs_8_ = bf16[2048,8192]{1,0:T(8,128)(2,1)} async-done(((bf16[128,8192]{1,0:T(8,128)(2,1)}), bf16[2048,8192]{1,0:T(8,128)(2,1)}) %all-gather.5.cloned.1.call-update) | async-done | bytes 33554448 | tf_op jit(solution)/shard_map/all_gather | solution.py:891
  336.5 16.1 %multiply_convert_fusion = (bf16[512,4096]{1,0:T(8,128)(2,1)}, f32[512,4096]{1,0:T(8,128)}) fusion(bf16[512,2048]{1,0:T(8,128)(2,1)} %add_convert_fusion, bf16[2048,8192]{1,0:T(8,128)(2,1)} %all-gather.5.cloned.1.call-done.refs_8_), kind=kOutput, calls=%fused_computation.12 | convolution fusion | flops 8600420352 | bytes 31457280 | tf_op jit(solution)/shard_map/dot_general | solution.py:935
  352.7 17.2 %fusion.10.refs_2_.refs_3_ = bf16[512,4096]{1,0:T(8,128)(2,1)} fusion(f32[512,4096]{1,0:T(8,128)} %get-tuple-element.79, bf16[2048,8192]{1,0:T(8,128)(2,1)} %all-gather.5.cloned.1.call-done.refs_8_, bf16[1,512,2048]{2,1,0:T(8,128)(2,1)S(1)} %copy-done.4), kind=kOutput, calls=%fused_computation.11 | convolution fusion | flops 8610906112 | bytes 31457280 | tf_op jit(solution)/shard_map/dot_general | solution.py:942
  369.9 120.6 %backward_middle.1 = (f32[128,4096]{1,0:T(8,128)}, bf16[512,2048]{1,0:T(8,128)(2,1)}, f32[512,2048]{1,0:T(8,128)}, bf16[2048,512]{1,0:T(8,128)(2,1)}, f32[2048,128]{1,0:T(8,128)}, /*index=5*/bf16[512,1024]{1,0:T(8,128)(2,1)}) custom-call(bf16[2048,512]{1,0:T(8,128)(2,1)} %copy.60.refs_0_, bf16[512,4096]{1,0:T(8,128)(2,1)} %get-tuple-element.78.refs_1_, ...), custom_call_target="tpu_custom_call" | custom-call | flops 51539607552 | bytes 33554432 | tf_op jit(solution)/shard_map/backward_middle/pallas_call | solution.py:528
  490.5 264.8 %backward_tail.1 = (f32[128,4096]{1,0:T(8,128)}, f32[128,1024]{1,0:T(8,128)}, f32[128,1024]{1,0:T(8,128)}, f32[128,1024]{1,0:T(8,128)}, f32[128,1024]{1,0:T(8,12...) custom-call(bf16[2048,512]{1,0:T(8,128)(2,1)} %copy.64.refs_0_, bf16[2048,512]{1,0:T(8,128)(2,1)} %get-tuple-element.37.refs_1_, ...), custom_call_target="tpu_custom_call" | custom-call | flops 68719476736 | bytes 16777216 | tf_op jit(solution)/shard_map/backward_tail/pallas_call | solution.py:801
  (111 shorter events, 65.2 us)
Async XLA Ops:
  7.2 4.9 copy-start.13
  7.2 4.9 copy-start.14
  7.2 6.0 copy-start.8
  7.2 147.1 %all-gather.3.cloned.1.call-start = ((), (), s32[]{:S(2)}) async-start(), calls=%async_computation | async-start | bytes 18382848 | tf_op jit(solution)/shard_map/all_gather | solution.py:885
  13.2 9.1 %copy-start.16 = (s32[1,2048]{1,0:T(1,128)S(1)}, s32[1,2048]{1,0:T(1,128)}, u32[]{:S(2)}) copy-start(s32[1,2048]{1,0:T(1,128)} %param.14) | copy-start | bytes 24580
  13.2 323.4 %all-gather.5.cloned.1.call-start = ((), (), s32[]{:S(2)}) async-start(), calls=%async_computation.1 | async-start | bytes 35651584 | tf_op jit(solution)/shard_map/all_gather | solution.py:891
  17.2 39.2 %collective-permute-start = (bf16[256,2048]{1,0:T(8,128)(2,1)}, bf16[256,2048]{1,0:T(8,128)(2,1)S(1)}, u32[]{:S(2)}, u32[]{:S(2)}) collective-permute-start(bf16[256,2048]{1,0:T(8,128)(2,1)} %dynamic-slice_bitcast_fusion), channel_id=1, source_target_pairs={{0,2},{2,4},{4,6},{1,3},{3,5},{5,7},{8,10},{10,12},{12,14},{9,11},... | collective-permute-start | bytes 3145736 | tf_op jit(solution)/shard_map/ppermute | solution.py:135
  22.3 78.0 %copy-start.15 = (s32[1,512]{1,0:T(1,128)}, s32[1,512]{1,0:T(1,128)S(1)}, u32[]{:S(2)}) copy-start(s32[1,512]{1,0:T(1,128)S(1)} %get-tuple-element.69.refs_0_.refs_11_) | copy-start | bytes 6148
  56.4 37.9 %collective-permute-start.2 = (bf16[256,2048]{1,0:T(8,128)(2,1)S(1)}, bf16[256,2048]{1,0:T(8,128)(2,1)}, u32[]{:S(2)}, u32[]{:S(2)}) collective-permute-start(bf16[256,2048]{1,0:T(8,128)(2,1)S(1)} %collective-permute-done), channel_id=1, source_target_pairs={{0,2},{2,4},{4,6},{1,3},{3,5},{5,7},{8,10},{10,12},{12,14},{9,11},... | collective-permute-start | bytes 3145736 | tf_op jit(solution)/shard_map/ppermute | solution.py:135
  61.7 33.9 %collective-permute-start.1 = (bf16[256,2048]{1,0:T(8,128)(2,1)S(1)}, bf16[256,2048]{1,0:T(8,128)(2,1)}, u32[]{:S(2)}, u32[]{:S(2)}) collective-permute-start(bf16[256,2048]{1,0:T(8,128)(2,1)S(1)} %collective-permute-done), channel_id=1, source_target_pairs={{0,1},{1,0},{2,3},{3,2},{4,5},{5,4},{6,7},{7,6},{8,9},{9,8},{10,11... | collective-permute-start | bytes 3145736 | tf_op jit(solution)/shard_map/ppermute | solution.py:130
  94.4 23.2 %collective-permute-start.3 = (bf16[256,2048]{1,0:T(8,128)(2,1)}, bf16[256,2048]{1,0:T(8,128)(2,1)S(1)}, u32[]{:S(2)}, u32[]{:S(2)}) collective-permute-start(bf16[256,2048]{1,0:T(8,128)(2,1)} %collective-permute-done.2), channel_id=1, source_target_pairs={{0,1},{1,0},{2,3},{3,2},{4,5},{5,4},{6,7},{7,6},{8,9},{9,8},{10,11... | collective-permute-start | bytes 3145736 | tf_op jit(solution)/shard_map/ppermute | solution.py:130
  158.1 12.6 %slice-start = ((s8[17301504]{0:T(1024)(128)(4,1)}), s8[4194304]{0:T(1024)(128)(4,1)S(1)}, s32[]{:S(2)}) async-start(s8[17301504]{0:T(1024)(128)(4,1)} %bitcast.95), calls=%async_computation.2 | async-start | bytes 8388608
  161.4 9.3 %slice-start.1 = ((s8[17301504]{0:T(1024)(128)(4,1)}), s8[4194304]{0:T(1024)(128)(4,1)S(1)}, s32[]{:S(2)}) async-start(s8[17301504]{0:T(1024)(128)(4,1)} %bitcast.95), calls=%async_computation.3 | async-start | bytes 8388608
  161.4 9.3 %slice-start.2 = ((s8[17301504]{0:T(1024)(128)(4,1)}), s8[4194304]{0:T(1024)(128)(4,1)S(1)}, s32[]{:S(2)}) async-start(s8[17301504]{0:T(1024)(128)(4,1)} %bitcast.95), calls=%async_computation.4 | async-start | bytes 8388608
  161.4 9.3 %slice-start.3 = ((s8[17301504]{0:T(1024)(128)(4,1)}), s8[4194304]{0:T(1024)(128)(4,1)S(1)}, s32[]{:S(2)}) async-start(s8[17301504]{0:T(1024)(128)(4,1)} %bitcast.95), calls=%async_computation.5 | async-start | bytes 8388608
  161.4 9.3 %slice-start.4 = ((s8[17301504]{0:T(1024)(128)(4,1)}), s8[524288]{0:T(1024)(128)(4,1)S(1)}, s32[]{:S(2)}) async-start(s8[17301504]{0:T(1024)(128)(4,1)} %bitcast.95), calls=%async_computation.6 | async-start | bytes 1048576
  202.1 42.8 %collective-permute-start.4 = (bf16[512,2048]{1,0:T(8,128)(2,1)}, bf16[512,2048]{1,0:T(8,128)(2,1)}, u32[]{:S(2)}, u32[]{:S(2)}) collective-permute-start(bf16[512,2048]{1,0:T(8,128)(2,1)} %fusion.36), channel_id=1, source_target_pairs={{0,1},{1,0},{2,3},{3,2},{4,5},{5,4},{6,7},{7,6},{8,9},{9,8},{10,11... | collective-permute-start | bytes 6291464 | tf_op jit(solution)/shard_map/ppermute | solution.py:130
  258.2 8.0 %copy-start.3 = (bf16[2048,512]{0,1:T(8,128)(2,1)S(1)}, bf16[2048,512]{0,1:T(8,128)(2,1)}, u32[]{:S(2)}) copy-start(bf16[2048,512]{0,1:T(8,128)(2,1)} %get-tuple-element.34) | copy-start | bytes 6291460
  273.1 79.6 %copy-start.4 = (bf16[1,512,2048]{2,1,0:T(8,128)(2,1)S(1)}, bf16[1,512,2048]{2,1,0:T(8,128)(2,1)}, u32[]{:S(2)}) copy-start(bf16[1,512,2048]{2,1,0:T(8,128)(2,1)} %param.25) | copy-start | bytes 6291460
  755.3 10.2 %copy-start.7 = (bf16[512,2048]{1,0:T(8,128)(2,1)S(1)}, bf16[512,2048]{1,0:T(8,128)(2,1)}, u32[]{:S(2)}) copy-start(bf16[512,2048]{1,0:T(8,128)(2,1)} %get-tuple-element.42) | copy-start | bytes 6291460
  756.3 4.3 collective-permute-start.5
  762.2 4.6 copy-start.12
  762.2 5.4 copy-start.11
  762.2 6.2 copy-start.10
  (6 other events, 21.5 us)
Sparse Core Ops, SparseCore 0:
  13.3 140.9 all-gather.2
  155.8 180.6 all-gather.4

commit v6 on v5

--- a/solution.py
+++ b/solution.py
@@ -502,12 +502,12 @@
         during(s, 1, norm_block)
         during(s, 1 + blocks, lambda b: send_block(blocks + b, act))
 
-        @pl.when(s == blocks + 3)
+        @pl.when(s == blocks + 4)
         def _():
             norm_means()
             out_copy().wait()
 
-        during(s, blocks + 4, norm_result)
+        during(s, blocks + 6, norm_result)
         during(s, blocks + 5, output_block)
 
     assert 2 * blocks <= total

time: 784 us -> 785 us (level)
  no operation moved by 1% of the time
where the time goes in v6:
time: 785 us; the launch traced here: 781 us
  Pallas kernels  397 us (51%)
  waiting for transfers between devices  203 us (26%)
  matrix products  62.9 us (8%)
  other arithmetic  46.2 us (6%)
  local copies, waits for them, and re-layouts  39.9 us (5%)
  between operations  15.9 us (2%)
  starting transfers between devices  15.3 us (2%)
    pallas_call x1, Pallas kernels, backward_tail(): pl.pallas_call(functools.partial(tail_kernel, sizes, width, reach), out_s...  265 us
    pallas_call x1, Pallas kernels, backward_middle(): pl.pallas_call(functools.partial(middle_kernel, sizes, width), out_shape=...  122 us
    all_gather x1, waiting for transfers between devices, per_device(): lax.all_gather(jnp.concatenate([up_weight, down_weight], axis=1), weight_...  63.5 us
    ppermute x2, waiting for transfers between devices, line_move(): return lax.ppermute(array, axis, moves)  58.3 us
    ppermute x4, waiting for transfers between devices, swap(): return lax.ppermute(array, axis, [(i, i ^ 1) for i in range(size)])  53 us
    all_gather x1, waiting for transfers between devices, per_device(): lax.all_gather(jnp.concatenate([query_weight, pair_weight, out_weight, ve...  28.2 us
    dot_general x1, matrix products, per_device(): grad_act = jnp.dot(grad_rows, full_down, preferred_element_type=f32)  17.2 us
    dot_general x1, matrix products, per_device(): jnp.dot(after(normed_two, row_left, up_left, one_left), full_up, preferre...  16.1 us
  transfers between devices with their start and end apart: 8, of which 7 were waited for; matrix products, arithmetic and copies ran while one was open for 12% of the time, Pallas kernels for 1%

profile of v6, /device:TPU:0, one launch (start us, length us, event | category | flops | bytes accessed | tf_op | source)
XLA Modules:
  0.0 780.6 jit_solution(4759410319822344569)
XLA Ops:
  17.2 5.0 collective-permute-start
  22.3 34.1 %collective-permute-done = bf16[256,2048]{1,0:T(8,128)(2,1)S(1)} collective-permute-done((bf16[256,2048]{1,0:T(8,128)(2,1)}, bf16[256,2048]{1,0:T(8,128)(2,1)S(1)}, u32[]{:S(2)}, u32[]{:S(2)}) %collective-permute-start) | collective-permute-done | bytes 1048608 | tf_op jit(solution)/shard_map/ppermute | solution.py:135
  56.4 5.2 collective-permute-start.2
  70.2 24.2 %collective-permute-done.2 = bf16[256,2048]{1,0:T(8,128)(2,1)} collective-permute-done((bf16[256,2048]{1,0:T(8,128)(2,1)S(1)}, bf16[256,2048]{1,0:T(8,128)(2,1)}, u32[]{:S(2)}, u32[]{:S(2)}) %collective-permute-start.2) | collective-permute-done | bytes 1048608 | tf_op jit(solution)/shard_map/ppermute | solution.py:135
  100.3 4.0 fusion.46
  104.3 13.2 %collective-permute-done.3 = bf16[256,2048]{1,0:T(8,128)(2,1)S(1)} collective-permute-done((bf16[256,2048]{1,0:T(8,128)(2,1)}, bf16[256,2048]{1,0:T(8,128)(2,1)S(1)}, u32[]{:S(2)}, u32[]{:S(2)}) %collective-permute-start.3) | collective-permute-done | bytes 1048608 | tf_op jit(solution)/shard_map/ppermute | solution.py:130
  122.2 3.9 fusion.47
  126.1 28.2 %all-gather.3.cloned.1.call-done.refs_9_.refs_14_ = bf16[2048,4224]{1,0:T(8,128)(2,1)} async-done(((bf16[128,4224]{1,0:T(8,128)(2,1)}), bf16[2048,4224]{1,0:T(8,128)(2,1)}) %all-gather.3.cloned.1.call-update) | async-done | bytes 17301520 | tf_op jit(solution)/shard_map/all_gather | solution.py:885
  161.5 9.3 %fusion.42.refs_7_.refs_8_.refs_18_ = bf16[512,2048]{1,0:T(8,128)(2,1)} fusion(bf16[512,2048]{1,0:T(8,128)(2,1)S(1)} %get-tuple-element.67, bf16[2048,4224]{1,0:T(8,128)(2,1)} %all-gather.3.cloned.1.call-done.refs_9_.refs_14_), kind=kOutput, calls=%fused_computation.46 | convolution fusion | flops 4296015872 | bytes 12582912 | tf_op jit(solution)/shard_map/dot_general | solution.py:912
  170.7 5.7 fusion.39.refs_5_.refs_6_.refs_17_
  176.4 8.3 %fusion.19.refs_2_.refs_3_.refs_4_.refs_16_ = bf16[512,3072]{1,0:T(8,128)(2,1)} fusion(bf16[2048,4224]{1,0:T(8,128)(2,1)S(1)} %bitcast.96, f32[2048]{0:T(1024)S(1)} %get-tuple-element.63, f32[2048]{0:T(1024)S(1)} %get-tuple-element.65, f32[512]{0:T(512)S(1)} %add_rsqrt_fusion.1, f32[512]{0:T(512)S(1)} %broadcast_multiply_fusion.3, ...), kind=kOutput, calls=%fused_computation.23 | convolution fusion | flops 6450315264 | bytes 17846272 | tf_op jit(solution)/shard_map/dot_general | solution.py:905
  184.7 11.1 %attention_forward.1 = (bf16[512,1024]{1,0:T(8,128)(2,1)}, f32[8,1,512]{2,1,0:T(1,128)}) custom-call(s32[2]{0:T(128)} %add_convert_fusion.1.flags, s32[1,512]{1,0:T(1,128)} %copy-done.15, s32[3,512,1]{2,1,0:T(8,128)} %copy.58.refs_1_.refs_12_, bf16[512,3072]{1,0:T(8,128)(2,1)} %fusion.19.refs_2_.refs_3_.refs_4_.refs_16_, ...), custom_call_target="tpu_custom_call" | custom-call | flops 3221225472 | bytes 8388608 | tf_op jit(solution)/shard_map/attention_forward/pallas_call | solution.py:102
  195.8 6.3 fusion.36
  208.4 36.5 %collective-permute-done.4 = bf16[512,2048]{1,0:T(8,128)(2,1)} collective-permute-done((bf16[512,2048]{1,0:T(8,128)(2,1)}, bf16[512,2048]{1,0:T(8,128)(2,1)}, u32[]{:S(2)}, u32[]{:S(2)}) %collective-permute-start.4) | collective-permute-done | bytes 2097184 | tf_op jit(solution)/shard_map/ppermute | solution.py:130
  244.9 4.6 fusion.56
  253.8 4.4 fusion.63
  258.2 4.1 copy.60.refs_0_
  262.3 3.9 copy.64.refs_0_
  268.7 4.4 add_convert_fusion
  273.1 63.5 %all-gather.5.cloned.1.call-done.refs_8_ = bf16[2048,8192]{1,0:T(8,128)(2,1)} async-done(((bf16[128,8192]{1,0:T(8,128)(2,1)}), bf16[2048,8192]{1,0:T(8,128)(2,1)}) %all-gather.5.cloned.1.call-update) | async-done | bytes 33554448 | tf_op jit(solution)/shard_map/all_gather | solution.py:891
  336.5 16.1 %multiply_convert_fusion = (bf16[512,4096]{1,0:T(8,128)(2,1)}, f32[512,4096]{1,0:T(8,128)}) fusion(bf16[512,2048]{1,0:T(8,128)(2,1)} %add_convert_fusion, bf16[2048,8192]{1,0:T(8,128)(2,1)} %all-gather.5.cloned.1.call-done.refs_8_), kind=kOutput, calls=%fused_computation.12 | convolution fusion | flops 8600420352 | bytes 31457280 | tf_op jit(solution)/shard_map/dot_general | solution.py:935
  352.7 17.2 %fusion.10.refs_2_.refs_3_ = bf16[512,4096]{1,0:T(8,128)(2,1)} fusion(f32[512,4096]{1,0:T(8,128)} %get-tuple-element.79, bf16[2048,8192]{1,0:T(8,128)(2,1)} %all-gather.5.cloned.1.call-done.refs_8_, bf16[1,512,2048]{2,1,0:T(8,128)(2,1)S(1)} %copy-done.4), kind=kOutput, calls=%fused_computation.11 | convolution fusion | flops 8610906112 | bytes 31457280 | tf_op jit(solution)/shard_map/dot_general | solution.py:942
  369.9 121.6 %backward_middle.1 = (f32[128,4096]{1,0:T(8,128)}, bf16[512,2048]{1,0:T(8,128)(2,1)}, f32[512,2048]{1,0:T(8,128)}, bf16[2048,512]{1,0:T(8,128)(2,1)}, f32[2048,128]{1,0:T(8,128)}, /*index=5*/bf16[512,1024]{1,0:T(8,128)(2,1)}) custom-call(bf16[2048,512]{1,0:T(8,128)(2,1)} %copy.60.refs_0_, bf16[512,4096]{1,0:T(8,128)(2,1)} %get-tuple-element.78.refs_1_, ...), custom_call_target="tpu_custom_call" | custom-call | flops 51539607552 | bytes 33554432 | tf_op jit(solution)/shard_map/backward_middle/pallas_call | solution.py:528
  491.5 264.8 %backward_tail.1 = (f32[128,4096]{1,0:T(8,128)}, f32[128,1024]{1,0:T(8,128)}, f32[128,1024]{1,0:T(8,128)}, f32[128,1024]{1,0:T(8,128)}, f32[128,1024]{1,0:T(8,12...) custom-call(bf16[2048,512]{1,0:T(8,128)(2,1)} %copy.64.refs_0_, bf16[2048,512]{1,0:T(8,128)(2,1)} %get-tuple-element.37.refs_1_, ...), custom_call_target="tpu_custom_call" | custom-call | flops 68719476736 | bytes 16777216 | tf_op jit(solution)/shard_map/backward_tail/pallas_call | solution.py:801
  (111 shorter events, 65.2 us)
Async XLA Ops:
  7.2 4.9 copy-start.13
  7.2 4.9 copy-start.14
  7.2 6.0 copy-start.8
  7.2 147.1 %all-gather.3.cloned.1.call-start = ((), (), s32[]{:S(2)}) async-start(), calls=%async_computation | async-start | bytes 18382848 | tf_op jit(solution)/shard_map/all_gather | solution.py:885
  13.2 9.1 %copy-start.16 = (s32[1,2048]{1,0:T(1,128)S(1)}, s32[1,2048]{1,0:T(1,128)}, u32[]{:S(2)}) copy-start(s32[1,2048]{1,0:T(1,128)} %param.14) | copy-start | bytes 24580
  13.2 323.4 %all-gather.5.cloned.1.call-start = ((), (), s32[]{:S(2)}) async-start(), calls=%async_computation.1 | async-start | bytes 35651584 | tf_op jit(solution)/shard_map/all_gather | solution.py:891
  17.2 39.2 %collective-permute-start = (bf16[256,2048]{1,0:T(8,128)(2,1)}, bf16[256,2048]{1,0:T(8,128)(2,1)S(1)}, u32[]{:S(2)}, u32[]{:S(2)}) collective-permute-start(bf16[256,2048]{1,0:T(8,128)(2,1)} %dynamic-slice_bitcast_fusion), channel_id=1, source_target_pairs={{0,2},{2,4},{4,6},{1,3},{3,5},{5,7},{8,10},{10,12},{12,14},{9,11},... | collective-permute-start | bytes 3145736 | tf_op jit(solution)/shard_map/ppermute | solution.py:135
  22.3 78.0 %copy-start.15 = (s32[1,512]{1,0:T(1,128)}, s32[1,512]{1,0:T(1,128)S(1)}, u32[]{:S(2)}) copy-start(s32[1,512]{1,0:T(1,128)S(1)} %get-tuple-element.69.refs_0_.refs_11_) | copy-start | bytes 6148
  56.4 37.9 %collective-permute-start.2 = (bf16[256,2048]{1,0:T(8,128)(2,1)S(1)}, bf16[256,2048]{1,0:T(8,128)(2,1)}, u32[]{:S(2)}, u32[]{:S(2)}) collective-permute-start(bf16[256,2048]{1,0:T(8,128)(2,1)S(1)} %collective-permute-done), channel_id=1, source_target_pairs={{0,2},{2,4},{4,6},{1,3},{3,5},{5,7},{8,10},{10,12},{12,14},{9,11},... | collective-permute-start | bytes 3145736 | tf_op jit(solution)/shard_map/ppermute | solution.py:135
  61.7 33.9 %collective-permute-start.1 = (bf16[256,2048]{1,0:T(8,128)(2,1)S(1)}, bf16[256,2048]{1,0:T(8,128)(2,1)}, u32[]{:S(2)}, u32[]{:S(2)}) collective-permute-start(bf16[256,2048]{1,0:T(8,128)(2,1)S(1)} %collective-permute-done), channel_id=1, source_target_pairs={{0,1},{1,0},{2,3},{3,2},{4,5},{5,4},{6,7},{7,6},{8,9},{9,8},{10,11... | collective-permute-start | bytes 3145736 | tf_op jit(solution)/shard_map/ppermute | solution.py:130
  94.4 23.2 %collective-permute-start.3 = (bf16[256,2048]{1,0:T(8,128)(2,1)}, bf16[256,2048]{1,0:T(8,128)(2,1)S(1)}, u32[]{:S(2)}, u32[]{:S(2)}) collective-permute-start(bf16[256,2048]{1,0:T(8,128)(2,1)} %collective-permute-done.2), channel_id=1, source_target_pairs={{0,1},{1,0},{2,3},{3,2},{4,5},{5,4},{6,7},{7,6},{8,9},{9,8},{10,11... | collective-permute-start | bytes 3145736 | tf_op jit(solution)/shard_map/ppermute | solution.py:130
  158.1 12.6 %slice-start = ((s8[17301504]{0:T(1024)(128)(4,1)}), s8[4194304]{0:T(1024)(128)(4,1)S(1)}, s32[]{:S(2)}) async-start(s8[17301504]{0:T(1024)(128)(4,1)} %bitcast.95), calls=%async_computation.2 | async-start | bytes 8388608
  161.4 9.3 %slice-start.1 = ((s8[17301504]{0:T(1024)(128)(4,1)}), s8[4194304]{0:T(1024)(128)(4,1)S(1)}, s32[]{:S(2)}) async-start(s8[17301504]{0:T(1024)(128)(4,1)} %bitcast.95), calls=%async_computation.3 | async-start | bytes 8388608
  161.4 9.3 %slice-start.2 = ((s8[17301504]{0:T(1024)(128)(4,1)}), s8[4194304]{0:T(1024)(128)(4,1)S(1)}, s32[]{:S(2)}) async-start(s8[17301504]{0:T(1024)(128)(4,1)} %bitcast.95), calls=%async_computation.4 | async-start | bytes 8388608
  161.4 9.3 %slice-start.3 = ((s8[17301504]{0:T(1024)(128)(4,1)}), s8[4194304]{0:T(1024)(128)(4,1)S(1)}, s32[]{:S(2)}) async-start(s8[17301504]{0:T(1024)(128)(4,1)} %bitcast.95), calls=%async_computation.5 | async-start | bytes 8388608
  161.4 9.3 %slice-start.4 = ((s8[17301504]{0:T(1024)(128)(4,1)}), s8[524288]{0:T(1024)(128)(4,1)S(1)}, s32[]{:S(2)}) async-start(s8[17301504]{0:T(1024)(128)(4,1)} %bitcast.95), calls=%async_computation.6 | async-start | bytes 1048576
  202.1 42.8 %collective-permute-start.4 = (bf16[512,2048]{1,0:T(8,128)(2,1)}, bf16[512,2048]{1,0:T(8,128)(2,1)}, u32[]{:S(2)}, u32[]{:S(2)}) collective-permute-start(bf16[512,2048]{1,0:T(8,128)(2,1)} %fusion.36), channel_id=1, source_target_pairs={{0,1},{1,0},{2,3},{3,2},{4,5},{5,4},{6,7},{7,6},{8,9},{9,8},{10,11... | collective-permute-start | bytes 6291464 | tf_op jit(solution)/shard_map/ppermute | solution.py:130
  258.2 8.0 %copy-start.3 = (bf16[2048,512]{0,1:T(8,128)(2,1)S(1)}, bf16[2048,512]{0,1:T(8,128)(2,1)}, u32[]{:S(2)}) copy-start(bf16[2048,512]{0,1:T(8,128)(2,1)} %get-tuple-element.34) | copy-start | bytes 6291460
  273.1 79.6 %copy-start.4 = (bf16[1,512,2048]{2,1,0:T(8,128)(2,1)S(1)}, bf16[1,512,2048]{2,1,0:T(8,128)(2,1)}, u32[]{:S(2)}) copy-start(bf16[1,512,2048]{2,1,0:T(8,128)(2,1)} %param.25) | copy-start | bytes 6291460
  756.3 10.2 %copy-start.7 = (bf16[512,2048]{1,0:T(8,128)(2,1)S(1)}, bf16[512,2048]{1,0:T(8,128)(2,1)}, u32[]{:S(2)}) copy-start(bf16[512,2048]{1,0:T(8,128)(2,1)} %get-tuple-element.42) | copy-start | bytes 6291460
  757.3 4.3 collective-permute-start.5
  763.2 4.6 copy-start.12
  763.2 5.4 copy-start.11
  763.2 6.2 copy-start.10
  (6 other events, 21.5 us)
Sparse Core Ops, SparseCore 0:
  13.3 140.9 all-gather.2
  155.8 180.6 all-gather.4
